TPU v7x, 32 devices: a whole 2x2x4 slice. The times are simulated.
32 devices in a mesh: strip: 2 (over x), ra: 16 (over z, y, core).
Axes of the slice: x: 2, y: 2, z: 4, core: 2. Of those that a mesh axis runs over, the one named last changes fastest.
Arguments:
- vis: bfloat16 [4, 32, 2048, 512], P(None, 'strip', 'ra'), parts along dimension 1, may hold values from -16 to 16
- beams: bfloat16 [4, 32, 16, 128], P(None, 'strip'), parts along dimension 1, may hold values from 0.19921875 to 1
- m_ra: bfloat16 [128, 512], replicated, may hold values from -0.25 to 0.25
- m_dec: bfloat16 [16, 16], replicated, may hold values from -0.75 to 0.75
- facet_of: int32 [4096, 1], P(('strip', 'ra')), parts along dimension 0, may hold values from 0 to 15; in each aligned block of 128 rows (0 to 127, 128 to 255, ...) at most 16 rows name the same one
- tile_of: int32 [4096], P(('strip', 'ra')), parts along dimension 0, may hold values from 0 to 1
- beam_of: int32 [4096], P(('strip', 'ra')), parts along dimension 0, may hold values from 0 to 15
- step_size: float32 [4], replicated, may hold values from 0.05 to 0.2
- thresholds: float32 [4, 4], replicated, may hold values from 0.5 to 5
Outputs:
- image: float32 [4, 32, 4096], P(None, 'strip', 'ra'), parts along dimension 1
There are 2 independent parts, one for each index of `strip`. A program takes and returns all parts, laid end to end along the dimension named above; an argument that names none is the same for every part. Nothing has to cross between parts.
Inputs may be any that keep to these rules, and one draw needn't show every extreme that they name: `facet_of`: among the pointings of one device (aligned blocks of 128 rows) no facet is named more than 16 times, a bound that some block reaches.
All inputs are finite; a program needn't handle non-finite values.
Results may differ from a plain program's by a relative error of at most 0.0058.
The roundings to bfloat16 on the way count: a program that leaves them out, or rounds other values in their place, can miss the bound.
Values may be sent and summed in bfloat16 or wider, within the bound.
No kernel may reach another device: no remote copies, remote signals or barrier semaphores. Data moves between devices by JAX's collectives and lax.ppermute only.
A program may use at most 128 MiB of HBM per device.

v0:
```python
import jax
import jax.numpy as jnp
import numpy as np
from jax import lax
from jax.sharding import PartitionSpec as P

BASES = 4
RA_DEV = 256


daub_coeffs = (
    (0.7071067811865476, 0.7071067811865476),
    (0.48296291314453416, 0.8365163037378079, 0.2241438680420134, -0.12940952255126037),
    (
        0.3326705529500825,
        0.8068915093110924,
        0.4598775021184914,
        -0.1350110200102546,
        -0.0854412738820267,
        0.0352262918857095,
    ),
    (
        0.2303778133088964,
        0.7148465705529155,
        0.6308807679298587,
        -0.0279837694168599,
        -0.1870348117190931,
        0.0308413818355607,
        0.0328830116668852,
        -0.010597401785069,
    ),
)


def shifted(value, axis, steps):
    count = lax.axis_size(axis)
    pairs = [(source, (source + steps) % count) for source in range(count)]
    return lax.ppermute(value, axis, pairs)


def filter_table(basis_count):
    low_pass = np.zeros((basis_count, 8))
    for basis_id in range(basis_count):
        coeffs = daub_coeffs[basis_id]
        low_pass[basis_id, : len(coeffs)] = coeffs
    high_pass = np.zeros((basis_count, 8))
    for column in range(8):
        high_pass[:, column] = (-1.0) ** column * low_pass[:, 7 - column]
    return (
        jnp.asarray(low_pass, jnp.float32),
        jnp.asarray(high_pass, jnp.float32),
        low_pass,
        high_pass,
    )


def dec_table(low_pass, high_pass, length):
    basis_count = low_pass.shape[0]
    half_size = length // 2
    matrix = np.zeros((basis_count, length, length))
    for basis_id in range(basis_count):
        for row_index in range(half_size):
            for column in range(8):
                target = (2 * row_index + column) % length
                matrix[basis_id, row_index, target] += low_pass[basis_id, column]
                matrix[basis_id, half_size + row_index, target] += high_pass[basis_id, column]
    return jnp.asarray(matrix, jnp.float32)


def taps(table, column):
    return table[:, column].reshape(-1, 1, 1, 1)


def ra_analysis(signal, tail, low_pass, high_pass):
    extended = jnp.concatenate([signal, tail], axis=-1)
    evens = extended[..., 0::2]
    odds = extended[..., 1::2]
    length = signal.shape[-1] // 2
    lower = jnp.float32(0.0)
    upper = jnp.float32(0.0)
    for tap_pair in range(4):
        even_part = evens[..., tap_pair : tap_pair + length]
        odd_part = odds[..., tap_pair : tap_pair + length]
        lower = (
            lower
            + taps(low_pass, 2 * tap_pair) * even_part
            + taps(low_pass, 2 * tap_pair + 1) * odd_part
        )
        upper = (
            upper
            + taps(high_pass, 2 * tap_pair) * even_part
            + taps(high_pass, 2 * tap_pair + 1) * odd_part
        )
    return (lower, upper)


def ra_synthesis(lower, upper, head_low, head_high, low_pass, high_pass):
    ext_low = jnp.concatenate([head_low, lower], axis=-1)
    ext_high = jnp.concatenate([head_high, upper], axis=-1)
    length = lower.shape[-1]
    evens = jnp.float32(0.0)
    odds = jnp.float32(0.0)
    for tap_pair in range(4):
        low_slice = ext_low[..., 3 - tap_pair : 3 - tap_pair + length]
        high_slice = ext_high[..., 3 - tap_pair : 3 - tap_pair + length]
        evens = (
            evens
            + taps(low_pass, 2 * tap_pair) * low_slice
            + taps(high_pass, 2 * tap_pair) * high_slice
        )
        odds = (
            odds
            + taps(low_pass, 2 * tap_pair + 1) * low_slice
            + taps(high_pass, 2 * tap_pair + 1) * high_slice
        )
    return jnp.stack([evens, odds], axis=-1).reshape(lower.shape[:-1] + (2 * length,))


def dec_apply(matrix, values):
    return jnp.einsum("qed,qcdn->qcen", matrix, values, precision=lax.Precision.HIGHEST)


def dec_adjoint(matrix, values):
    return jnp.einsum("qde,qcdn->qcen", matrix, values, precision=lax.Precision.HIGHEST)


def shrink(values, limits):
    return jnp.sign(values) * jnp.maximum(jnp.abs(values) - limits, 0.0)


def next_tail(values):
    return shifted(values[..., :6], "ra", -1)


def prev_head(lower, upper):
    return shifted((lower[..., -3:], upper[..., -3:]), "ra", 1)


def prox_image(field, limits, low_pass, high_pass, first_table, second_table):
    half_rows = field.shape[1] // 2
    bound = limits[:, :, None, None]
    tail_one = next_tail(field)[None]
    low_one, high_one = ra_analysis(field[None], tail_one, low_pass, high_pass)
    coarse_a = dec_apply(first_table, low_one)
    coarse_b = shrink(dec_apply(first_table, high_one), bound)
    smooth = coarse_a[:, :, :half_rows]
    detail = shrink(coarse_a[:, :, half_rows:], bound)
    tail_two = next_tail(smooth)
    low_two, high_two = ra_analysis(smooth, tail_two, low_pass, high_pass)
    fine_a = shrink(dec_apply(second_table, low_two), bound)
    fine_b = shrink(dec_apply(second_table, high_two), bound)
    back_low = dec_adjoint(second_table, fine_a)
    back_high = dec_adjoint(second_table, fine_b)
    head_low, head_high = prev_head(back_low, back_high)
    smooth_new = ra_synthesis(back_low, back_high, head_low, head_high, low_pass, high_pass)
    merged = jnp.concatenate([smooth_new, detail], axis=2)
    top_low = dec_adjoint(first_table, merged)
    top_high = dec_adjoint(first_table, coarse_b)
    edge_low, edge_high = prev_head(top_low, top_high)
    rebuilt = ra_synthesis(top_low, top_high, edge_low, edge_high, low_pass, high_pass)
    return jnp.maximum(jnp.mean(rebuilt, axis=0), 0.0)


def local(vis, beams, m_ra, m_dec, facet_of, tile_of, beam_of, step_size, thresholds):
    ra_count = lax.axis_size("ra")
    channels, dec_rows, owned_count, samples = vis.shape
    patch_width = m_ra.shape[0]
    tile_count = RA_DEV // patch_width
    capacity = max(2, 2 * owned_count // ra_count)
    slot_count = ra_count * capacity
    facets = facet_of[:, 0]
    positions = jnp.arange(owned_count, dtype=jnp.int32)
    before = (facets[None, :] == facets[:, None]) & (positions[None, :] < positions[:, None])
    rank_in = jnp.sum(before.astype(jnp.int32), axis=1)
    slot_of = facets * capacity + rank_in
    wanted = jnp.full((slot_count,), -1, jnp.int32).at[slot_of].set(tile_of)
    requested = lax.all_to_all(
        wanted.reshape(ra_count, capacity), "ra", split_axis=0, concat_axis=0, tiled=True
    ).reshape(slot_count)
    picker = (requested[None, :] == jnp.arange(tile_count, dtype=jnp.int32)[:, None]).astype(
        jnp.bfloat16
    )
    beam_pick = (beam_of[:, None] == jnp.arange(beams.shape[2], dtype=jnp.int32)[None, :]).astype(
        jnp.bfloat16
    )
    beam_tiles = jnp.einsum("pb,cdbw->cdpw", beam_pick, beams, preferred_element_type=jnp.float32)
    low_pass, high_pass, low_np, high_np = filter_table(BASES)
    first_table = dec_table(low_np, high_np, dec_rows)
    second_table = dec_table(low_np, high_np, dec_rows // 2)
    limits = thresholds * step_size[None, :]

    def spread(residual):
        dec_back = jnp.einsum(
            "ed,cepk->cdpk", m_dec, residual, preferred_element_type=jnp.float32
        ).astype(jnp.bfloat16)
        patches = jnp.einsum("cdpk,tk->cdpt", dec_back, m_ra, preferred_element_type=jnp.float32)
        gradients = (beam_tiles * patches).astype(jnp.bfloat16)
        outgoing = (
            jnp.zeros((channels, dec_rows, slot_count, patch_width), jnp.bfloat16)
            .at[:, :, slot_of, :]
            .set(gradients)
        )
        incoming = lax.all_to_all(outgoing, "ra", split_axis=2, concat_axis=2, tiled=True)
        summed = jnp.einsum("ts,cdsw->cdtw", picker, incoming, preferred_element_type=jnp.float32)
        return summed.reshape(channels, dec_rows, tile_count * patch_width)

    gradient = spread(-vis)
    first_image = prox_image(
        -step_size[:, None, None] * gradient, limits, low_pass, high_pass, first_table, second_table
    )
    image_tiles = first_image.astype(jnp.bfloat16).reshape(
        channels, dec_rows, tile_count, patch_width
    )
    global_tile = facets * tile_count + tile_of
    blank_tiles = jnp.zeros((channels, dec_rows, owned_count, patch_width), jnp.bfloat16)
    shards = lax.all_gather(image_tiles, "ra", axis=2, tiled=True)
    inside = (global_tile >= 0) & (global_tile < shards.shape[2])
    picked = jnp.take(shards, jnp.clip(global_tile, 0, shards.shape[2] - 1), axis=2)
    weighted = (
        beam_tiles * jnp.where(inside[None, None, :, None], picked, blank_tiles).astype(jnp.float32)
    ).astype(jnp.bfloat16)
    along_ra = jnp.einsum(
        "cdpt,tk->cdpk", weighted, m_ra, preferred_element_type=jnp.float32
    ).astype(jnp.bfloat16)
    predicted = jnp.einsum("ed,cdpk->cepk", m_dec, along_ra, preferred_element_type=jnp.float32)
    gradient_two = spread((predicted - vis.astype(jnp.float32)).astype(jnp.bfloat16))
    return prox_image(
        first_image - step_size[:, None, None] * gradient_two,
        limits,
        low_pass,
        high_pass,
        first_table,
        second_table,
    )


def solution(mesh):
    in_specs = (
        P(None, "strip", "ra", None),
        P(None, "strip", None, None),
        P(),
        P(),
        P(("strip", "ra"), None),
        P(("strip", "ra")),
        P(("strip", "ra")),
        P(),
        P(),
    )
    out_specs = P(None, "strip", "ra")
    return jax.shard_map(local, mesh=mesh, in_specs=in_specs, out_specs=out_specs, check_vma=False)
```

profile of v0, /device:TPU:0, one launch (start us, length us, event | category | flops | bytes accessed | tf_op | source)
XLA Modules:
  0.0 446.7 jit_solution(14267247574342125141)
XLA Ops:
  3.4 7.4 %all-to-all-start.1 = ((s32[16,1,16]{2,1,0:T(1,128)}), s32[16,1,16]{2,1,0:T(1,128)S(1)}, u32[]{:S(2)}, u32[]{:S(2)}) async-start(s32[16,1,16]{2,1,0:T(1,128)} %all_to_all.13), calls=%async_computation.1 | async-start | bytes 16384 | tf_op jit(solution)/shard_map/all_to_all | solution.py:177
  10.8 9.0 %neg.8 = bf16[4,16,128,512]{3,2,1,0:T(8,128)(2,1)} negate(bf16[4,16,128,512]{3,2,1,0:T(8,128)(2,1)} %param.13) | non-fusion elementwise | flops 4194304 | bytes 16777216 | tf_op jit(solution)/shard_map/neg | solution.py:207
  20.6 10.2 %convert_bitcast_fusion.1 = bf16[4,16,128,512]{3,1,2,0:T(8,128)(2,1)S(1)} fusion(bf16[4,16,128,512]{3,2,1,0:T(8,128)(2,1)} %neg.8, bf16[16,16]{1,0:T(8,128)(2,1)S(1)} %copy-done.19), kind=kOutput, calls=%fused_computation.14 | convolution fusion | flops 138412032 | bytes 16777728 | tf_op jit(solution)/shard_map/ed,cepk->cdpk/dot_general | solution.py:193
  30.8 9.8 %fusion.20 = bf16[128,4,16,128]{3,0,2,1:T(8,128)(2,1)S(1)} fusion(f32[128,4,16,128]{3,0,2,1:T(8,128)S(1)} %fusion.359, bf16[4,16,128,512]{3,1,2,0:T(8,128)(2,1)S(1)} %convert_bitcast_fusion.1, bf16[128,512]{1,0:T(8,128)(2,1)S(1)} %copy-done.3), kind=kOutput, calls=%fused_computation.27 | convolution fusion | flops 1075838976 | bytes 14811136 | tf_op jit(solution)/shard_map/cdpk,tk->cdpt/dot_general | solution.py:196
  41.9 2.6 broadcast.98.clone
  44.5 16.1 %scatter_fusion = bf16[4,16,256,128]{3,1,2,0:T(8,128)(2,1)} fusion(bf16[4,16,256,128]{3,1,2,0:T(8,128)(2,1)} %broadcast.98.clone, s32[128]{0:T(128)S(1)} %fusion.369, bf16[128,4,16,128]{3,2,1,0:T(8,128)(2,1)S(1)} %copy.132), kind=kCustom, calls=%fused_computation.1 | custom fusion | bytes 6291968 | tf_op jit(solution)/shard_map/scatter | solution.py:201
  60.6 5.5 %copy.133 = bf16[4,16,256,128]{3,1,0,2:T(8,128)(2,1)} copy(bf16[4,16,256,128]{3,1,2,0:T(8,128)(2,1)} %scatter_fusion) | data formatting | bytes 8388608 | tf_op jit(solution)/shard_map/scatter | solution.py:201
  66.1 6.2 %all-to-all-start = ((bf16[4,16,256,128]{3,1,0,2:T(8,128)(2,1)}), bf16[4,16,256,128]{3,1,0,2:T(8,128)(2,1)}, u32[]{:S(2)}, u32[]{:S(2)}) async-start(bf16[4,16,256,128]{3,1,0,2:T(8,128)(2,1)} %copy.133), calls=%async_computation | async-start | bytes 8388608 | tf_op jit(solution)/shard_map/all_to_all | solution.py:203
  73.8 76.2 %all-to-all-done = bf16[4,16,256,128]{3,1,0,2:T(8,128)(2,1)} async-done(((bf16[4,16,256,128]{3,1,0,2:T(8,128)(2,1)}), bf16[4,16,256,128]{3,1,0,2:T(8,128)(2,1)}, u32[]{:S(2)}, u32[]{:S(2)}) %all-to-all-start) | async-done | bytes 4194336 | tf_op jit(solution)/shard_map/all_to_all | solution.py:203
  150.0 4.5 %fusion.30 = f32[4,16,2,128]{3,2,1,0:T(2,128)S(1)} fusion(bf16[4,16,256,128]{3,1,0,2:T(8,128)(2,1)} %all-to-all-done, s32[256]{0:T(256)S(1)} %eq.50), kind=kOutput, calls=%fused_computation.38 | convolution fusion | flops 8389120 | bytes 4260864 | tf_op jit(solution)/shard_map/ts,cdsw->cdtw/dot_general | solution.py:204
  154.6 31.2 %collective-permute-start = (f32[4,16,6]{2,1,0:T(8,128)S(1)}, f32[4,16,6]{2,1,0:T(8,128)S(1)}, u32[]{:S(2)}, u32[]{:S(2)}) collective-permute-start(f32[4,16,6]{2,1,0:T(8,128)S(1)} %slice_multiply_fusion), channel_id=1, source_target_pairs={{0,15},{1,0},{2,1},{3,2},{4,3},{5,4},{6,5},{7,6},{8,7},{9,8},{10,9... | collective-permute-start | bytes 4616 | tf_op jit(solution)/shard_map/ppermute | solution.py:38
  185.9 1.5 collective-permute-done
  190.4 4.5 %collective-permute-start.1 = (f32[4,4,8,6]{3,2,1,0:T(8,128)S(1)}, f32[4,4,8,6]{3,2,1,0:T(8,128)S(1)}, u32[]{:S(2)}, u32[]{:S(2)}) collective-permute-start(f32[4,4,8,6]{3,2,1,0:T(8,128)S(1)} %slice.510), channel_id=1, source_target_pairs={{0,15},{1,0},{2,1},{3,2},{4,3},{5,4},{6,5},{7,6},{8,7},{9,8},{10,9... | collective-permute-start | bytes 9224 | tf_op jit(solution)/shard_map/ppermute | solution.py:38
  198.2 1.5 slice.425
  201.8 5.5 %collective-permute-done.2 = f32[4,4,8,3]{3,2,1,0:T(8,128)S(1)} collective-permute-done((f32[4,4,8,3]{3,2,1,0:T(8,128)S(1)}, f32[4,4,8,3]{3,2,1,0:T(8,128)S(1)}, u32[]{:S(2)}, u32[]{:S(2)}) %collective-permute-start.2) | collective-permute-done | bytes 1568 | tf_op jit(solution)/shard_map/ppermute | solution.py:38
  210.0 7.2 %collective-permute-done.4 = f32[4,4,16,3]{3,2,1,0:T(8,128)S(1)} collective-permute-done((f32[4,4,16,3]{3,2,1,0:T(8,128)S(1)}, f32[4,4,16,3]{3,2,1,0:T(8,128)S(1)}, u32[]{:S(2)}, u32[]{:S(2)}) %collective-permute-start.4) | collective-permute-done | bytes 3104 | tf_op jit(solution)/shard_map/ppermute | solution.py:38
  218.4 18.7 %all_gather.3 = bf16[4,16,32,128]{3,1,2,0:T(8,128)(2,1)S(1)} all-gather(bf16[4,16,2,128]{3,1,2,0:T(8,128)(2,1)S(1)} %copy.143), channel_id=1, replica_groups=mesh['strip'=2,'ra'=16] {'ra'}, dimensions={2}, use_global_device_ids=true | all-gather | bytes 557056 | tf_op jit(solution)/shard_map/all_gather | solution.py:216
  238.2 8.7 %convolution_convert_fusion = bf16[4,16,128,512]{3,2,1,0:T(8,128)(2,1)} fusion(f32[128,4,16,128]{3,0,2,1:T(8,128)} %copy-done.2, bf16[128,4,16,128]{3,2,1,0:T(8,128)(2,1)S(1)} %gather_fusion, pred[128]{0:T(512)(128)(4,1)S(1)} %get-tuple-element.29, pred[128]{0:T(512)(128)(4,1)S(1)} %get-tuple-element.5, bf16[128,512]{1,0:T(8,128)(2,1)S(1)} %copy-done.3), kind=kOutput, calls=%fused_computation.15 | convolution fusion | flops 1083179008 | bytes 14811392 | tf_op jit(solution)/shard_map/cdpt,tk->cdpk/dot_general | solution.py:222
  246.8 21.2 %convert_bitcast_fusion = bf16[4,16,128,512]{3,1,2,0:T(8,128)(2,1)} fusion(bf16[4,16,128,512]{3,2,1,0:T(8,128)(2,1)} %param.13, bf16[4,16,128,512]{3,2,1,0:T(8,128)(2,1)} %convolution_convert_fusion, bf16[16,16]{1,0:T(8,128)(2,1)S(1)} %copy-done.19), kind=kOutput, calls=%fused_computation.13 | convolution fusion | flops 285212672 | bytes 25166336 | tf_op jit(solution)/shard_map/ed,cepk->cdpk/dot_general | solution.py:193
  268.1 14.1 %fusion.19 = bf16[128,4,16,128]{3,0,2,1:T(8,128)(2,1)S(1)} fusion(f32[128,4,16,128]{3,0,2,1:T(8,128)} %copy-done.2, bf16[4,16,128,512]{3,1,2,0:T(8,128)(2,1)} %convert_bitcast_fusion, bf16[128,512]{1,0:T(8,128)(2,1)S(1)} %copy-done.3), kind=kOutput, calls=%fused_computation.26 | convolution fusion | flops 1075838976 | bytes 14811136 | tf_op jit(solution)/shard_map/cdpk,tk->cdpt/dot_general | solution.py:196
  283.5 2.6 broadcast.98
  286.1 16.3 %scatter_fusion.1 = bf16[4,16,256,128]{3,1,2,0:T(8,128)(2,1)} fusion(bf16[4,16,256,128]{3,1,2,0:T(8,128)(2,1)} %broadcast.98, s32[128]{0:T(128)S(1)} %fusion.369, bf16[128,4,16,128]{3,2,1,0:T(8,128)(2,1)S(1)} %copy.149), kind=kCustom, calls=%fused_computation.3 | custom fusion | bytes 6291968 | tf_op jit(solution)/shard_map/scatter | solution.py:201
  302.4 5.5 %copy.150 = bf16[4,16,256,128]{3,1,0,2:T(8,128)(2,1)} copy(bf16[4,16,256,128]{3,1,2,0:T(8,128)(2,1)} %scatter_fusion.1) | data formatting | bytes 8388608 | tf_op jit(solution)/shard_map/scatter | solution.py:201
  307.9 4.5 %all-to-all-start.2 = ((bf16[4,16,256,128]{3,1,0,2:T(8,128)(2,1)}), bf16[4,16,256,128]{3,1,0,2:T(8,128)(2,1)}, u32[]{:S(2)}, u32[]{:S(2)}) async-start(bf16[4,16,256,128]{3,1,0,2:T(8,128)(2,1)} %copy.150), calls=%async_computation.2 | async-start | bytes 8388608 | tf_op jit(solution)/shard_map/all_to_all | solution.py:203
  312.9 77.2 %all-to-all-done.2 = bf16[4,16,256,128]{3,1,0,2:T(8,128)(2,1)} async-done(((bf16[4,16,256,128]{3,1,0,2:T(8,128)(2,1)}), bf16[4,16,256,128]{3,1,0,2:T(8,128)(2,1)}, u32[]{:S(2)}, u32[]{:S(2)}) %all-to-all-start.2) | async-done | bytes 4194336 | tf_op jit(solution)/shard_map/all_to_all | solution.py:203
  390.0 4.5 %fusion.33 = f32[4,16,2,128]{3,2,1,0:T(2,128)S(1)} fusion(bf16[4,16,256,128]{3,1,0,2:T(8,128)(2,1)} %all-to-all-done.2, s32[256]{0:T(256)S(1)} %eq.50), kind=kOutput, calls=%fused_computation.39 | convolution fusion | flops 8389120 | bytes 4260864 | tf_op jit(solution)/shard_map/ts,cdsw->cdtw/dot_general | solution.py:204
  394.9 18.1 %collective-permute-start.6 = (f32[4,16,6]{1,2,0:T(8,128)S(1)}, f32[4,16,6]{1,2,0:T(8,128)S(1)}, u32[]{:S(2)}, u32[]{:S(2)}) collective-permute-start(f32[4,16,6]{1,2,0:T(8,128)S(1)} %slice_subtract_fusion), channel_id=1, source_target_pairs={{0,15},{1,0},{2,1},{3,2},{4,3},{5,4},{6,5},{7,6},{8,7},{9,8},{10,9... | collective-permute-start | bytes 4616 | tf_op jit(solution)/shard_map/ppermute | solution.py:38
  417.9 4.5 %collective-permute-start.7 = (f32[4,4,8,6]{3,2,1,0:T(8,128)S(1)}, f32[4,4,8,6]{3,2,1,0:T(8,128)S(1)}, u32[]{:S(2)}, u32[]{:S(2)}) collective-permute-start(f32[4,4,8,6]{3,2,1,0:T(8,128)S(1)} %slice.551), channel_id=1, source_target_pairs={{0,15},{1,0},{2,1},{3,2},{4,3},{5,4},{6,5},{7,6},{8,7},{9,8},{10,9... | collective-permute-start | bytes 9224 | tf_op jit(solution)/shard_map/ppermute | solution.py:38
  422.4 1.8 collective-permute-done.7
  425.7 1.5 slice.473
  429.3 5.5 %collective-permute-done.8 = f32[4,4,8,3]{3,2,1,0:T(8,128)S(1)} collective-permute-done((f32[4,4,8,3]{3,2,1,0:T(8,128)S(1)}, f32[4,4,8,3]{3,2,1,0:T(8,128)S(1)}, u32[]{:S(2)}, u32[]{:S(2)}) %collective-permute-start.8) | collective-permute-done | bytes 1568 | tf_op jit(solution)/shard_map/ppermute | solution.py:38
  437.5 7.1 %collective-permute-done.10 = f32[4,4,16,3]{3,2,1,0:T(8,128)S(1)} collective-permute-done((f32[4,4,16,3]{3,2,1,0:T(8,128)S(1)}, f32[4,4,16,3]{3,2,1,0:T(8,128)S(1)}, u32[]{:S(2)}, u32[]{:S(2)}) %collective-permute-start.10) | collective-permute-done | bytes 3104 | tf_op jit(solution)/shard_map/ppermute | solution.py:38
  (152 shorter events, 35.3 us)
Async XLA Ops:
  0.0 19.8 %copy-start = (bf16[4,16,16,128]{3,2,1,0:T(8,128)(2,1)S(1)}, bf16[4,16,16,128]{3,2,1,0:T(8,128)(2,1)}, u32[]{:S(2)}) copy-start(bf16[4,16,16,128]{3,2,1,0:T(8,128)(2,1)} %param.14) | copy-start | bytes 786436
  3.4 62.7 %all-to-all-start.1 = ((s32[16,1,16]{2,1,0:T(1,128)}), s32[16,1,16]{2,1,0:T(1,128)S(1)}, u32[]{:S(2)}, u32[]{:S(2)}) async-start(s32[16,1,16]{2,1,0:T(1,128)} %all_to_all.13), calls=%async_computation.1 | async-start | bytes 16384 | tf_op jit(solution)/shard_map/all_to_all | solution.py:177
  20.5 10.2 %copy-start.2 = (f32[128,4,16,128]{3,0,2,1:T(8,128)}, f32[128,4,16,128]{3,0,2,1:T(8,128)S(1)}, u32[]{:S(2)}) copy-start(f32[128,4,16,128]{3,0,2,1:T(8,128)S(1)} %fusion.359) | copy-start | bytes 12582916
  66.1 83.8 %all-to-all-start = ((bf16[4,16,256,128]{3,1,0,2:T(8,128)(2,1)}), bf16[4,16,256,128]{3,1,0,2:T(8,128)(2,1)}, u32[]{:S(2)}, u32[]{:S(2)}) async-start(bf16[4,16,256,128]{3,1,0,2:T(8,128)(2,1)} %copy.133), calls=%async_computation | async-start | bytes 8388608 | tf_op jit(solution)/shard_map/all_to_all | solution.py:203
  72.3 117.6 %copy-start.4 = (f32[4,16,16,1]{2,1,3,0:T(8,128)S(1)}, f32[4,16,16,1]{2,1,3,0:T(8,128)}, u32[]{:S(2)}) copy-start(f32[4,16,16,1]{2,1,3,0:T(8,128)} %constant.85) | copy-start | bytes 12292
  72.3 117.6 %copy-start.6 = (f32[4]{0:T(128)S(1)}, f32[4]{0:T(128)}, u32[]{:S(2)}) copy-start(f32[4]{0:T(128)} %constant.56) | copy-start | bytes 52
  72.3 117.6 %copy-start.7 = (f32[4]{0:T(128)S(1)}, f32[4]{0:T(128)}, u32[]{:S(2)}) copy-start(f32[4]{0:T(128)} %constant.60) | copy-start | bytes 52
  72.3 117.6 %copy-start.8 = (f32[4]{0:T(128)S(1)}, f32[4]{0:T(128)}, u32[]{:S(2)}) copy-start(f32[4]{0:T(128)} %constant.64) | copy-start | bytes 52
  72.3 117.6 %copy-start.9 = (f32[4]{0:T(128)S(1)}, f32[4]{0:T(128)}, u32[]{:S(2)}) copy-start(f32[4]{0:T(128)} %constant.68) | copy-start | bytes 52
  72.3 117.6 %copy-start.10 = (f32[4]{0:T(128)S(1)}, f32[4]{0:T(128)}, u32[]{:S(2)}) copy-start(f32[4]{0:T(128)} %constant.54) | copy-start | bytes 52
  72.4 117.6 %copy-start.15 = (f32[4]{0:T(128)S(1)}, f32[4]{0:T(128)}, u32[]{:S(2)}) copy-start(f32[4]{0:T(128)} %constant.58) | copy-start | bytes 52
  72.4 117.6 %copy-start.16 = (f32[4]{0:T(128)S(1)}, f32[4]{0:T(128)}, u32[]{:S(2)}) copy-start(f32[4]{0:T(128)} %constant.62) | copy-start | bytes 52
  72.4 117.6 %copy-start.17 = (f32[4]{0:T(128)S(1)}, f32[4]{0:T(128)}, u32[]{:S(2)}) copy-start(f32[4]{0:T(128)} %constant.66) | copy-start | bytes 52
  72.4 122.5 %copy-start.11 = (f32[4]{0:T(128)S(1)}, f32[4]{0:T(128)}, u32[]{:S(2)}) copy-start(f32[4]{0:T(128)} %constant.72) | copy-start | bytes 52
  72.4 122.4 %copy-start.12 = (f32[4]{0:T(128)S(1)}, f32[4]{0:T(128)}, u32[]{:S(2)}) copy-start(f32[4]{0:T(128)} %constant.76) | copy-start | bytes 52
  72.4 122.4 %copy-start.13 = (f32[4]{0:T(128)S(1)}, f32[4]{0:T(128)}, u32[]{:S(2)}) copy-start(f32[4]{0:T(128)} %constant.80) | copy-start | bytes 52
  72.4 122.4 %copy-start.14 = (f32[4]{0:T(128)S(1)}, f32[4]{0:T(128)}, u32[]{:S(2)}) copy-start(f32[4]{0:T(128)} %constant.84) | copy-start | bytes 52
  73.8 125.9 %copy-start.5 = (f32[4,8,8,1]{2,1,3,0:T(8,128)S(1)}, f32[4,8,8,1]{2,1,3,0:T(8,128)}, u32[]{:S(2)}) copy-start(f32[4,8,8,1]{2,1,3,0:T(8,128)} %constant.86) | copy-start | bytes 3076
  154.6 32.8 %collective-permute-start = (f32[4,16,6]{2,1,0:T(8,128)S(1)}, f32[4,16,6]{2,1,0:T(8,128)S(1)}, u32[]{:S(2)}, u32[]{:S(2)}) collective-permute-start(f32[4,16,6]{2,1,0:T(8,128)S(1)} %slice_multiply_fusion), channel_id=1, source_target_pairs={{0,15},{1,0},{2,1},{3,2},{4,3},{5,4},{6,5},{7,6},{8,7},{9,8},{10,9... | collective-permute-start | bytes 4616 | tf_op jit(solution)/shard_map/ppermute | solution.py:38
  190.4 6.4 %collective-permute-start.1 = (f32[4,4,8,6]{3,2,1,0:T(8,128)S(1)}, f32[4,4,8,6]{3,2,1,0:T(8,128)S(1)}, u32[]{:S(2)}, u32[]{:S(2)}) collective-permute-start(f32[4,4,8,6]{3,2,1,0:T(8,128)S(1)} %slice.510), channel_id=1, source_target_pairs={{0,15},{1,0},{2,1},{3,2},{4,3},{5,4},{6,5},{7,6},{8,7},{9,8},{10,9... | collective-permute-start | bytes 9224 | tf_op jit(solution)/shard_map/ppermute | solution.py:38
  200.9 6.5 %collective-permute-start.2 = (f32[4,4,8,3]{3,2,1,0:T(8,128)S(1)}, f32[4,4,8,3]{3,2,1,0:T(8,128)S(1)}, u32[]{:S(2)}, u32[]{:S(2)}) collective-permute-start(f32[4,4,8,3]{3,2,1,0:T(8,128)S(1)} %slice.519), channel_id=1, source_target_pairs={{0,1},{1,2},{2,3},{3,4},{4,5},{5,6},{6,7},{7,8},{8,9},{9,10},{10,1... | collective-permute-start | bytes 4616 | tf_op jit(solution)/shard_map/ppermute | solution.py:38
  201.3 6.8 %collective-permute-start.3 = (f32[4,4,8,3]{3,2,1,0:T(8,128)S(1)}, f32[4,4,8,3]{3,2,1,0:T(8,128)S(1)}, u32[]{:S(2)}, u32[]{:S(2)}) collective-permute-start(f32[4,4,8,3]{3,2,1,0:T(8,128)S(1)} %slice.522), channel_id=1, source_target_pairs={{0,1},{1,2},{2,3},{3,4},{4,5},{5,6},{6,7},{7,8},{8,9},{9,10},{10,1... | collective-permute-start | bytes 4616 | tf_op jit(solution)/shard_map/ppermute | solution.py:38
  201.8 8.2 %collective-permute-start.5 = (f32[4,4,16,3]{3,2,1,0:T(8,128)S(1)}, f32[4,4,16,3]{3,2,1,0:T(8,128)S(1)}, u32[]{:S(2)}, u32[]{:S(2)}) collective-permute-start(f32[4,4,16,3]{3,2,1,0:T(8,128)S(1)} %slice.533), channel_id=1, source_target_pairs={{0,1},{1,2},{2,3},{3,4},{4,5},{5,6},{6,7},{7,8},{8,9},{9,10},{10,1... | collective-permute-start | bytes 9224 | tf_op jit(solution)/shard_map/ppermute | solution.py:38
  209.9 7.2 %collective-permute-start.4 = (f32[4,4,16,3]{3,2,1,0:T(8,128)S(1)}, f32[4,4,16,3]{3,2,1,0:T(8,128)S(1)}, u32[]{:S(2)}, u32[]{:S(2)}) collective-permute-start(f32[4,4,16,3]{3,2,1,0:T(8,128)S(1)} %slice.530), channel_id=1, source_target_pairs={{0,1},{1,2},{2,3},{3,4},{4,5},{5,6},{6,7},{7,8},{8,9},{9,10},{10,1... | collective-permute-start | bytes 9224 | tf_op jit(solution)/shard_map/ppermute | solution.py:38
  307.9 82.2 %all-to-all-start.2 = ((bf16[4,16,256,128]{3,1,0,2:T(8,128)(2,1)}), bf16[4,16,256,128]{3,1,0,2:T(8,128)(2,1)}, u32[]{:S(2)}, u32[]{:S(2)}) async-start(bf16[4,16,256,128]{3,1,0,2:T(8,128)(2,1)} %copy.150), calls=%async_computation.2 | async-start | bytes 8388608 | tf_op jit(solution)/shard_map/all_to_all | solution.py:203
  394.9 19.6 %collective-permute-start.6 = (f32[4,16,6]{1,2,0:T(8,128)S(1)}, f32[4,16,6]{1,2,0:T(8,128)S(1)}, u32[]{:S(2)}, u32[]{:S(2)}) collective-permute-start(f32[4,16,6]{1,2,0:T(8,128)S(1)} %slice_subtract_fusion), channel_id=1, source_target_pairs={{0,15},{1,0},{2,1},{3,2},{4,3},{5,4},{6,5},{7,6},{8,7},{9,8},{10,9... | collective-permute-start | bytes 4616 | tf_op jit(solution)/shard_map/ppermute | solution.py:38
  417.9 6.4 %collective-permute-start.7 = (f32[4,4,8,6]{3,2,1,0:T(8,128)S(1)}, f32[4,4,8,6]{3,2,1,0:T(8,128)S(1)}, u32[]{:S(2)}, u32[]{:S(2)}) collective-permute-start(f32[4,4,8,6]{3,2,1,0:T(8,128)S(1)} %slice.551), channel_id=1, source_target_pairs={{0,15},{1,0},{2,1},{3,2},{4,3},{5,4},{6,5},{7,6},{8,7},{9,8},{10,9... | collective-permute-start | bytes 9224 | tf_op jit(solution)/shard_map/ppermute | solution.py:38
  427.2 19.3 %copy-start.1 = (bf16[4,16,16,128]{3,2,1,0:T(8,128)(2,1)S(1)}, bf16[4,16,16,128]{3,2,1,0:T(8,128)(2,1)}, u32[]{:S(2)}) copy-start(bf16[4,16,16,128]{3,2,1,0:T(8,128)(2,1)} %param.14) | copy-start | bytes 786436
  428.4 6.5 %collective-permute-start.8 = (f32[4,4,8,3]{3,2,1,0:T(8,128)S(1)}, f32[4,4,8,3]{3,2,1,0:T(8,128)S(1)}, u32[]{:S(2)}, u32[]{:S(2)}) collective-permute-start(f32[4,4,8,3]{3,2,1,0:T(8,128)S(1)} %slice.560), channel_id=1, source_target_pairs={{0,1},{1,2},{2,3},{3,4},{4,5},{5,6},{6,7},{7,8},{8,9},{9,10},{10,1... | collective-permute-start | bytes 4616 | tf_op jit(solution)/shard_map/ppermute | solution.py:38
  428.8 6.8 %collective-permute-start.9 = (f32[4,4,8,3]{3,2,1,0:T(8,128)S(1)}, f32[4,4,8,3]{3,2,1,0:T(8,128)S(1)}, u32[]{:S(2)}, u32[]{:S(2)}) collective-permute-start(f32[4,4,8,3]{3,2,1,0:T(8,128)S(1)} %slice.563), channel_id=1, source_target_pairs={{0,1},{1,2},{2,3},{3,4},{4,5},{5,6},{6,7},{7,8},{8,9},{9,10},{10,1... | collective-permute-start | bytes 4616 | tf_op jit(solution)/shard_map/ppermute | solution.py:38
  429.3 8.2 %collective-permute-start.11 = (f32[4,4,16,3]{3,2,1,0:T(8,128)S(1)}, f32[4,4,16,3]{3,2,1,0:T(8,128)S(1)}, u32[]{:S(2)}, u32[]{:S(2)}) collective-permute-start(f32[4,4,16,3]{3,2,1,0:T(8,128)S(1)} %slice.574), channel_id=1, source_target_pairs={{0,1},{1,2},{2,3},{3,4},{4,5},{5,6},{6,7},{7,8},{8,9},{9,10},{10,1... | collective-permute-start | bytes 9224 | tf_op jit(solution)/shard_map/ppermute | solution.py:38
  437.4 7.1 %collective-permute-start.10 = (f32[4,4,16,3]{3,2,1,0:T(8,128)S(1)}, f32[4,4,16,3]{3,2,1,0:T(8,128)S(1)}, u32[]{:S(2)}, u32[]{:S(2)}) collective-permute-start(f32[4,4,16,3]{3,2,1,0:T(8,128)S(1)} %slice.571), channel_id=1, source_target_pairs={{0,1},{1,2},{2,3},{3,4},{4,5},{5,6},{6,7},{7,8},{8,9},{9,10},{10,1... | collective-permute-start | bytes 9224 | tf_op jit(solution)/shard_map/ppermute | solution.py:38
  (7 other events, 45.3 us)
where the time goes:
time: 455 us; the launch traced here: 447 us
  waiting for transfers between devices  186 us (41%)
  matrix products  79.2 us (17%)
  starting transfers between devices  76.7 us (17%)
  local copies, waits for them, and re-layouts  70.3 us (15%)
  blocking collectives  18.7 us (4%)
  other arithmetic  14.7 us (3%)
    all_to_all x2, waiting for transfers between devices, spread(): lax.all_to_all(outgoing, 'ra', split_axis=2, concat_axis=2, tiled=True)  153 us
    ppermute x12, starting transfers between devices, shifted(): return lax.ppermute(value, axis, pairs)  58.6 us
    scatter x4, local copies, waits for them, and re-layouts, spread(): outgoing = jnp.zeros((channels, dec_rows, slot_count, patch_width), jnp.b...  43.4 us
    ppermute x12, waiting for transfers between devices, shifted(): return lax.ppermute(value, axis, pairs)  32.8 us
    dot_general x2, matrix products, spread(): jnp.einsum('ed,cepk->cdpk', m_dec, residual, preferred_element_type=jnp.f...  31.4 us
    dot_general x2, matrix products, spread(): jnp.einsum('cdpk,tk->cdpt', dec_back, m_ra, preferred_element_type=jnp.fl...  23.8 us
    all_gather x1, blocking collectives, local(): shards = lax.all_gather(image_tiles, 'ra', axis=2, tiled=True)  18.7 us
    all_to_all x2, starting transfers between devices, spread(): lax.all_to_all(outgoing, 'ra', split_axis=2, concat_axis=2, tiled=True)  10.7 us
  transfers between devices with their start and end apart: 15, of which 12 were waited for; matrix products, arithmetic and copies ran while one was open for 14% of the time, Pallas kernels for 0%

commit v1 on v0

v1 whole, which is shorter than its diff:
```python
import functools

import jax
import jax.numpy as jnp
import numpy as np
from jax import lax
from jax.experimental import pallas as pl
from jax.experimental.pallas import tpu as pltpu
from jax.sharding import PartitionSpec as P

BASES = 4
RA_DEV = 256
GROUP = 16
PHASES = 4
LANES = 128
SPAN = LANES // PHASES
SLOTS = 3

daub_coeffs = (
    (0.7071067811865476, 0.7071067811865476),
    (0.48296291314453416, 0.8365163037378079, 0.2241438680420134, -0.12940952255126037),
    (
        0.3326705529500825,
        0.8068915093110924,
        0.4598775021184914,
        -0.1350110200102546,
        -0.0854412738820267,
        0.0352262918857095,
    ),
    (
        0.2303778133088964,
        0.7148465705529155,
        0.6308807679298587,
        -0.0279837694168599,
        -0.1870348117190931,
        0.0308413818355607,
        0.0328830116668852,
        -0.010597401785069,
    ),
)


def filter_table(basis_count):
    low_pass = np.zeros((basis_count, 8))
    for basis_id in range(basis_count):
        coeffs = daub_coeffs[basis_id]
        low_pass[basis_id, : len(coeffs)] = coeffs
    high_pass = np.zeros((basis_count, 8))
    for column in range(8):
        high_pass[:, column] = (-1.0) ** column * low_pass[:, 7 - column]
    return low_pass.astype(np.float32), high_pass.astype(np.float32)


def iota(shape, axis):
    return lax.broadcasted_iota(jnp.int32, shape, axis)


def where_equal(left, right):
    return jnp.where(left == right, 1.0, 0.0)


def dot(left, right, contract=((1,), (0,))):
    return lax.dot_general(left, right, (contract, ((), ())), preferred_element_type=jnp.float32)


def phase_rows(width):
    row, column = iota((width, width), 0), iota((width, width), 1)
    span = width // PHASES
    return where_equal(column, PHASES * (row % span) + row // span).astype(jnp.bfloat16)


def back_matrix(m_dec):
    size = GROUP * GROUP
    pick = where_equal(iota((size, GROUP), 0) % GROUP, iota((size, GROUP), 1)).astype(jnp.bfloat16)
    place = where_equal(iota((GROUP, size), 0), iota((GROUP, size), 1) // GROUP).astype(jnp.bfloat16)
    wide = dot(dot(pick, m_dec, ((1,), (1,))).astype(jnp.bfloat16), place)
    return (wide * where_equal(iota((size, size), 0) // GROUP, iota((size, size), 1) % GROUP)).astype(jnp.bfloat16)


def forward_matrix(m_dec):
    size = GROUP * GROUP
    pick = where_equal(iota((size, GROUP), 0) // GROUP, iota((size, GROUP), 1)).astype(jnp.bfloat16)
    place = where_equal(iota((GROUP, size), 0), iota((GROUP, size), 1) % GROUP).astype(jnp.bfloat16)
    wide = dot(dot(pick, m_dec).astype(jnp.bfloat16), place)
    return (wide * where_equal(iota((size, size), 0) % GROUP, iota((size, size), 1) // GROUP)).astype(jnp.bfloat16)


def swap_rows(size_a, size_b):
    size = size_a * size_b
    row, column = iota((size, size), 0), iota((size, size), 1)
    return where_equal((row % size_a) * size_b + row // size_a, column).astype(jnp.bfloat16)


def gradient_kernel(second, patch_ref, beam_ref, vis_ref, beams_ref, m_ra_ref, m_dec_ref, *refs):
    if second:
        tiles_ref, out_ref, back, forward, ra_out, ra_in, table, total = refs
    else:
        out_ref, back, ra_out, table, total = refs
    channel = pl.program_id(0)
    channels = pl.num_programs(0)
    dec_rows, owned = vis_ref.shape[1], vis_ref.shape[2]
    width = m_ra_ref.shape[0]
    beam_count = beams_ref.shape[2]
    facets = out_ref.shape[0]

    @pl.when(channel == 0)
    def _():
        back[...] = back_matrix(m_dec_ref[...])
        order = phase_rows(width)
        ra_out[...] = dot(m_ra_ref[...], order, ((0,), (1,))).astype(jnp.bfloat16)
        if second:
            forward[...] = forward_matrix(m_dec_ref[...])
            ra_in[...] = dot(order, m_ra_ref[...]).astype(jnp.bfloat16)

    rows = beams_ref[0].reshape(dec_rows * beam_count, width)
    swapped = dot(swap_rows(dec_rows, beam_count), rows).astype(jnp.bfloat16)
    table[...] = (
        dot(swapped, phase_rows(width), ((1,), (1,)))
        .astype(jnp.bfloat16)
        .reshape(beam_count, dec_rows, width)
    )
    total[...] = jnp.zeros_like(total)

    def one_group(group, carry):
        first = pl.multiple_of(group * GROUP, GROUP)
        data = vis_ref[0, :, pl.ds(first, GROUP), :].reshape(dec_rows * GROUP, vis_ref.shape[3])
        patch_ids = [patch_ref[first + p] for p in range(GROUP)]
        slabs = [table[beam_ref[first + p]].astype(jnp.float32) for p in range(GROUP)]
        if second:
            weighted = jnp.concatenate(
                [
                    (slabs[p] * tiles_ref[patch_ids[p] * channels + channel].astype(jnp.float32)).astype(
                        jnp.bfloat16
                    )
                    for p in range(GROUP)
                ],
                axis=0,
            )
            along_ra = dot(weighted, ra_in[...]).astype(jnp.bfloat16)
            predicted = dot(forward[...], along_ra)
            data = (predicted - data.astype(jnp.float32)).astype(jnp.bfloat16)
        dec_back = dot(back[...], data).astype(jnp.bfloat16)
        patches = dot(dec_back, ra_out[...])
        for p in range(GROUP):
            patch = patches[p * dec_rows : (p + 1) * dec_rows]
            patch_grad = (slabs[p] * patch).astype(jnp.bfloat16).astype(jnp.float32)
            total[patch_ids[p]] = total[patch_ids[p]] + patch_grad
        return carry

    lax.fori_loop(0, owned // GROUP, one_group, 0)
    from_left = iota((dec_rows, width), 1) % SPAN >= SPAN // 2
    tiles = total.shape[0]

    def one_facet(facet, carry):
        own = 2 * facet
        left, right = lax.rem(own + tiles - 1, tiles), lax.rem(own + 2, tiles)
        out_ref[facet, 0, 0] = total[own].astype(jnp.bfloat16)
        out_ref[facet, 1, 0] = total[own + 1].astype(jnp.bfloat16)
        out_ref[facet, 2, 0] = jnp.where(from_left, total[left], total[right]).astype(jnp.bfloat16)
        return carry

    lax.fori_loop(0, facets, one_facet, 0)


def gradient_call(patch_of, beam_of, vis, beams, m_ra, m_dec, facets, tiles=None):
    channels, dec_rows, owned, samples = vis.shape
    width = m_ra.shape[0]
    beam_count = beams.shape[2]
    second = tiles is not None
    whole = lambda c, *_: (0, 0)
    in_specs = [
        pl.BlockSpec((1, dec_rows, owned, samples), lambda c, *_: (c, 0, 0, 0)),
        pl.BlockSpec((1, dec_rows, beam_count, width), lambda c, *_: (c, 0, 0, 0)),
        pl.BlockSpec(m_ra.shape, whole),
        pl.BlockSpec(m_dec.shape, whole),
    ]
    operands = [vis, beams, m_ra, m_dec]
    size = GROUP * GROUP
    back = pltpu.VMEM((size, size), jnp.bfloat16)
    ra_out = pltpu.VMEM((samples, width), jnp.bfloat16)
    ra_in = pltpu.VMEM((width, samples), jnp.bfloat16)
    tail = [
        pltpu.VMEM((beam_count, dec_rows, width), jnp.bfloat16),
        pltpu.VMEM((2 * facets, dec_rows, width), jnp.float32),
    ]
    if second:
        in_specs.append(pl.BlockSpec(tiles.shape, lambda c, *_: (0, 0, 0)))
        operands.append(tiles)
        scratch = [back, back, ra_out, ra_in] + tail
    else:
        scratch = [back, ra_out] + tail
    work = channels * owned * samples * dec_rows
    return pl.pallas_call(
        functools.partial(gradient_kernel, second),
        out_shape=jax.ShapeDtypeStruct((facets, SLOTS, channels, dec_rows, width), jnp.bfloat16),
        grid_spec=pltpu.PrefetchScalarGridSpec(
            num_scalar_prefetch=2,
            grid=(channels,),
            in_specs=in_specs,
            out_specs=pl.BlockSpec((facets, SLOTS, 1, dec_rows, width), lambda c, *_: (0, 0, c, 0, 0)),
            scratch_shapes=scratch,
        ),
        compiler_params=pltpu.CompilerParams(vmem_limit_bytes=48 << 20),
        cost_estimate=pl.CostEstimate(
            flops=(4 if second else 2) * 256 * work, bytes_accessed=2 * work, transcendentals=0
        ),
        name="second_gradient" if second else "first_gradient",
    )(patch_of, beam_of, *operands)


def shrink(values, bound):
    return values - jnp.clip(values, -bound, bound)


def combine(terms):
    total = None
    for factor, value in terms:
        if factor == 0.0:
            continue
        term = value * jnp.float32(factor)
        total = term if total is None else total + term
    return total


def dec_analysis(rows, low, high):
    count = len(rows)
    half = count // 2
    lows = [combine([(low[j], rows[(2 * k + j) % count]) for j in range(8)]) for k in range(half)]
    highs = [combine([(high[j], rows[(2 * k + j) % count]) for j in range(8)]) for k in range(half)]
    return lows + highs


def dec_synthesis(rows, low, high):
    count = len(rows)
    half = count // 2
    gathered = [[] for _ in range(count)]
    for k in range(half):
        for j in range(8):
            gathered[(2 * k + j) % count].append((low[j], rows[k]))
            gathered[(2 * k + j) % count].append((high[j], rows[half + k]))
    return [combine(terms) for terms in gathered]


def prox_kernel(second, recv_ref, thresholds_ref, step_ref, *refs):
    if second:
        first_ref, out_ref, summed, columns, natural = refs
    else:
        first_ref, out_ref, summed, columns, natural = refs
    sources, rows = recv_ref.shape[0], recv_ref.shape[1]
    dec_rows = first_ref.shape[1]
    channels = step_ref.shape[0]
    half = 4
    shape = (8, LANES)
    upper = iota(shape, 0) >= half
    channel = iota(shape, 0) % half
    lane = iota(shape, 1)
    block = lane // SPAN

    def add_source(source, total):
        return total + recv_ref[source].astype(jnp.float32)

    total = lax.fori_loop(1, sources, add_source, recv_ref[0].astype(jnp.float32))
    summed[:rows] = total
    summed[rows:] = total[rows - channels * dec_rows :]

    def spread(scalars):
        value = jnp.full(shape, scalars[channels - 1], jnp.float32)
        for c in range(channels - 1):
            value = jnp.where(channel == c, scalars[c], value)
        return value

    step = spread([step_ref[c] for c in range(channels)])
    roll = lambda value, shift: pltpu.roll(value, shift % LANES, 1)
    swap = lambda value: pltpu.roll(value, half, 0)
    halves = lambda low, high: jnp.where(upper, high, low)

    for d in range(dec_rows):
        own = summed[pl.ds(d, 8, stride=dec_rows), :]
        edge = summed[pl.ds(8 * dec_rows + d, 8, stride=dec_rows), :]
        other = swap(own)
        own_32, own_64 = roll(own, -32), roll(own, -64)
        other_up, other_64 = roll(other, 32), roll(other, -64)
        edge_32, edge_64, edge_96 = roll(edge, 32), roll(edge, 64), roll(edge, 96)
        evens = jnp.where(
            block == 0,
            halves(own, other_64),
            jnp.where(
                block == 1,
                halves(other_up, own_32),
                jnp.where(block == 2, halves(edge_64, edge), halves(edge_96, edge_32)),
            ),
        )
        odds = jnp.where(
            block == 0,
            halves(own_32, other_up),
            jnp.where(
                block == 1,
                halves(other, own_64),
                jnp.where(block == 2, halves(edge_32, edge_96), halves(edge_64, edge)),
            ),
        )
        evens, odds = step * evens, step * odds
        if second:
            evens, odds = first_ref[0, d] - evens, first_ref[1, d] - odds
        columns[0, d], columns[1, d] = evens, odds
        for e, value in enumerate((evens, odds)):
            later = roll(value, -1)
            middle = swap(halves(later, value))
            columns[2 + e, d] = middle
            columns[4 + e, d] = later
            columns[6 + e, d] = roll(middle, -1)

    low_pass, high_pass = filter_table(BASES)
    result = [[None] * dec_rows for _ in range(2)]
    for b in range(BASES):
        low, high = [float(v) for v in low_pass[b]], [float(v) for v in high_pass[b]]
        bound = spread([thresholds_ref[b, c] for c in range(channels)]) * step
        ra_low = [combine([(low[j], columns[j, d]) for j in range(8)]) for d in range(dec_rows)]
        ra_high = [combine([(high[j], columns[j, d]) for j in range(8)]) for d in range(dec_rows)]
        coarse_a = dec_analysis(ra_low, low, high)
        coarse_b = [shrink(v, bound) for v in dec_analysis(ra_high, low, high)]
        smooth, detail = coarse_a[: dec_rows // 2], [shrink(v, bound) for v in coarse_a[dec_rows // 2 :]]
        pair = lambda even, odd: jnp.where(upper, jnp.float32(odd), jnp.float32(even))
        fine = []
        for value in smooth:
            moved = [value] + [roll(value, -i) for i in (1, 2, 3)]
            lows = sum(pair(low[2 * i], low[2 * i + 1]) * moved[i] for i in range(4))
            highs = sum(pair(high[2 * i], high[2 * i + 1]) * moved[i] for i in range(4))
            fine.append(halves(lows, highs) + swap(halves(highs, lows)))
        fine = [shrink(v, bound) for v in dec_analysis(fine, low, high)]
        fine = dec_synthesis(fine, low, high)
        smooth = []
        for value in fine:
            moved = [value] + [roll(value, i) for i in (1, 2, 3)]
            evens = sum(pair(low[2 * i], high[2 * i]) * moved[i] for i in range(4))
            odds = sum(pair(low[2 * i + 1], high[2 * i + 1]) * moved[i] for i in range(4))
            smooth.append(halves(evens, odds) + swap(halves(odds, evens)))
        top_low = dec_synthesis(smooth + detail, low, high)
        top_high = dec_synthesis(coarse_b, low, high)
        for d in range(dec_rows):
            shifted = []
            for value in (top_low[d], top_high[d]):
                other = swap(value)
                before = halves(roll(other, 1), other)
                shifted.append([value, before, roll(value, 1), roll(before, 1)])
            for e in range(2):
                terms = []
                for i in range(4):
                    terms.append((low[2 * i + e], shifted[0][i]))
                    terms.append((high[2 * i + e], shifted[1][i]))
                value = combine(terms)
                result[e][d] = value if b == 0 else result[e][d] + value

    for d in range(dec_rows):
        evens = jnp.maximum(result[0][d] * (1.0 / BASES), 0.0)
        odds = jnp.maximum(result[1][d] * (1.0 / BASES), 0.0)
        if not second:
            first_ref[0, d], first_ref[1, d] = evens, odds
        even_other, odd_other = swap(evens), swap(odds)
        value = jnp.where(
            block == 0,
            halves(evens, roll(even_other, -32)),
            jnp.where(
                block == 1,
                halves(roll(odds, 32), odd_other),
                jnp.where(
                    block == 2,
                    halves(roll(even_other, 64), roll(evens, 32)),
                    halves(roll(odd_other, 96), roll(odds, 64)),
                ),
            ),
        )
        natural[pl.ds(d, 8, stride=dec_rows), :] = value
    if second:
        order = phase_rows(LANES).astype(jnp.float32)
        image = lax.dot_general(
            natural[...],
            order,
            (((1,), (0,)), ((), ())),
            precision=lax.Precision.HIGHEST,
            preferred_element_type=jnp.float32,
        )
        for tile in range(2):
            for c in range(channels):
                start = (tile * channels + c) * dec_rows
                out_ref[c, :, tile * LANES : (tile + 1) * LANES] = image[start : start + dec_rows]
    else:
        out_ref[...] = natural[...].astype(jnp.bfloat16)


def prox_call(received, thresholds, step_size, dec_rows, first=None):
    second = first is not None
    sources = received.shape[0]
    channels = step_size.shape[0]
    received = received.reshape(sources, SLOTS * channels * dec_rows, LANES)
    vmem = pl.BlockSpec(memory_space=pltpu.VMEM)
    smem = pl.BlockSpec(memory_space=pltpu.SMEM)
    held = jax.ShapeDtypeStruct((2, dec_rows, 8, LANES), jnp.float32)
    if second:
        out_shape = jax.ShapeDtypeStruct((channels, dec_rows, RA_DEV), jnp.float32)
        out_specs = vmem
    else:
        out_shape = (held, jax.ShapeDtypeStruct((2 * channels * dec_rows, LANES), jnp.bfloat16))
        out_specs = (vmem, vmem)
    return pl.pallas_call(
        functools.partial(prox_kernel, second),
        out_shape=out_shape,
        in_specs=[vmem, smem, smem] + ([vmem] if second else []),
        out_specs=out_specs,
        scratch_shapes=[
            pltpu.VMEM((4 * channels * dec_rows, LANES), jnp.float32),
            pltpu.VMEM((8, dec_rows, 8, LANES), jnp.float32),
            pltpu.VMEM((2 * channels * dec_rows, LANES), jnp.float32),
        ],
        compiler_params=pltpu.CompilerParams(vmem_limit_bytes=32 << 20),
        name="second_prox" if second else "first_prox",
    )(received, thresholds, step_size, *([first] if second else []))


def local(vis, beams, m_ra, m_dec, facet_of, tile_of, beam_of, step_size, thresholds):
    facets = lax.axis_size("ra")
    channels, dec_rows, owned, samples = vis.shape
    width = m_ra.shape[0]
    patch_of = facet_of[:, 0] * (RA_DEV // width) + tile_of

    def exchange(sums):
        return lax.all_to_all(sums, "ra", split_axis=0, concat_axis=0, tiled=True)

    sums = gradient_call(patch_of, beam_of, vis, beams, m_ra, m_dec, facets)
    first, tiles = prox_call(exchange(sums), thresholds, step_size, dec_rows)
    tiles = lax.all_gather(tiles, "ra", axis=0, tiled=True)
    tiles = tiles.reshape(facets * 2 * channels, dec_rows, width)
    sums = gradient_call(patch_of, beam_of, vis, beams, m_ra, m_dec, facets, tiles)
    return prox_call(exchange(sums), thresholds, step_size, dec_rows, first)


def solution(mesh):
    in_specs = (
        P(None, "strip", "ra", None),
        P(None, "strip", None, None),
        P(),
        P(),
        P(("strip", "ra"), None),
        P(("strip", "ra")),
        P(("strip", "ra")),
        P(),
        P(),
    )
    out_specs = P(None, "strip", "ra")
    return jax.shard_map(local, mesh=mesh, in_specs=in_specs, out_specs=out_specs, check_vma=False)
```

time: 455 us -> 132 us (0.29); the launches traced: 447 us -> 131 us
  waiting for transfers between devices: 186 us -> 0 us
  matrix products: 79.2 us -> 0 us
  starting transfers between devices: 76.7 us -> 0 us
  local copies, waits for them, and re-layouts: 70.3 us -> 3.2 us
  Pallas kernels: 0 us -> 55.6 us
  blocking collectives: 18.7 us -> 71.4 us
  other arithmetic: 14.7 us -> 0.69 us
    all_to_all x3 -> x0, waiting for transfers between devices: 153 us -> none  [the longest x2 153 us: spread(): lax.all_to_all(outgoing, 'ra', split_axis=2, concat_axis=2, tiled=True)]
    dot_general x24 -> x0, matrix products: 79.2 us -> none  [the longest x2 31.4 us: spread(): jnp.einsum('ed,cepk->cdpk', m_dec, residual, preferred_element_type=jnp.f...]
    ppermute x12 -> x0, starting transfers between devices: 58.6 us -> none  [shifted(): return lax.ppermute(value, axis, pairs)]
    pallas_call x0 -> x4, Pallas kernels: none -> 55.6 us  [the longest x2 45.3 us: gradient_call(): pl.pallas_call(functools.partial(gradient_kernel, second), out_shape=jax....]
    all_to_all x0 -> x2, blocking collectives: none -> 50.3 us  [exchange(): return lax.all_to_all(sums, 'ra', split_axis=0, concat_axis=0, tiled=True)]
    scatter x5 -> x0, local copies, waits for them, and re-layouts: 44.5 us -> none  [the longest x4 43.4 us: spread(): outgoing = jnp.zeros((channels, dec_rows, slot_count, patch_width), jnp.b...]
    ppermute x12 -> x0, waiting for transfers between devices: 32.8 us -> none  [shifted(): return lax.ppermute(value, axis, pairs)]
    all_to_all x3 -> x0, starting transfers between devices: 18.1 us -> none  [the longest x2 10.7 us: spread(): lax.all_to_all(outgoing, 'ra', split_axis=2, concat_axis=2, tiled=True)]
  transfers between devices with their start and end apart: 15 -> 0, of which waited for: 12 -> 0; matrix products, arithmetic and copies ran while one was open for 14% -> 0% of each run, Pallas kernels for 0% -> 0%
where the time goes in v1:
time: 132 us; the launch traced here: 131 us
  blocking collectives  71.4 us (54%)
  Pallas kernels  55.6 us (42%)
  local copies, waits for them, and re-layouts  3.2 us (2%)
    all_to_all x2, blocking collectives, exchange(): return lax.all_to_all(sums, 'ra', split_axis=0, concat_axis=0, tiled=True)  50.3 us
    pallas_call x2, Pallas kernels, gradient_call(): pl.pallas_call(functools.partial(gradient_kernel, second), out_shape=jax....  45.3 us
    all_gather x1, blocking collectives, local(): tiles = lax.all_gather(tiles, 'ra', axis=0, tiled=True)  21.1 us
    pallas_call x2, Pallas kernels, prox_call(): pl.pallas_call(functools.partial(prox_kernel, second), out_shape=out_shap...  10.2 us
    unnamed x12, local copies, waits for them, and re-layouts  3.2 us

profile of v1, /device:TPU:0, one launch (start us, length us, event | category | flops | bytes accessed | tf_op | source)
XLA Modules:
  0.0 130.9 jit_solution(15262900509846099697)
XLA Ops:
  0.0 0.0 copy-start.4
  0.0 0.7 bitcast_add_fusion.patch_ref
  0.7 0.0 copy-start
  0.7 0.9 copy-done
  1.6 0.0 copy-start.1
  1.6 0.9 copy-done.1
  2.5 0.0 copy-start.3
  2.5 0.7 copy-done.3
  3.2 0.0 copy-start.5
  3.2 0.7 copy-done.5
  3.9 0.0 copy-start.2
  3.9 16.5 %first_gradient.1 = bf16[16,3,4,16,128]{4,3,2,1,0:T(8,128)(2,1)S(1)} custom-call(s32[128]{0:T(128)S(1)} %bitcast_add_fusion.patch_ref, s32[128]{0:T(128)S(1)} %copy-done.5, bf16[4,16,128,512]{3,2,1,0:T(8,128)(2,1)} %vis_ref.3, bf16[4,16,16,128]{3,2,1,0:T(8,128)(2,1)S(1)} %copy-done, bf16[128,512]{1,0:T(8,128)(2,1)S(1)} %copy-done.1, bf16[16,16]{1,0:T(8,128)(2,1)S(1)} %copy-done.3), custom_call_target="tpu_custom_call" | custom-call | flops 2147483648 | bytes 8388608 | tf_op jit(solution)/shard_map/first_gradient/pallas_call | solution.py:193
  20.4 27.5 %all_to_all.10 = bf16[16,3,4,16,128]{4,3,2,1,0:T(8,128)(2,1)S(1)} all-to-all(bf16[16,3,4,16,128]{4,3,2,1,0:T(8,128)(2,1)S(1)} %first_gradient.1), channel_id=1, replica_groups=mesh['strip'=2,'ra'=16] {'ra'}, dimensions={0} | all-to-all | bytes 1572864 | tf_op jit(solution)/shard_map/all_to_all | solution.py:427
  47.9 0.0 copy-done.4
  47.9 0.0 copy-done.2
  47.9 5.5 %first_prox.1 = (f32[2,16,8,128]{3,2,1,0:T(8,128)S(1)}, bf16[128,128]{1,0:T(8,128)(2,1)S(1)}) custom-call(bf16[16,192,128]{2,1,0:T(8,128)(2,1)S(1)} %bitcast.5, f32[4,4]{1,0:T(4,128)S(1)} %copy-done.2, f32[4]{0:T(128)S(1)} %copy-done.4), custom_call_target="tpu_custom_call" | custom-call | tf_op jit(solution)/shard_map/first_prox/pallas_call | solution.py:405
  53.4 21.1 %all_gather.3 = bf16[2048,128]{1,0:T(8,128)(2,1)S(1)} all-gather(bf16[128,128]{1,0:T(8,128)(2,1)S(1)} %get-tuple-element.7), channel_id=1, replica_groups=mesh['strip'=2,'ra'=16] {'ra'}, dimensions={0}, use_global_device_ids=true | all-gather | bytes 557056 | tf_op jit(solution)/shard_map/all_gather | solution.py:431
  74.5 28.8 %second_gradient.1 = bf16[16,3,4,16,128]{4,3,2,1,0:T(8,128)(2,1)S(1)} custom-call(s32[128]{0:T(128)S(1)} %bitcast_add_fusion.patch_ref, s32[128]{0:T(128)S(1)} %copy-done.5, bf16[4,16,128,512]{3,2,1,0:T(8,128)(2,1)} %vis_ref.3, bf16[4,16,16,128]{3,2,1,0:T(8,128)(2,1)S(1)} %copy-done, bf16[128,512]{1,0:T(8,128)(2,1)S(1)} %copy-done.1, ...), custom_call_target="tpu_custom_call" | custom-call | flops 4294967296 | bytes 8388608 | tf_op jit(solution)/shard_map/second_gradient/pallas_call | solution.py:193
  103.3 22.8 %all_to_all.11 = bf16[16,3,4,16,128]{4,3,2,1,0:T(8,128)(2,1)S(1)} all-to-all(bf16[16,3,4,16,128]{4,3,2,1,0:T(8,128)(2,1)S(1)} %second_gradient.1), channel_id=1, replica_groups=mesh['strip'=2,'ra'=16] {'ra'}, dimensions={0} | all-to-all | bytes 1572864 | tf_op jit(solution)/shard_map/all_to_all | solution.py:427
  126.1 4.8 %second_prox.1 = f32[4,16,256]{2,1,0:T(8,128)} custom-call(bf16[16,192,128]{2,1,0:T(8,128)(2,1)S(1)} %bitcast.6, f32[4,4]{1,0:T(4,128)S(1)} %copy-done.2, f32[4]{0:T(128)S(1)} %copy-done.4, f32[2,16,8,128]{3,2,1,0:T(8,128)S(1)} %get-tuple-element.8.refs_0_), custom_call_target="tpu_custom_call" | custom-call | tf_op jit(solution)/shard_map/second_prox/pallas_call | solution.py:405
Async XLA Ops:
  0.0 47.9 %copy-start.4 = (f32[4]{0:T(128)S(1)}, f32[4]{0:T(128)}, u32[]{:S(2)}) copy-start(f32[4]{0:T(128)} %step_ref.3) | copy-start | bytes 52
  0.7 0.9 copy-start
  1.6 0.9 copy-start.1
  2.5 0.7 copy-start.3
  3.2 0.7 copy-start.5
  3.9 44.0 %copy-start.2 = (f32[4,4]{1,0:T(4,128)S(1)}, f32[4,4]{1,0:T(4,128)}, u32[]{:S(2)}) copy-start(f32[4,4]{1,0:T(4,128)} %thresholds_ref.3) | copy-start | bytes 196

commit v2 on v1

--- a/solution.py
+++ b/solution.py
@@ -15,6 +15,7 @@
 LANES = 128
 SPAN = LANES // PHASES
 SLOTS = 3
+CHUNK = 256
 
 daub_coeffs = (
     (0.7071067811865476, 0.7071067811865476),
@@ -93,9 +94,9 @@
 
 def gradient_kernel(second, patch_ref, beam_ref, vis_ref, beams_ref, m_ra_ref, m_dec_ref, *refs):
     if second:
-        tiles_ref, out_ref, back, forward, ra_out, ra_in, table, total = refs
+        tiles_ref, out_ref, back, forward, ra_out, ra_in, table, total, along, weighted = refs
     else:
-        out_ref, back, ra_out, table, total = refs
+        out_ref, back, ra_out, table, total, along, weighted = refs
     channel = pl.program_id(0)
     channels = pl.num_programs(0)
     dec_rows, owned = vis_ref.shape[1], vis_ref.shape[2]
@@ -121,33 +122,32 @@
     )
     total[...] = jnp.zeros_like(total)
 
-    def one_group(group, carry):
-        first = pl.multiple_of(group * GROUP, GROUP)
-        data = vis_ref[0, :, pl.ds(first, GROUP), :].reshape(dec_rows * GROUP, vis_ref.shape[3])
-        patch_ids = [patch_ref[first + p] for p in range(GROUP)]
-        slabs = [table[beam_ref[first + p]].astype(jnp.float32) for p in range(GROUP)]
+    samples = vis_ref.shape[3]
+    size = GROUP * dec_rows
+    groups = owned // GROUP
+
+    if second:
+        for p in range(owned):
+            weighted[p * dec_rows : (p + 1) * dec_rows] = (
+                table[beam_ref[p]].astype(jnp.float32)
+                * tiles_ref[patch_ref[p] * channels + channel].astype(jnp.float32)
+            ).astype(jnp.bfloat16)
+        for m in range(0, owned * dec_rows, CHUNK):
+            along[m : m + CHUNK] = dot(weighted[m : m + CHUNK], ra_in[...]).astype(jnp.bfloat16)
+    for group in range(groups):
+        rows = slice(group * size, (group + 1) * size)
+        data = vis_ref[0, :, group * GROUP : (group + 1) * GROUP, :].reshape(size, samples)
         if second:
-            weighted = jnp.concatenate(
-                [
-                    (slabs[p] * tiles_ref[patch_ids[p] * channels + channel].astype(jnp.float32)).astype(
-                        jnp.bfloat16
-                    )
-                    for p in range(GROUP)
-                ],
-                axis=0,
-            )
-            along_ra = dot(weighted, ra_in[...]).astype(jnp.bfloat16)
-            predicted = dot(forward[...], along_ra)
+            predicted = dot(forward[...], along[rows])
             data = (predicted - data.astype(jnp.float32)).astype(jnp.bfloat16)
-        dec_back = dot(back[...], data).astype(jnp.bfloat16)
-        patches = dot(dec_back, ra_out[...])
-        for p in range(GROUP):
-            patch = patches[p * dec_rows : (p + 1) * dec_rows]
-            patch_grad = (slabs[p] * patch).astype(jnp.bfloat16).astype(jnp.float32)
-            total[patch_ids[p]] = total[patch_ids[p]] + patch_grad
-        return carry
-
-    lax.fori_loop(0, owned // GROUP, one_group, 0)
+        along[rows] = dot(back[...], data).astype(jnp.bfloat16)
+    for m in range(0, owned * dec_rows, CHUNK):
+        patches = dot(along[m : m + CHUNK], ra_out[...])
+        for i in range(CHUNK // dec_rows):
+            p = m // dec_rows + i
+            patch = patches[i * dec_rows : (i + 1) * dec_rows]
+            patch_grad = (table[beam_ref[p]].astype(jnp.float32) * patch).astype(jnp.bfloat16).astype(jnp.float32)
+            total[patch_ref[p]] = total[patch_ref[p]] + patch_grad
     from_left = iota((dec_rows, width), 1) % SPAN >= SPAN // 2
     tiles = total.shape[0]
 
@@ -159,7 +159,7 @@
         out_ref[facet, 2, 0] = jnp.where(from_left, total[left], total[right]).astype(jnp.bfloat16)
         return carry
 
-    lax.fori_loop(0, facets, one_facet, 0)
+    lax.fori_loop(0, facets, one_facet, 0, unroll=4)
 
 
 def gradient_call(patch_of, beam_of, vis, beams, m_ra, m_dec, facets, tiles=None):
@@ -182,6 +182,8 @@
     tail = [
         pltpu.VMEM((beam_count, dec_rows, width), jnp.bfloat16),
         pltpu.VMEM((2 * facets, dec_rows, width), jnp.float32),
+        pltpu.VMEM((owned * dec_rows, samples), jnp.bfloat16),
+        pltpu.VMEM((owned * dec_rows, width), jnp.bfloat16),
     ]
     if second:
         in_specs.append(pl.BlockSpec(tiles.shape, lambda c, *_: (0, 0, 0)))
@@ -421,6 +423,9 @@
     facets = lax.axis_size("ra")
     channels, dec_rows, owned, samples = vis.shape
     width = m_ra.shape[0]
+    beams, m_ra, m_dec, beam_of = (
+        pltpu.with_memory_space_constraint(x, pltpu.HBM) for x in (beams, m_ra, m_dec, beam_of)
+    )
     patch_of = facet_of[:, 0] * (RA_DEV // width) + tile_of
 
     def exchange(sums):

time: 132 us -> 111 us (0.84)
  Pallas kernels: 55.6 us -> 38.4 us
  local copies, waits for them, and re-layouts: 3.2 us -> 0.01 us
    pallas_call x2, Pallas kernels: 45.3 us -> 28.1 us  [gradient_call(): pl.pallas_call(functools.partial(gradient_kernel, second), out_shape=jax....]
    unnamed x12 -> x4, local copies, waits for them, and re-layouts: 3.2 us -> 0.01 us
where the time goes in v2:
time: 111 us
  blocking collectives  71.4 us (64%)
  Pallas kernels  38.4 us (35%)
    all_to_all x2, blocking collectives, exchange(): return lax.all_to_all(sums, 'ra', split_axis=0, concat_axis=0, tiled=True)  50.3 us
    pallas_call x2, Pallas kernels, gradient_call(): pl.pallas_call(functools.partial(gradient_kernel, second), out_shape=jax....  28.1 us
    all_gather x1, blocking collectives, local(): tiles = lax.all_gather(tiles, 'ra', axis=0, tiled=True)  21.1 us
    pallas_call x2, Pallas kernels, prox_call(): pl.pallas_call(functools.partial(prox_kernel, second), out_shape=out_shap...  10.2 us

profile of v2, /device:TPU:0, one launch (start us, length us, event | category | flops | bytes accessed | tf_op | source)
XLA Modules:
  0.0 110.5 jit_solution(5237086702053857055)
XLA Ops:
  0.0 0.0 copy-start
  0.0 0.0 copy-start.1
  0.0 0.7 bitcast_add_fusion.patch_ref
  0.7 9.3 %first_gradient.1 = bf16[16,3,4,16,128]{4,3,2,1,0:T(8,128)(2,1)S(1)} custom-call(s32[128]{0:T(128)S(1)} %bitcast_add_fusion.patch_ref, s32[128]{0:T(128)} %beam_ref.3, bf16[4,16,128,512]{3,2,1,0:T(8,128)(2,1)} %vis_ref.3, bf16[4,16,16,128]{3,2,1,0:T(8,128)(2,1)} %beams_ref.3, bf16[128,512]{1,0:T(8,128)(2,1)} %m_ra_ref.3, bf16[16,16]{1,0:T(8,128)(2,1)} %m_dec_ref.3), custom_call_target="tpu_custom_call" | custom-call | flops 2147483648 | bytes 8388608 | tf_op jit(solution)/shard_map/first_gradient/pallas_call | solution.py:195
  10.0 27.5 %all_to_all.10 = bf16[16,3,4,16,128]{4,3,2,1,0:T(8,128)(2,1)S(1)} all-to-all(bf16[16,3,4,16,128]{4,3,2,1,0:T(8,128)(2,1)S(1)} %first_gradient.1), channel_id=1, replica_groups=mesh['strip'=2,'ra'=16] {'ra'}, dimensions={0} | all-to-all | bytes 1572864 | tf_op jit(solution)/shard_map/all_to_all | solution.py:432
  37.5 0.0 copy-done
  37.5 0.0 copy-done.1
  37.5 5.5 %first_prox.1 = (f32[2,16,8,128]{3,2,1,0:T(8,128)S(1)}, bf16[128,128]{1,0:T(8,128)(2,1)S(1)}) custom-call(bf16[16,192,128]{2,1,0:T(8,128)(2,1)S(1)} %bitcast.5, f32[4,4]{1,0:T(4,128)S(1)} %copy-done, f32[4]{0:T(128)S(1)} %copy-done.1), custom_call_target="tpu_custom_call" | custom-call | tf_op jit(solution)/shard_map/first_prox/pallas_call | solution.py:407
  42.9 21.1 %all_gather.3 = bf16[2048,128]{1,0:T(8,128)(2,1)S(1)} all-gather(bf16[128,128]{1,0:T(8,128)(2,1)S(1)} %get-tuple-element.7), channel_id=1, replica_groups=mesh['strip'=2,'ra'=16] {'ra'}, dimensions={0}, use_global_device_ids=true | all-gather | bytes 557056 | tf_op jit(solution)/shard_map/all_gather | solution.py:436
  64.0 18.9 %second_gradient.1 = bf16[16,3,4,16,128]{4,3,2,1,0:T(8,128)(2,1)S(1)} custom-call(s32[128]{0:T(128)S(1)} %bitcast_add_fusion.patch_ref, s32[128]{0:T(128)} %beam_ref.3, bf16[4,16,128,512]{3,2,1,0:T(8,128)(2,1)} %vis_ref.3, bf16[4,16,16,128]{3,2,1,0:T(8,128)(2,1)} %beams_ref.3, bf16[128,512]{1,0:T(8,128)(2,1)} %m_ra_ref.3, bf16[16,16]{1,0:T(8,128)(2,1)} %m_dec_ref.3, ...), custom_call_target="tpu_custom_call" | custom-call | flops 4294967296 | bytes 8388608 | tf_op jit(solution)/shard_map/second_gradient/pallas_call | solution.py:195
  82.9 22.8 %all_to_all.11 = bf16[16,3,4,16,128]{4,3,2,1,0:T(8,128)(2,1)S(1)} all-to-all(bf16[16,3,4,16,128]{4,3,2,1,0:T(8,128)(2,1)S(1)} %second_gradient.1), channel_id=1, replica_groups=mesh['strip'=2,'ra'=16] {'ra'}, dimensions={0} | all-to-all | bytes 1572864 | tf_op jit(solution)/shard_map/all_to_all | solution.py:432
  105.7 4.8 %second_prox.1 = f32[4,16,256]{2,1,0:T(8,128)} custom-call(bf16[16,192,128]{2,1,0:T(8,128)(2,1)S(1)} %bitcast.6, f32[4,4]{1,0:T(4,128)S(1)} %copy-done, f32[4]{0:T(128)S(1)} %copy-done.1, f32[2,16,8,128]{3,2,1,0:T(8,128)S(1)} %get-tuple-element.8.refs_0_), custom_call_target="tpu_custom_call" | custom-call | tf_op jit(solution)/shard_map/second_prox/pallas_call | solution.py:407
Async XLA Ops:
  0.0 37.5 %copy-start = (f32[4,4]{1,0:T(4,128)S(1)}, f32[4,4]{1,0:T(4,128)}, u32[]{:S(2)}) copy-start(f32[4,4]{1,0:T(4,128)} %thresholds_ref.3) | copy-start | bytes 196
  0.0 37.5 %copy-start.1 = (f32[4]{0:T(128)S(1)}, f32[4]{0:T(128)}, u32[]{:S(2)}) copy-start(f32[4]{0:T(128)} %step_ref.3) | copy-start | bytes 52

commit v3 on v2

--- a/solution.py
+++ b/solution.py
@@ -92,17 +92,25 @@
     return where_equal((row % size_a) * size_b + row // size_a, column).astype(jnp.bfloat16)
 
 
-def gradient_kernel(second, patch_ref, beam_ref, vis_ref, beams_ref, m_ra_ref, m_dec_ref, *refs):
-    if second:
-        tiles_ref, out_ref, back, forward, ra_out, ra_in, table, total, along, weighted = refs
+def gradient_kernel(second, paired, patch_ref, beam_ref, *refs):
+    if paired:
+        me_ref, *refs = refs
+    if second:
+        slot_ref, *refs = refs
+    vis_ref, beams_ref, m_ra_ref, m_dec_ref, *refs = refs
+    if second:
+        tiles_ref, *refs = refs
+    outs, refs = refs[: 1 + paired], refs[1 + paired :]
+    if second:
+        back, forward, ra_out, ra_in, table, total, along, weighted = refs
     else:
-        out_ref, back, ra_out, table, total, along, weighted = refs
+        back, ra_out, table, total, along, weighted = refs
     channel = pl.program_id(0)
     channels = pl.num_programs(0)
     dec_rows, owned = vis_ref.shape[1], vis_ref.shape[2]
     width = m_ra_ref.shape[0]
     beam_count = beams_ref.shape[2]
-    facets = out_ref.shape[0]
+    facets = outs[0].shape[0]
 
     @pl.when(channel == 0)
     def _():
@@ -130,7 +138,7 @@
         for p in range(owned):
             weighted[p * dec_rows : (p + 1) * dec_rows] = (
                 table[beam_ref[p]].astype(jnp.float32)
-                * tiles_ref[patch_ref[p] * channels + channel].astype(jnp.float32)
+                * tiles_ref[slot_ref[p] * channels + channel].astype(jnp.float32)
             ).astype(jnp.bfloat16)
         for m in range(0, owned * dec_rows, CHUNK):
             along[m : m + CHUNK] = dot(weighted[m : m + CHUNK], ra_in[...]).astype(jnp.bfloat16)
@@ -151,22 +159,25 @@
     from_left = iota((dec_rows, width), 1) % SPAN >= SPAN // 2
     tiles = total.shape[0]
 
-    def one_facet(facet, carry):
-        own = 2 * facet
-        left, right = lax.rem(own + tiles - 1, tiles), lax.rem(own + 2, tiles)
-        out_ref[facet, 0, 0] = total[own].astype(jnp.bfloat16)
-        out_ref[facet, 1, 0] = total[own + 1].astype(jnp.bfloat16)
-        out_ref[facet, 2, 0] = jnp.where(from_left, total[left], total[right]).astype(jnp.bfloat16)
+    def one_facet(index, carry):
+        for side, out_ref in enumerate(outs):
+            facet = (2 * index + side) ^ me_ref[0] if paired else index
+            own = 2 * facet
+            left, right = lax.rem(own + tiles - 1, tiles), lax.rem(own + 2, tiles)
+            out_ref[index, 0, 0] = total[own].astype(out_ref.dtype)
+            out_ref[index, 1, 0] = total[own + 1].astype(out_ref.dtype)
+            out_ref[index, 2, 0] = jnp.where(from_left, total[left], total[right]).astype(out_ref.dtype)
         return carry
 
     lax.fori_loop(0, facets, one_facet, 0, unroll=4)
 
 
-def gradient_call(patch_of, beam_of, vis, beams, m_ra, m_dec, facets, tiles=None):
+def gradient_call(patch_of, beam_of, vis, beams, m_ra, m_dec, facets, me=None, slot_of=None, tiles=None):
     channels, dec_rows, owned, samples = vis.shape
     width = m_ra.shape[0]
     beam_count = beams.shape[2]
-    second = tiles is not None
+    second, paired = tiles is not None, me is not None
+    scalars = [patch_of, beam_of] + [me] * paired + [slot_of] * second
     whole = lambda c, *_: (0, 0)
     in_specs = [
         pl.BlockSpec((1, dec_rows, owned, samples), lambda c, *_: (c, 0, 0, 0)),
@@ -192,14 +203,16 @@
     else:
         scratch = [back, ra_out] + tail
     work = channels * owned * samples * dec_rows
+    kept, sum_type = (facets // 2, jnp.float32) if paired else (facets, jnp.bfloat16)
+    out_shape = jax.ShapeDtypeStruct((kept, SLOTS, channels, dec_rows, width), sum_type)
     return pl.pallas_call(
-        functools.partial(gradient_kernel, second),
-        out_shape=jax.ShapeDtypeStruct((facets, SLOTS, channels, dec_rows, width), jnp.bfloat16),
+        functools.partial(gradient_kernel, second, paired),
+        out_shape=[out_shape] * (1 + paired),
         grid_spec=pltpu.PrefetchScalarGridSpec(
-            num_scalar_prefetch=2,
+            num_scalar_prefetch=len(scalars),
             grid=(channels,),
             in_specs=in_specs,
-            out_specs=pl.BlockSpec((facets, SLOTS, 1, dec_rows, width), lambda c, *_: (0, 0, c, 0, 0)),
+            out_specs=[pl.BlockSpec((kept, SLOTS, 1, dec_rows, width), lambda c, *_: (0, 0, c, 0, 0))] * (1 + paired),
             scratch_shapes=scratch,
         ),
         compiler_params=pltpu.CompilerParams(vmem_limit_bytes=48 << 20),
@@ -207,7 +220,7 @@
             flops=(4 if second else 2) * 256 * work, bytes_accessed=2 * work, transcendentals=0
         ),
         name="second_gradient" if second else "first_gradient",
-    )(patch_of, beam_of, *operands)
+    )(*scalars, *operands)
 
 
 def shrink(values, bound):
@@ -243,12 +256,10 @@
     return [combine(terms) for terms in gathered]
 
 
-def prox_kernel(second, recv_ref, thresholds_ref, step_ref, *refs):
-    if second:
-        first_ref, out_ref, summed, columns, natural = refs
-    else:
-        first_ref, out_ref, summed, columns, natural = refs
-    sources, rows = recv_ref.shape[0], recv_ref.shape[1]
+def prox_kernel(second, parts, *refs):
+    part_refs, (thresholds_ref, step_ref, *refs) = refs[:parts], refs[parts:]
+    first_ref, out_ref, summed, columns, natural = refs
+    rows = part_refs[0].shape[1]
     dec_rows = first_ref.shape[1]
     channels = step_ref.shape[0]
     half = 4
@@ -258,10 +269,11 @@
     lane = iota(shape, 1)
     block = lane // SPAN
 
-    def add_source(source, total):
-        return total + recv_ref[source].astype(jnp.float32)
-
-    total = lax.fori_loop(1, sources, add_source, recv_ref[0].astype(jnp.float32))
+    total = part_refs[0][0].astype(jnp.float32)
+    for part_ref in part_refs[1:]:
+        total = total + part_ref[0].astype(jnp.float32)
+    for index in range(1, part_refs[0].shape[0]):
+        total = total + part_refs[0][index].astype(jnp.float32)
     summed[:rows] = total
     summed[rows:] = total[rows - channels * dec_rows :]
 
@@ -392,9 +404,8 @@
 
 def prox_call(received, thresholds, step_size, dec_rows, first=None):
     second = first is not None
-    sources = received.shape[0]
     channels = step_size.shape[0]
-    received = received.reshape(sources, SLOTS * channels * dec_rows, LANES)
+    received = [part.reshape(-1, SLOTS * channels * dec_rows, LANES) for part in received]
     vmem = pl.BlockSpec(memory_space=pltpu.VMEM)
     smem = pl.BlockSpec(memory_space=pltpu.SMEM)
     held = jax.ShapeDtypeStruct((2, dec_rows, 8, LANES), jnp.float32)
@@ -405,9 +416,9 @@
         out_shape = (held, jax.ShapeDtypeStruct((2 * channels * dec_rows, LANES), jnp.bfloat16))
         out_specs = (vmem, vmem)
     return pl.pallas_call(
-        functools.partial(prox_kernel, second),
+        functools.partial(prox_kernel, second, len(received)),
         out_shape=out_shape,
-        in_specs=[vmem, smem, smem] + ([vmem] if second else []),
+        in_specs=[vmem] * len(received) + [smem, smem] + ([vmem] if second else []),
         out_specs=out_specs,
         scratch_shapes=[
             pltpu.VMEM((4 * channels * dec_rows, LANES), jnp.float32),
@@ -416,27 +427,87 @@
         ],
         compiler_params=pltpu.CompilerParams(vmem_limit_bytes=32 << 20),
         name="second_prox" if second else "first_prox",
-    )(received, thresholds, step_size, *([first] if second else []))
+    )(*received, thresholds, step_size, *([first] if second else []))
+
+
+def fold_kernel(keep_ref, got_ref, *outs):
+    for index, out_ref in enumerate(outs):
+        out_ref[0] = (keep_ref[index] + got_ref[index]).astype(out_ref.dtype)
+
+
+def join_kernel(*refs):
+    *parts, out_ref = refs
+    start = 0
+    for part_ref in parts:
+        out_ref[start : start + part_ref.shape[0]] = part_ref[...]
+        start += part_ref.shape[0]
+
+
+def small_call(kernel, name, out_shape, *operands):
+    vmem = pl.BlockSpec(memory_space=pltpu.VMEM)
+    return pl.pallas_call(
+        kernel,
+        out_shape=out_shape,
+        in_specs=[vmem] * len(operands),
+        out_specs=jax.tree.map(lambda _: vmem, out_shape),
+        compiler_params=pltpu.CompilerParams(vmem_limit_bytes=16 << 20),
+        name=name,
+    )(*operands)
+
+
+def join(*parts):
+    rows = sum(part.shape[0] for part in parts)
+    shape = jax.ShapeDtypeStruct((rows,) + parts[0].shape[1:], parts[0].dtype)
+    return small_call(join_kernel, "join", shape, *parts)
+
+
+def across(value, difference):
+    count = lax.axis_size("ra")
+    return lax.ppermute(value, "ra", [(source, source ^ difference) for source in range(count)])
+
+
+def pair_exchange(keep, send):
+    got = across(send, 1)
+    shape = (1,) + keep.shape[1:]
+    kinds = [jnp.float32] + [jnp.bfloat16] * (keep.shape[0] - 1)
+    parts = small_call(fold_kernel, "fold", [jax.ShapeDtypeStruct(shape, kind) for kind in kinds], keep, got)
+    far = [across(parts[index], 2 * index) for index in reversed(range(1, len(parts)))]
+    return [parts[0]] + far
+
+
+def pair_gather(tiles):
+    tiles = join(tiles, across(tiles, 2))
+    far = [across(tiles, difference) for difference in (12, 8, 4)]
+    tiles = join(tiles, *reversed(far))
+    return join(tiles, across(tiles, 1))
 
 
 def local(vis, beams, m_ra, m_dec, facet_of, tile_of, beam_of, step_size, thresholds):
     facets = lax.axis_size("ra")
     channels, dec_rows, owned, samples = vis.shape
     width = m_ra.shape[0]
+    per_facet = RA_DEV // width
     beams, m_ra, m_dec, beam_of = (
         pltpu.with_memory_space_constraint(x, pltpu.HBM) for x in (beams, m_ra, m_dec, beam_of)
     )
-    patch_of = facet_of[:, 0] * (RA_DEV // width) + tile_of
-
-    def exchange(sums):
-        return lax.all_to_all(sums, "ra", split_axis=0, concat_axis=0, tiled=True)
-
-    sums = gradient_call(patch_of, beam_of, vis, beams, m_ra, m_dec, facets)
-    first, tiles = prox_call(exchange(sums), thresholds, step_size, dec_rows)
-    tiles = lax.all_gather(tiles, "ra", axis=0, tiled=True)
-    tiles = tiles.reshape(facets * 2 * channels, dec_rows, width)
-    sums = gradient_call(patch_of, beam_of, vis, beams, m_ra, m_dec, facets, tiles)
-    return prox_call(exchange(sums), thresholds, step_size, dec_rows, first)
+    patch_of = facet_of[:, 0] * per_facet + tile_of
+    paired = facets == 16
+    if paired:
+        me = lax.axis_index("ra").astype(jnp.int32)
+        apart = facet_of[:, 0] ^ me
+        slot_of = ((apart & 1) * (facets // 2) + (apart >> 1)) * per_facet + tile_of
+        me = me.reshape(1)
+        exchange, gather = pair_exchange, pair_gather
+    else:
+        me, slot_of = None, patch_of
+        exchange = lambda sums: [lax.all_to_all(sums, "ra", split_axis=0, concat_axis=0, tiled=True)]
+        gather = lambda tiles: lax.all_gather(tiles, "ra", axis=0, tiled=True)
+
+    sums = gradient_call(patch_of, beam_of, vis, beams, m_ra, m_dec, facets, me)
+    first, tiles = prox_call(exchange(*sums), thresholds, step_size, dec_rows)
+    tiles = gather(tiles).reshape(facets * per_facet * channels, dec_rows, width)
+    sums = gradient_call(patch_of, beam_of, vis, beams, m_ra, m_dec, facets, me, slot_of, tiles)
+    return prox_call(exchange(*sums), thresholds, step_size, dec_rows, first)
 
 
 def solution(mesh):

time: 111 us -> 88.9 us (0.80)
  blocking collectives: 71.4 us -> 0 us
  starting transfers between devices: 0 us -> 29.7 us
  waiting for transfers between devices: 0 us -> 19.6 us
    all_to_all x2 -> x0, blocking collectives: 50.3 us -> none  [exchange(): return lax.all_to_all(sums, 'ra', split_axis=0, concat_axis=0, tiled=True)]
    ppermute x0 -> x21, starting transfers between devices: none -> 29.7 us  [across(): lax.ppermute(value, 'ra', [(source, source ^ difference) for source in ra...]
    all_gather x1 -> x0, blocking collectives: 21.1 us -> none  [local(): tiles = lax.all_gather(tiles, 'ra', axis=0, tiled=True)]
    ppermute x0 -> x21, waiting for transfers between devices: none -> 19.6 us  [across(): lax.ppermute(value, 'ra', [(source, source ^ difference) for source in ra...]
    pallas_call x4 -> x9, Pallas kernels: 38.4 us -> 38.6 us  [the longest x2 28.5 us: gradient_call(): pl.pallas_call(functools.partial(gradient_kernel, second, paired), out_sh...]
  transfers between devices with their start and end apart: 0 -> 21, of which waited for: 0 -> 14; matrix products, arithmetic and copies ran while one was open for 0% -> 0% of each run, Pallas kernels for 0% -> 0%
where the time goes in v3:
time: 88.9 us; the launch traced here: 88.7 us
  Pallas kernels  38.6 us (43%)
  starting transfers between devices  29.7 us (33%)
  waiting for transfers between devices  19.6 us (22%)
    ppermute x21, starting transfers between devices, across(): lax.ppermute(value, 'ra', [(source, source ^ difference) for source in ra...  29.7 us
    pallas_call x2, Pallas kernels, gradient_call(): pl.pallas_call(functools.partial(gradient_kernel, second, paired), out_sh...  28.5 us
    ppermute x21, waiting for transfers between devices, across(): lax.ppermute(value, 'ra', [(source, source ^ difference) for source in ra...  19.6 us
    pallas_call x2, Pallas kernels, prox_call(): pl.pallas_call(functools.partial(prox_kernel, second, len(received)), out...  9.78 us
  transfers between devices with their start and end apart: 21, of which 14 were waited for; matrix products, arithmetic and copies ran while one was open for 0% of the time, Pallas kernels for 0%

profile of v3, /device:TPU:0, one launch (start us, length us, event | category | flops | bytes accessed | tf_op | source)
XLA Modules:
  0.0 88.7 jit_solution(5486448142316313634)
XLA Ops:
  0.0 0.7 bitcast_add_fusion
  0.7 9.5 %first_gradient.1 = (f32[8,3,4,16,128]{4,3,2,1,0:T(8,128)S(1)}, f32[8,3,4,16,128]{4,3,2,1,0:T(8,128)S(1)}) custom-call(s32[128]{0:T(128)S(1)} %get-tuple-element.50.patch_ref, s32[128]{0:T(128)} %beam_ref.3, s32[1]{0:T(128)} %bitcast.1.refs_0_, bf16[4,16,128,512]{3,2,1,0:T(8,128)(2,1)} %refs_2_.3, bf16[4,16,16,128]{3,2,1,0:T(8,128)(2,1)} %refs_3_.3, ...), custom_call_target="tpu_custom_call" | custom-call | flops 2147483648 | bytes 8388608 | tf_op jit(solution)/shard_map/first_gradient/pallas_call | solution.py:208
  10.2 0.5 collective-permute-start
  10.7 1.9 %collective-permute-done.got_ref = f32[8,3,4,16,128]{4,3,2,1,0:T(8,128)S(1)} collective-permute-done((f32[8,3,4,16,128]{4,3,2,1,0:T(8,128)S(1)}, f32[8,3,4,16,128]{4,3,2,1,0:T(8,128)S(1)}, u32[]{:S(2)}, u32[]{:S(2)}) %collective-permute-start) | collective-permute-done | bytes 786464 | tf_op jit(solution)/shard_map/ppermute | solution.py:466
  12.8 6.0 %collective-permute-start.1 = (bf16[1,3,4,16,128]{4,3,2,1,0:T(8,128)(2,1)S(1)}, bf16[1,3,4,16,128]{4,3,2,1,0:T(8,128)(2,1)S(1)}, u32[]{:S(2)}, u32[]{:S(2)}) collective-permute-start(bf16[1,3,4,16,128]{4,3,2,1,0:T(8,128)(2,1)S(1)} %get-tuple-element.30), channel_id=1, source_target_pairs={{0,14},{1,15},{2,12},{3,13},{4,10},{5,11},{6,8},{7,9},{8,6},{9,7},... | collective-permute-start | bytes 147464 | tf_op jit(solution)/shard_map/ppermute | solution.py:466
  19.0 0.7 collective-permute-start.3
  19.7 2.0 %collective-permute-start.4 = (bf16[1,3,4,16,128]{4,3,2,1,0:T(8,128)(2,1)S(1)}, bf16[1,3,4,16,128]{4,3,2,1,0:T(8,128)(2,1)S(1)}, u32[]{:S(2)}, u32[]{:S(2)}) collective-permute-start(bf16[1,3,4,16,128]{4,3,2,1,0:T(8,128)(2,1)S(1)} %get-tuple-element.33), channel_id=1, source_target_pairs={{0,8},{1,9},{2,10},{3,11},{4,12},{5,13},{6,14},{7,15},{8,0},{9,1},... | collective-permute-start | bytes 147464 | tf_op jit(solution)/shard_map/ppermute | solution.py:466
  21.8 2.3 %collective-permute-start.5 = (bf16[1,3,4,16,128]{4,3,2,1,0:T(8,128)(2,1)S(1)}, bf16[1,3,4,16,128]{4,3,2,1,0:T(8,128)(2,1)S(1)}, u32[]{:S(2)}, u32[]{:S(2)}) collective-permute-start(bf16[1,3,4,16,128]{4,3,2,1,0:T(8,128)(2,1)S(1)} %get-tuple-element.34), channel_id=1, source_target_pairs={{0,6},{1,7},{2,4},{3,5},{4,2},{5,3},{6,0},{7,1},{8,14},{9,15},{10,... | collective-permute-start | bytes 147464 | tf_op jit(solution)/shard_map/ppermute | solution.py:466
  24.0 0.8 collective-permute-start.6
  25.2 1.0 %collective-permute-done.3 = bf16[1,3,4,16,128]{4,3,2,1,0:T(8,128)(2,1)S(1)} collective-permute-done((bf16[1,3,4,16,128]{4,3,2,1,0:T(8,128)(2,1)S(1)}, bf16[1,3,4,16,128]{4,3,2,1,0:T(8,128)(2,1)S(1)}, u32[]{:S(2)}, u32[]{:S(2)}) %collective-permute-start.3) | collective-permute-done | bytes 49184 | tf_op jit(solution)/shard_map/ppermute | solution.py:466
  26.2 1.5 %collective-permute-done.4 = bf16[1,3,4,16,128]{4,3,2,1,0:T(8,128)(2,1)S(1)} collective-permute-done((bf16[1,3,4,16,128]{4,3,2,1,0:T(8,128)(2,1)S(1)}, bf16[1,3,4,16,128]{4,3,2,1,0:T(8,128)(2,1)S(1)}, u32[]{:S(2)}, u32[]{:S(2)}) %collective-permute-start.4) | collective-permute-done | bytes 49184 | tf_op jit(solution)/shard_map/ppermute | solution.py:466
  27.7 0.5 collective-permute-done.5
  28.5 0.5 collective-permute-done.7
  28.9 5.2 %first_prox.1 = (f32[2,16,8,128]{3,2,1,0:T(8,128)S(1)}, bf16[128,128]{1,0:T(8,128)(2,1)S(1)}) custom-call(f32[1,192,128]{2,1,0:T(8,128)S(1)} %bitcast.23, bf16[1,192,128]{2,1,0:T(8,128)(2,1)S(1)} %bitcast.32, bf16[1,192,128]{2,1,0:T(8,128)(2,1)S(1)} %bitcast.33, bf16[1,192,128]{2,1,0:T(8,128)(2,1)S(1)} %bitcast.34, bf16[1,192,128]{2,1,0:T(8,128)(2,1)S(1)} %bitcast.35, ...), custom_call_target="tpu_custom_call" | custom-call | tf_op jit(solution)/shard_map/first_prox/pallas_call | solution.py:418
  34.2 0.9 collective-permute-start.8
  35.1 3.1 %collective-permute-done.8.refs_1_ = bf16[128,128]{1,0:T(8,128)(2,1)S(1)} collective-permute-done((bf16[128,128]{1,0:T(8,128)(2,1)S(1)}, bf16[128,128]{1,0:T(8,128)(2,1)S(1)}, u32[]{:S(2)}, u32[]{:S(2)}) %collective-permute-start.8) | collective-permute-done | bytes 32800 | tf_op jit(solution)/shard_map/ppermute | solution.py:466
  38.2 3.6 %collective-permute-start.11 = (bf16[256,128]{1,0:T(8,128)(2,1)S(1)}, bf16[256,128]{1,0:T(8,128)(2,1)S(1)}, u32[]{:S(2)}, u32[]{:S(2)}) collective-permute-start(bf16[256,128]{1,0:T(8,128)(2,1)S(1)} %join.3.refs_0_), channel_id=1, source_target_pairs={{0,12},{1,13},{2,14},{3,15},{4,8},{5,9},{6,10},{7,11},{8,4},{9,5},... | collective-permute-start | bytes 196616 | tf_op jit(solution)/shard_map/ppermute | solution.py:466
  41.8 0.8 collective-permute-start.9
  42.6 1.8 %collective-permute-done.11.refs_3_ = bf16[256,128]{1,0:T(8,128)(2,1)S(1)} collective-permute-done((bf16[256,128]{1,0:T(8,128)(2,1)S(1)}, bf16[256,128]{1,0:T(8,128)(2,1)S(1)}, u32[]{:S(2)}, u32[]{:S(2)}) %collective-permute-start.11) | collective-permute-done | bytes 65568 | tf_op jit(solution)/shard_map/ppermute | solution.py:466
  44.3 2.6 %collective-permute-done.10.refs_2_ = bf16[256,128]{1,0:T(8,128)(2,1)S(1)} collective-permute-done((bf16[256,128]{1,0:T(8,128)(2,1)S(1)}, bf16[256,128]{1,0:T(8,128)(2,1)S(1)}, u32[]{:S(2)}, u32[]{:S(2)}) %collective-permute-start.10) | collective-permute-done | bytes 65568 | tf_op jit(solution)/shard_map/ppermute | solution.py:466
  47.0 1.5 %collective-permute-done.12.refs_1_ = bf16[1024,128]{1,0:T(8,128)(2,1)S(1)} collective-permute-done((bf16[1024,128]{1,0:T(8,128)(2,1)S(1)}, bf16[1024,128]{1,0:T(8,128)(2,1)S(1)}, u32[]{:S(2)}, u32[]{:S(2)}) %collective-permute-start.12) | collective-permute-done | bytes 262176 | tf_op jit(solution)/shard_map/ppermute | solution.py:466
  48.6 19.0 %second_gradient.1 = (f32[8,3,4,16,128]{4,3,2,1,0:T(8,128)S(1)}, f32[8,3,4,16,128]{4,3,2,1,0:T(8,128)S(1)}) custom-call(s32[128]{0:T(128)S(1)} %get-tuple-element.50.patch_ref, s32[128]{0:T(128)} %beam_ref.3, s32[1]{0:T(128)} %bitcast.1.refs_0_, s32[128]{0:T(128)S(1)} %get-tuple-element.49.refs_1_, bf16[4,16,128,512]{3,2,1,0:T(8,128)(2,1)} %refs_2_.3, ...), custom_call_target="tpu_custom_call" | custom-call | flops 4294967296 | bytes 8388608 | tf_op jit(solution)/shard_map/second_gradient/pallas_call | solution.py:208
  67.8 2.2 %collective-permute-done.13.got_ref = f32[8,3,4,16,128]{4,3,2,1,0:T(8,128)S(1)} collective-permute-done((f32[8,3,4,16,128]{4,3,2,1,0:T(8,128)S(1)}, f32[8,3,4,16,128]{4,3,2,1,0:T(8,128)S(1)}, u32[]{:S(2)}, u32[]{:S(2)}) %collective-permute-start.13) | collective-permute-done | bytes 786464 | tf_op jit(solution)/shard_map/ppermute | solution.py:466
  70.1 1.9 %collective-permute-start.14 = (bf16[1,3,4,16,128]{4,3,2,1,0:T(8,128)(2,1)S(1)}, bf16[1,3,4,16,128]{4,3,2,1,0:T(8,128)(2,1)S(1)}, u32[]{:S(2)}, u32[]{:S(2)}) collective-permute-start(bf16[1,3,4,16,128]{4,3,2,1,0:T(8,128)(2,1)S(1)} %get-tuple-element.41), channel_id=1, source_target_pairs={{0,14},{1,15},{2,12},{3,13},{4,10},{5,11},{6,8},{7,9},{8,6},{9,7},... | collective-permute-start | bytes 147464 | tf_op jit(solution)/shard_map/ppermute | solution.py:466
  72.0 1.8 %collective-permute-start.15 = (bf16[1,3,4,16,128]{4,3,2,1,0:T(8,128)(2,1)S(1)}, bf16[1,3,4,16,128]{4,3,2,1,0:T(8,128)(2,1)S(1)}, u32[]{:S(2)}, u32[]{:S(2)}) collective-permute-start(bf16[1,3,4,16,128]{4,3,2,1,0:T(8,128)(2,1)S(1)} %get-tuple-element.42), channel_id=1, source_target_pairs={{0,12},{1,13},{2,14},{3,15},{4,8},{5,9},{6,10},{7,11},{8,4},{9,5},... | collective-permute-start | bytes 147464 | tf_op jit(solution)/shard_map/ppermute | solution.py:466
  73.8 1.2 %collective-permute-start.16 = (bf16[1,3,4,16,128]{4,3,2,1,0:T(8,128)(2,1)S(1)}, bf16[1,3,4,16,128]{4,3,2,1,0:T(8,128)(2,1)S(1)}, u32[]{:S(2)}, u32[]{:S(2)}) collective-permute-start(bf16[1,3,4,16,128]{4,3,2,1,0:T(8,128)(2,1)S(1)} %get-tuple-element.43), channel_id=1, source_target_pairs={{0,10},{1,11},{2,8},{3,9},{4,14},{5,15},{6,12},{7,13},{8,2},{9,3},... | collective-permute-start | bytes 147464 | tf_op jit(solution)/shard_map/ppermute | solution.py:466
  75.0 2.7 %collective-permute-start.17 = (bf16[1,3,4,16,128]{4,3,2,1,0:T(8,128)(2,1)S(1)}, bf16[1,3,4,16,128]{4,3,2,1,0:T(8,128)(2,1)S(1)}, u32[]{:S(2)}, u32[]{:S(2)}) collective-permute-start(bf16[1,3,4,16,128]{4,3,2,1,0:T(8,128)(2,1)S(1)} %get-tuple-element.44), channel_id=1, source_target_pairs={{0,8},{1,9},{2,10},{3,11},{4,12},{5,13},{6,14},{7,15},{8,0},{9,1},... | collective-permute-start | bytes 147464 | tf_op jit(solution)/shard_map/ppermute | solution.py:466
  77.8 1.9 %collective-permute-start.19 = (bf16[1,3,4,16,128]{4,3,2,1,0:T(8,128)(2,1)S(1)}, bf16[1,3,4,16,128]{4,3,2,1,0:T(8,128)(2,1)S(1)}, u32[]{:S(2)}, u32[]{:S(2)}) collective-permute-start(bf16[1,3,4,16,128]{4,3,2,1,0:T(8,128)(2,1)S(1)} %get-tuple-element.46), channel_id=1, source_target_pairs={{0,4},{1,5},{2,6},{3,7},{4,0},{5,1},{6,2},{7,3},{8,12},{9,13},{10,... | collective-permute-start | bytes 147464 | tf_op jit(solution)/shard_map/ppermute | solution.py:466
  79.7 1.6 %collective-permute-start.20 = (bf16[1,3,4,16,128]{4,3,2,1,0:T(8,128)(2,1)S(1)}, bf16[1,3,4,16,128]{4,3,2,1,0:T(8,128)(2,1)S(1)}, u32[]{:S(2)}, u32[]{:S(2)}) collective-permute-start(bf16[1,3,4,16,128]{4,3,2,1,0:T(8,128)(2,1)S(1)} %get-tuple-element.47), channel_id=1, source_target_pairs={{0,2},{1,3},{2,0},{3,1},{4,6},{5,7},{6,4},{7,5},{8,10},{9,11},{10,... | collective-permute-start | bytes 147464 | tf_op jit(solution)/shard_map/ppermute | solution.py:466
  81.3 1.0 %collective-permute-done.16 = bf16[1,3,4,16,128]{4,3,2,1,0:T(8,128)(2,1)S(1)} collective-permute-done((bf16[1,3,4,16,128]{4,3,2,1,0:T(8,128)(2,1)S(1)}, bf16[1,3,4,16,128]{4,3,2,1,0:T(8,128)(2,1)S(1)}, u32[]{:S(2)}, u32[]{:S(2)}) %collective-permute-start.16) | collective-permute-done | bytes 49184 | tf_op jit(solution)/shard_map/ppermute | solution.py:466
  82.2 1.6 %collective-permute-done.18 = bf16[1,3,4,16,128]{4,3,2,1,0:T(8,128)(2,1)S(1)} collective-permute-done((bf16[1,3,4,16,128]{4,3,2,1,0:T(8,128)(2,1)S(1)}, bf16[1,3,4,16,128]{4,3,2,1,0:T(8,128)(2,1)S(1)}, u32[]{:S(2)}, u32[]{:S(2)}) %collective-permute-start.18) | collective-permute-done | bytes 49184 | tf_op jit(solution)/shard_map/ppermute | solution.py:466
  84.1 4.5 %second_prox.1 = f32[4,16,256]{2,1,0:T(8,128)} custom-call(f32[1,192,128]{2,1,0:T(8,128)S(1)} %bitcast.24, bf16[1,192,128]{2,1,0:T(8,128)(2,1)S(1)} %bitcast.25, bf16[1,192,128]{2,1,0:T(8,128)(2,1)S(1)} %bitcast.26, bf16[1,192,128]{2,1,0:T(8,128)(2,1)S(1)} %bitcast.27, bf16[1,192,128]{2,1,0:T(8,128)(2,1)S(1)} %bitcast.28, bf16[1,192,128]{2,1,0:T(8,128)(2,1)S(1)} %bitcast.29, ...), custom_call_target="tpu_custom_call" | custom-call | tf_op jit(solution)/shard_map/second_prox/pallas_call | solution.py:418
  (24 shorter events, 1.8 us)
Async XLA Ops:
  0.0 28.9 %copy-start = (f32[4,4]{1,0:T(4,128)S(1)}, f32[4,4]{1,0:T(4,128)}, u32[]{:S(2)}) copy-start(f32[4,4]{1,0:T(4,128)} %refs_8_.3) | copy-start | bytes 196
  0.0 28.9 %copy-start.1 = (f32[4]{0:T(128)S(1)}, f32[4]{0:T(128)}, u32[]{:S(2)}) copy-start(f32[4]{0:T(128)} %refs_9_.3) | copy-start | bytes 52
  10.2 2.4 %collective-permute-start = (f32[8,3,4,16,128]{4,3,2,1,0:T(8,128)S(1)}, f32[8,3,4,16,128]{4,3,2,1,0:T(8,128)S(1)}, u32[]{:S(2)}, u32[]{:S(2)}) collective-permute-start(f32[8,3,4,16,128]{4,3,2,1,0:T(8,128)S(1)} %get-tuple-element.28), channel_id=1, source_target_pairs={{0,1},{1,0},{2,3},{3,2},{4,5},{5,4},{6,7},{7,6},{8,9},{9,8},{10,11... | collective-permute-start | bytes 2359304 | tf_op jit(solution)/shard_map/ppermute | solution.py:466
  12.8 11.3 %collective-permute-start.1 = (bf16[1,3,4,16,128]{4,3,2,1,0:T(8,128)(2,1)S(1)}, bf16[1,3,4,16,128]{4,3,2,1,0:T(8,128)(2,1)S(1)}, u32[]{:S(2)}, u32[]{:S(2)}) collective-permute-start(bf16[1,3,4,16,128]{4,3,2,1,0:T(8,128)(2,1)S(1)} %get-tuple-element.30), channel_id=1, source_target_pairs={{0,14},{1,15},{2,12},{3,13},{4,10},{5,11},{6,8},{7,9},{8,6},{9,7},... | collective-permute-start | bytes 147464 | tf_op jit(solution)/shard_map/ppermute | solution.py:466
  18.7 6.1 %collective-permute-start.2 = (bf16[1,3,4,16,128]{4,3,2,1,0:T(8,128)(2,1)S(1)}, bf16[1,3,4,16,128]{4,3,2,1,0:T(8,128)(2,1)S(1)}, u32[]{:S(2)}, u32[]{:S(2)}) collective-permute-start(bf16[1,3,4,16,128]{4,3,2,1,0:T(8,128)(2,1)S(1)} %get-tuple-element.31), channel_id=1, source_target_pairs={{0,12},{1,13},{2,14},{3,15},{4,8},{5,9},{6,10},{7,11},{8,4},{9,5},... | collective-permute-start | bytes 147464 | tf_op jit(solution)/shard_map/ppermute | solution.py:466
  19.0 7.3 %collective-permute-start.3 = (bf16[1,3,4,16,128]{4,3,2,1,0:T(8,128)(2,1)S(1)}, bf16[1,3,4,16,128]{4,3,2,1,0:T(8,128)(2,1)S(1)}, u32[]{:S(2)}, u32[]{:S(2)}) collective-permute-start(bf16[1,3,4,16,128]{4,3,2,1,0:T(8,128)(2,1)S(1)} %get-tuple-element.32), channel_id=1, source_target_pairs={{0,10},{1,11},{2,8},{3,9},{4,14},{5,15},{6,12},{7,13},{8,2},{9,3},... | collective-permute-start | bytes 147464 | tf_op jit(solution)/shard_map/ppermute | solution.py:466
  19.7 8.0 %collective-permute-start.4 = (bf16[1,3,4,16,128]{4,3,2,1,0:T(8,128)(2,1)S(1)}, bf16[1,3,4,16,128]{4,3,2,1,0:T(8,128)(2,1)S(1)}, u32[]{:S(2)}, u32[]{:S(2)}) collective-permute-start(bf16[1,3,4,16,128]{4,3,2,1,0:T(8,128)(2,1)S(1)} %get-tuple-element.33), channel_id=1, source_target_pairs={{0,8},{1,9},{2,10},{3,11},{4,12},{5,13},{6,14},{7,15},{8,0},{9,1},... | collective-permute-start | bytes 147464 | tf_op jit(solution)/shard_map/ppermute | solution.py:466
  21.8 6.5 %collective-permute-start.5 = (bf16[1,3,4,16,128]{4,3,2,1,0:T(8,128)(2,1)S(1)}, bf16[1,3,4,16,128]{4,3,2,1,0:T(8,128)(2,1)S(1)}, u32[]{:S(2)}, u32[]{:S(2)}) collective-permute-start(bf16[1,3,4,16,128]{4,3,2,1,0:T(8,128)(2,1)S(1)} %get-tuple-element.34), channel_id=1, source_target_pairs={{0,6},{1,7},{2,4},{3,5},{4,2},{5,3},{6,0},{7,1},{8,14},{9,15},{10,... | collective-permute-start | bytes 147464 | tf_op jit(solution)/shard_map/ppermute | solution.py:466
  24.0 4.4 %collective-permute-start.6 = (bf16[1,3,4,16,128]{4,3,2,1,0:T(8,128)(2,1)S(1)}, bf16[1,3,4,16,128]{4,3,2,1,0:T(8,128)(2,1)S(1)}, u32[]{:S(2)}, u32[]{:S(2)}) collective-permute-start(bf16[1,3,4,16,128]{4,3,2,1,0:T(8,128)(2,1)S(1)} %get-tuple-element.35), channel_id=1, source_target_pairs={{0,4},{1,5},{2,6},{3,7},{4,0},{5,1},{6,2},{7,3},{8,12},{9,13},{10,... | collective-permute-start | bytes 147464 | tf_op jit(solution)/shard_map/ppermute | solution.py:466
  24.8 4.1 %collective-permute-start.7 = (bf16[1,3,4,16,128]{4,3,2,1,0:T(8,128)(2,1)S(1)}, bf16[1,3,4,16,128]{4,3,2,1,0:T(8,128)(2,1)S(1)}, u32[]{:S(2)}, u32[]{:S(2)}) collective-permute-start(bf16[1,3,4,16,128]{4,3,2,1,0:T(8,128)(2,1)S(1)} %get-tuple-element.36), channel_id=1, source_target_pairs={{0,2},{1,3},{2,0},{3,1},{4,6},{5,7},{6,4},{7,5},{8,10},{9,11},{10,... | collective-permute-start | bytes 147464 | tf_op jit(solution)/shard_map/ppermute | solution.py:466
  34.2 4.0 %collective-permute-start.8 = (bf16[128,128]{1,0:T(8,128)(2,1)S(1)}, bf16[128,128]{1,0:T(8,128)(2,1)S(1)}, u32[]{:S(2)}, u32[]{:S(2)}) collective-permute-start(bf16[128,128]{1,0:T(8,128)(2,1)S(1)} %get-tuple-element.37.refs_0_), channel_id=1, source_target_pairs={{0,2},{1,3},{2,0},{3,1},{4,6},{5,7},{6,4},{7,5},{8,10},{9,11},{10,... | collective-permute-start | bytes 98312 | tf_op jit(solution)/shard_map/ppermute | solution.py:466
  38.2 6.2 %collective-permute-start.11 = (bf16[256,128]{1,0:T(8,128)(2,1)S(1)}, bf16[256,128]{1,0:T(8,128)(2,1)S(1)}, u32[]{:S(2)}, u32[]{:S(2)}) collective-permute-start(bf16[256,128]{1,0:T(8,128)(2,1)S(1)} %join.3.refs_0_), channel_id=1, source_target_pairs={{0,12},{1,13},{2,14},{3,15},{4,8},{5,9},{6,10},{7,11},{8,4},{9,5},... | collective-permute-start | bytes 196616 | tf_op jit(solution)/shard_map/ppermute | solution.py:466
  41.8 5.2 %collective-permute-start.10 = (bf16[256,128]{1,0:T(8,128)(2,1)S(1)}, bf16[256,128]{1,0:T(8,128)(2,1)S(1)}, u32[]{:S(2)}, u32[]{:S(2)}) collective-permute-start(bf16[256,128]{1,0:T(8,128)(2,1)S(1)} %join.3.refs_0_), channel_id=1, source_target_pairs={{0,8},{1,9},{2,10},{3,11},{4,12},{5,13},{6,14},{7,15},{8,0},{9,1},... | collective-permute-start | bytes 196616 | tf_op jit(solution)/shard_map/ppermute | solution.py:466
  41.8 5.2 %collective-permute-start.9 = (bf16[256,128]{1,0:T(8,128)(2,1)S(1)}, bf16[256,128]{1,0:T(8,128)(2,1)S(1)}, u32[]{:S(2)}, u32[]{:S(2)}) collective-permute-start(bf16[256,128]{1,0:T(8,128)(2,1)S(1)} %join.3.refs_0_), channel_id=1, source_target_pairs={{0,4},{1,5},{2,6},{3,7},{4,0},{5,1},{6,2},{7,3},{8,12},{9,13},{10,... | collective-permute-start | bytes 196616 | tf_op jit(solution)/shard_map/ppermute | solution.py:466
  46.9 1.6 %collective-permute-start.12 = (bf16[1024,128]{1,0:T(8,128)(2,1)S(1)}, bf16[1024,128]{1,0:T(8,128)(2,1)S(1)}, u32[]{:S(2)}, u32[]{:S(2)}) collective-permute-start(bf16[1024,128]{1,0:T(8,128)(2,1)S(1)} %join.4.refs_0_), channel_id=1, source_target_pairs={{0,1},{1,0},{2,3},{3,2},{4,5},{5,4},{6,7},{7,6},{8,9},{9,8},{10,11... | collective-permute-start | bytes 786440 | tf_op jit(solution)/shard_map/ppermute | solution.py:466
  67.6 2.4 %collective-permute-start.13 = (f32[8,3,4,16,128]{4,3,2,1,0:T(8,128)S(1)}, f32[8,3,4,16,128]{4,3,2,1,0:T(8,128)S(1)}, u32[]{:S(2)}, u32[]{:S(2)}) collective-permute-start(f32[8,3,4,16,128]{4,3,2,1,0:T(8,128)S(1)} %get-tuple-element.39), channel_id=1, source_target_pairs={{0,1},{1,0},{2,3},{3,2},{4,5},{5,4},{6,7},{7,6},{8,9},{9,8},{10,11... | collective-permute-start | bytes 2359304 | tf_op jit(solution)/shard_map/ppermute | solution.py:466
  70.1 7.7 %collective-permute-start.14 = (bf16[1,3,4,16,128]{4,3,2,1,0:T(8,128)(2,1)S(1)}, bf16[1,3,4,16,128]{4,3,2,1,0:T(8,128)(2,1)S(1)}, u32[]{:S(2)}, u32[]{:S(2)}) collective-permute-start(bf16[1,3,4,16,128]{4,3,2,1,0:T(8,128)(2,1)S(1)} %get-tuple-element.41), channel_id=1, source_target_pairs={{0,14},{1,15},{2,12},{3,13},{4,10},{5,11},{6,8},{7,9},{8,6},{9,7},... | collective-permute-start | bytes 147464 | tf_op jit(solution)/shard_map/ppermute | solution.py:466
  72.0 7.7 %collective-permute-start.15 = (bf16[1,3,4,16,128]{4,3,2,1,0:T(8,128)(2,1)S(1)}, bf16[1,3,4,16,128]{4,3,2,1,0:T(8,128)(2,1)S(1)}, u32[]{:S(2)}, u32[]{:S(2)}) collective-permute-start(bf16[1,3,4,16,128]{4,3,2,1,0:T(8,128)(2,1)S(1)} %get-tuple-element.42), channel_id=1, source_target_pairs={{0,12},{1,13},{2,14},{3,15},{4,8},{5,9},{6,10},{7,11},{8,4},{9,5},... | collective-permute-start | bytes 147464 | tf_op jit(solution)/shard_map/ppermute | solution.py:466
  73.8 8.4 %collective-permute-start.16 = (bf16[1,3,4,16,128]{4,3,2,1,0:T(8,128)(2,1)S(1)}, bf16[1,3,4,16,128]{4,3,2,1,0:T(8,128)(2,1)S(1)}, u32[]{:S(2)}, u32[]{:S(2)}) collective-permute-start(bf16[1,3,4,16,128]{4,3,2,1,0:T(8,128)(2,1)S(1)} %get-tuple-element.43), channel_id=1, source_target_pairs={{0,10},{1,11},{2,8},{3,9},{4,14},{5,15},{6,12},{7,13},{8,2},{9,3},... | collective-permute-start | bytes 147464 | tf_op jit(solution)/shard_map/ppermute | solution.py:466
  75.0 7.2 %collective-permute-start.17 = (bf16[1,3,4,16,128]{4,3,2,1,0:T(8,128)(2,1)S(1)}, bf16[1,3,4,16,128]{4,3,2,1,0:T(8,128)(2,1)S(1)}, u32[]{:S(2)}, u32[]{:S(2)}) collective-permute-start(bf16[1,3,4,16,128]{4,3,2,1,0:T(8,128)(2,1)S(1)} %get-tuple-element.44), channel_id=1, source_target_pairs={{0,8},{1,9},{2,10},{3,11},{4,12},{5,13},{6,14},{7,15},{8,0},{9,1},... | collective-permute-start | bytes 147464 | tf_op jit(solution)/shard_map/ppermute | solution.py:466
  77.8 6.1 %collective-permute-start.18 = (bf16[1,3,4,16,128]{4,3,2,1,0:T(8,128)(2,1)S(1)}, bf16[1,3,4,16,128]{4,3,2,1,0:T(8,128)(2,1)S(1)}, u32[]{:S(2)}, u32[]{:S(2)}) collective-permute-start(bf16[1,3,4,16,128]{4,3,2,1,0:T(8,128)(2,1)S(1)} %get-tuple-element.45), channel_id=1, source_target_pairs={{0,6},{1,7},{2,4},{3,5},{4,2},{5,3},{6,0},{7,1},{8,14},{9,15},{10,... | collective-permute-start | bytes 147464 | tf_op jit(solution)/shard_map/ppermute | solution.py:466
  77.8 6.0 %collective-permute-start.19 = (bf16[1,3,4,16,128]{4,3,2,1,0:T(8,128)(2,1)S(1)}, bf16[1,3,4,16,128]{4,3,2,1,0:T(8,128)(2,1)S(1)}, u32[]{:S(2)}, u32[]{:S(2)}) collective-permute-start(bf16[1,3,4,16,128]{4,3,2,1,0:T(8,128)(2,1)S(1)} %get-tuple-element.46), channel_id=1, source_target_pairs={{0,4},{1,5},{2,6},{3,7},{4,0},{5,1},{6,2},{7,3},{8,12},{9,13},{10,... | collective-permute-start | bytes 147464 | tf_op jit(solution)/shard_map/ppermute | solution.py:466
  79.7 4.5 %collective-permute-start.20 = (bf16[1,3,4,16,128]{4,3,2,1,0:T(8,128)(2,1)S(1)}, bf16[1,3,4,16,128]{4,3,2,1,0:T(8,128)(2,1)S(1)}, u32[]{:S(2)}, u32[]{:S(2)}) collective-permute-start(bf16[1,3,4,16,128]{4,3,2,1,0:T(8,128)(2,1)S(1)} %get-tuple-element.47), channel_id=1, source_target_pairs={{0,2},{1,3},{2,0},{3,1},{4,6},{5,7},{6,4},{7,5},{8,10},{9,11},{10,... | collective-permute-start | bytes 147464 | tf_op jit(solution)/shard_map/ppermute | solution.py:466

commit v4 on v3

--- a/solution.py
+++ b/solution.py
@@ -16,6 +16,7 @@
 SPAN = LANES // PHASES
 SLOTS = 3
 CHUNK = 256
+COLUMNS = 256
 
 daub_coeffs = (
     (0.7071067811865476, 0.7071067811865476),
@@ -92,72 +93,21 @@
     return where_equal((row % size_a) * size_b + row // size_a, column).astype(jnp.bfloat16)
 
 
-def gradient_kernel(second, paired, patch_ref, beam_ref, *refs):
-    if paired:
-        me_ref, *refs = refs
-    if second:
-        slot_ref, *refs = refs
-    vis_ref, beams_ref, m_ra_ref, m_dec_ref, *refs = refs
-    if second:
-        tiles_ref, *refs = refs
-    outs, refs = refs[: 1 + paired], refs[1 + paired :]
-    if second:
-        back, forward, ra_out, ra_in, table, total, along, weighted = refs
-    else:
-        back, ra_out, table, total, along, weighted = refs
-    channel = pl.program_id(0)
-    channels = pl.num_programs(0)
-    dec_rows, owned = vis_ref.shape[1], vis_ref.shape[2]
-    width = m_ra_ref.shape[0]
-    beam_count = beams_ref.shape[2]
-    facets = outs[0].shape[0]
-
-    @pl.when(channel == 0)
-    def _():
-        back[...] = back_matrix(m_dec_ref[...])
-        order = phase_rows(width)
-        ra_out[...] = dot(m_ra_ref[...], order, ((0,), (1,))).astype(jnp.bfloat16)
-        if second:
-            forward[...] = forward_matrix(m_dec_ref[...])
-            ra_in[...] = dot(order, m_ra_ref[...]).astype(jnp.bfloat16)
-
-    rows = beams_ref[0].reshape(dec_rows * beam_count, width)
-    swapped = dot(swap_rows(dec_rows, beam_count), rows).astype(jnp.bfloat16)
-    table[...] = (
-        dot(swapped, phase_rows(width), ((1,), (1,)))
-        .astype(jnp.bfloat16)
-        .reshape(beam_count, dec_rows, width)
-    )
-    total[...] = jnp.zeros_like(total)
-
-    samples = vis_ref.shape[3]
-    size = GROUP * dec_rows
-    groups = owned // GROUP
-
-    if second:
-        for p in range(owned):
-            weighted[p * dec_rows : (p + 1) * dec_rows] = (
-                table[beam_ref[p]].astype(jnp.float32)
-                * tiles_ref[slot_ref[p] * channels + channel].astype(jnp.float32)
-            ).astype(jnp.bfloat16)
-        for m in range(0, owned * dec_rows, CHUNK):
-            along[m : m + CHUNK] = dot(weighted[m : m + CHUNK], ra_in[...]).astype(jnp.bfloat16)
-    for group in range(groups):
-        rows = slice(group * size, (group + 1) * size)
-        data = vis_ref[0, :, group * GROUP : (group + 1) * GROUP, :].reshape(size, samples)
-        if second:
-            predicted = dot(forward[...], along[rows])
-            data = (predicted - data.astype(jnp.float32)).astype(jnp.bfloat16)
-        along[rows] = dot(back[...], data).astype(jnp.bfloat16)
-    for m in range(0, owned * dec_rows, CHUNK):
-        patches = dot(along[m : m + CHUNK], ra_out[...])
+def accumulate(patch_ref, beam_ref, table, dec_back, ra_out, total):
+    dec_rows = total.shape[1]
+    for m in range(0, dec_back.shape[0], CHUNK):
+        patches = dot(dec_back[m : m + CHUNK], ra_out[...])
         for i in range(CHUNK // dec_rows):
             p = m // dec_rows + i
             patch = patches[i * dec_rows : (i + 1) * dec_rows]
             patch_grad = (table[beam_ref[p]].astype(jnp.float32) * patch).astype(jnp.bfloat16).astype(jnp.float32)
             total[patch_ref[p]] = total[patch_ref[p]] + patch_grad
+
+
+def write_sums(total, me_ref, outs):
+    tiles, dec_rows, width = total.shape
     from_left = iota((dec_rows, width), 1) % SPAN >= SPAN // 2
-    tiles = total.shape[0]
+    paired = me_ref is not None
 
     def one_facet(index, carry):
         for side, out_ref in enumerate(outs):
@@ -169,50 +119,137 @@
             out_ref[index, 2, 0] = jnp.where(from_left, total[left], total[right]).astype(out_ref.dtype)
         return carry
 
-    lax.fori_loop(0, facets, one_facet, 0, unroll=4)
-
-
-def gradient_call(patch_of, beam_of, vis, beams, m_ra, m_dec, facets, me=None, slot_of=None, tiles=None):
+    lax.fori_loop(0, outs[0].shape[0], one_facet, 0, unroll=4)
+
+
+def vis_copy(vis_ref, held, arrived, channel):
+    return pltpu.make_async_copy(vis_ref.at[channel], held.at[channel], arrived.at[channel])
+
+
+def wait_and_start_next(vis_ref, held, arrived, channel):
+    vis_copy(vis_ref, held, arrived, channel).wait()
+
+    @pl.when(channel + 1 < held.shape[0])
+    def _():
+        vis_copy(vis_ref, held, arrived, channel + 1).start()
+
+
+def group_data(held, channel, group, columns):
+    data = held[channel, :, group * GROUP : (group + 1) * GROUP, columns]
+    return data.reshape(-1, data.shape[-1])
+
+
+def blocks(owned, samples):
+    groups = owned // GROUP
+    for group in range(groups):
+        for k in range(0, samples, COLUMNS):
+            yield group, slice(k, k + COLUMNS)
+
+
+def first_gradient_kernel(paired, patch_ref, beam_ref, *refs):
+    me_ref, refs = (refs[0], refs[1:]) if paired else (None, refs)
+    vis_ref, beams_ref, m_ra_ref, m_dec_ref, *refs = refs
+    outs, refs = refs[: 1 + paired], refs[1 + paired :]
+    table, back, forward, ra_out, ra_in, total, dec_back, swap, order, held, arrived = refs
+    channel = pl.program_id(0)
+    channels, dec_rows, owned, samples = held.shape
+    width = m_ra_ref.shape[0]
+    beam_count = beams_ref.shape[2]
+    size = GROUP * dec_rows
+
+    @pl.when(channel == 0)
+    def _():
+        vis_copy(vis_ref, held, arrived, 0).start()
+        back[...] = back_matrix(m_dec_ref[...])
+        forward[...] = forward_matrix(m_dec_ref[...])
+        order[...] = phase_rows(width)
+        swap[...] = swap_rows(dec_rows, beam_count)
+        ra_out[...] = dot(m_ra_ref[...], order[...], ((0,), (1,))).astype(jnp.bfloat16)
+        ra_in[...] = dot(order[...], m_ra_ref[...]).astype(jnp.bfloat16)
+
+    swapped = dot(swap[...], beams_ref[0].reshape(dec_rows * beam_count, width)).astype(jnp.bfloat16)
+    ordered = dot(swapped, order[...], ((1,), (1,))).astype(jnp.bfloat16)
+    table[0] = ordered.reshape(beam_count, dec_rows, width)
+    total[...] = jnp.zeros_like(total)
+    wait_and_start_next(vis_ref, held, arrived, channel)
+    for group, columns in blocks(owned, samples):
+        rows = slice(group * size, (group + 1) * size)
+        dec_back[rows, columns] = dot(back[...], group_data(held, channel, group, columns)).astype(jnp.bfloat16)
+    accumulate(patch_ref, beam_ref, table.at[0], dec_back, ra_out, total)
+    write_sums(total, me_ref, outs)
+
+
+def second_gradient_kernel(paired, patch_ref, beam_ref, slot_ref, *refs):
+    me_ref, refs = (refs[0], refs[1:]) if paired else (None, refs)
+    vis_ref, table, back, forward, ra_out, ra_in, tiles_ref, *refs = refs
+    outs, refs = refs[: 1 + paired], refs[1 + paired :]
+    total, rows_k, weighted, held, arrived = refs
+    channel = pl.program_id(0)
+    channels, dec_rows, owned, samples = held.shape
+    size = GROUP * dec_rows
+
+    @pl.when(channel == 0)
+    def _():
+        vis_copy(vis_ref, held, arrived, 0).start()
+
+    total[...] = jnp.zeros_like(total)
+    for p in range(owned):
+        weighted[p * dec_rows : (p + 1) * dec_rows] = (
+            table[0, beam_ref[p]].astype(jnp.float32)
+            * tiles_ref[slot_ref[p] * channels + channel].astype(jnp.float32)
+        ).astype(jnp.bfloat16)
+    for m in range(0, owned * dec_rows, CHUNK):
+        rows_k[m : m + CHUNK] = dot(weighted[m : m + CHUNK], ra_in[...]).astype(jnp.bfloat16)
+    wait_and_start_next(vis_ref, held, arrived, channel)
+    for group, columns in blocks(owned, samples):
+        rows = slice(group * size, (group + 1) * size)
+        predicted = dot(forward[...], rows_k[rows, columns])
+        data = group_data(held, channel, group, columns).astype(jnp.float32)
+        rows_k[rows, columns] = (predicted - data).astype(jnp.bfloat16)
+    for group, columns in blocks(owned, samples):
+        rows = slice(group * size, (group + 1) * size)
+        rows_k[rows, columns] = dot(back[...], rows_k[rows, columns]).astype(jnp.bfloat16)
+    accumulate(patch_ref, beam_ref, table.at[0], rows_k, ra_out, total)
+    write_sums(total, me_ref, outs)
+
+
+def gradient_call(scalars, vis, operands, facets, paired, second):
     channels, dec_rows, owned, samples = vis.shape
-    width = m_ra.shape[0]
-    beam_count = beams.shape[2]
-    second, paired = tiles is not None, me is not None
-    scalars = [patch_of, beam_of] + [me] * paired + [slot_of] * second
-    whole = lambda c, *_: (0, 0)
-    in_specs = [
-        pl.BlockSpec((1, dec_rows, owned, samples), lambda c, *_: (c, 0, 0, 0)),
-        pl.BlockSpec((1, dec_rows, beam_count, width), lambda c, *_: (c, 0, 0, 0)),
-        pl.BlockSpec(m_ra.shape, whole),
-        pl.BlockSpec(m_dec.shape, whole),
-    ]
-    operands = [vis, beams, m_ra, m_dec]
-    size = GROUP * GROUP
-    back = pltpu.VMEM((size, size), jnp.bfloat16)
-    ra_out = pltpu.VMEM((samples, width), jnp.bfloat16)
-    ra_in = pltpu.VMEM((width, samples), jnp.bfloat16)
-    tail = [
-        pltpu.VMEM((beam_count, dec_rows, width), jnp.bfloat16),
+    width = LANES
+    beam_count = operands[0].shape[2] if not second else operands[0].shape[1]
+    size = GROUP * dec_rows
+    whole = lambda shape: pl.BlockSpec(shape, lambda c, *_: (0,) * len(shape))
+    channel_block = lambda *shape: pl.BlockSpec((1,) + shape, lambda c, *_: (c,) + (0,) * len(shape))
+    kept, sum_type = (facets // 2, jnp.float32) if paired else (facets, jnp.bfloat16)
+    out_shapes = [jax.ShapeDtypeStruct((kept, SLOTS, channels, dec_rows, width), sum_type)] * (1 + paired)
+    out_specs = [pl.BlockSpec((kept, SLOTS, 1, dec_rows, width), lambda c, *_: (0, 0, c, 0, 0))] * (1 + paired)
+    in_specs = [pl.BlockSpec(memory_space=pltpu.HBM)]
+    in_specs.append(channel_block(*operands[0].shape[1:]))
+    if not second:
+        shared = [(size, size), (size, size), (samples, width), (width, samples)]
+        out_shapes.append(jax.ShapeDtypeStruct((channels, beam_count, dec_rows, width), jnp.bfloat16))
+        out_specs.append(channel_block(beam_count, dec_rows, width))
+        out_shapes += [jax.ShapeDtypeStruct(shape, jnp.bfloat16) for shape in shared]
+        out_specs += [whole(shape) for shape in shared]
+    in_specs += [whole(operand.shape) for operand in operands[1:]]
+    scratch = [
         pltpu.VMEM((2 * facets, dec_rows, width), jnp.float32),
         pltpu.VMEM((owned * dec_rows, samples), jnp.bfloat16),
-        pltpu.VMEM((owned * dec_rows, width), jnp.bfloat16),
     ]
     if second:
-        in_specs.append(pl.BlockSpec(tiles.shape, lambda c, *_: (0, 0, 0)))
-        operands.append(tiles)
-        scratch = [back, back, ra_out, ra_in] + tail
+        scratch.append(pltpu.VMEM((owned * dec_rows, width), jnp.bfloat16))
     else:
-        scratch = [back, ra_out] + tail
+        scratch += [pltpu.VMEM((size, size), jnp.bfloat16), pltpu.VMEM((width, width), jnp.bfloat16)]
+    scratch += [pltpu.VMEM(vis.shape, jnp.bfloat16), pltpu.SemaphoreType.DMA((channels,))]
     work = channels * owned * samples * dec_rows
-    kept, sum_type = (facets // 2, jnp.float32) if paired else (facets, jnp.bfloat16)
-    out_shape = jax.ShapeDtypeStruct((kept, SLOTS, channels, dec_rows, width), sum_type)
     return pl.pallas_call(
-        functools.partial(gradient_kernel, second, paired),
-        out_shape=[out_shape] * (1 + paired),
+        functools.partial(second_gradient_kernel if second else first_gradient_kernel, paired),
+        out_shape=out_shapes,
         grid_spec=pltpu.PrefetchScalarGridSpec(
             num_scalar_prefetch=len(scalars),
             grid=(channels,),
             in_specs=in_specs,
-            out_specs=[pl.BlockSpec((kept, SLOTS, 1, dec_rows, width), lambda c, *_: (0, 0, c, 0, 0))] * (1 + paired),
+            out_specs=out_specs,
             scratch_shapes=scratch,
         ),
         compiler_params=pltpu.CompilerParams(vmem_limit_bytes=48 << 20),
@@ -220,7 +257,7 @@
             flops=(4 if second else 2) * 256 * work, bytes_accessed=2 * work, transcendentals=0
         ),
         name="second_gradient" if second else "first_gradient",
-    )(*scalars, *operands)
+    )(*scalars, vis, *operands)
 
 
 def shrink(values, bound):
@@ -258,7 +295,7 @@
 
 def prox_kernel(second, parts, *refs):
     part_refs, (thresholds_ref, step_ref, *refs) = refs[:parts], refs[parts:]
-    first_ref, out_ref, summed, columns, natural = refs
+    first_ref, out_ref, summed, columns, natural, tops = refs
     rows = part_refs[0].shape[1]
     dec_rows = first_ref.shape[1]
     channels = step_ref.shape[0]
@@ -325,7 +362,6 @@
             columns[6 + e, d] = roll(middle, -1)
 
     low_pass, high_pass = filter_table(BASES)
-    result = [[None] * dec_rows for _ in range(2)]
     for b in range(BASES):
         low, high = [float(v) for v in low_pass[b]], [float(v) for v in high_pass[b]]
         bound = spread([thresholds_ref[b, c] for c in range(channels)]) * step
@@ -335,39 +371,40 @@
         coarse_b = [shrink(v, bound) for v in dec_analysis(ra_high, low, high)]
         smooth, detail = coarse_a[: dec_rows // 2], [shrink(v, bound) for v in coarse_a[dec_rows // 2 :]]
         pair = lambda even, odd: jnp.where(upper, jnp.float32(odd), jnp.float32(even))
+        pair_sum = lambda values, factors: sum(pair(*f) * v for f, v in zip(factors, values) if f != (0.0, 0.0))
         fine = []
         for value in smooth:
             moved = [value] + [roll(value, -i) for i in (1, 2, 3)]
-            lows = sum(pair(low[2 * i], low[2 * i + 1]) * moved[i] for i in range(4))
-            highs = sum(pair(high[2 * i], high[2 * i + 1]) * moved[i] for i in range(4))
+            lows = pair_sum(moved, [(low[2 * i], low[2 * i + 1]) for i in range(4)])
+            highs = pair_sum(moved, [(high[2 * i], high[2 * i + 1]) for i in range(4)])
             fine.append(halves(lows, highs) + swap(halves(highs, lows)))
         fine = [shrink(v, bound) for v in dec_analysis(fine, low, high)]
         fine = dec_synthesis(fine, low, high)
         smooth = []
         for value in fine:
             moved = [value] + [roll(value, i) for i in (1, 2, 3)]
-            evens = sum(pair(low[2 * i], high[2 * i]) * moved[i] for i in range(4))
-            odds = sum(pair(low[2 * i + 1], high[2 * i + 1]) * moved[i] for i in range(4))
+            evens = pair_sum(moved, [(low[2 * i], high[2 * i]) for i in range(4)])
+            odds = pair_sum(moved, [(low[2 * i + 1], high[2 * i + 1]) for i in range(4)])
             smooth.append(halves(evens, odds) + swap(halves(odds, evens)))
         top_low = dec_synthesis(smooth + detail, low, high)
         top_high = dec_synthesis(coarse_b, low, high)
         for d in range(dec_rows):
-            shifted = []
-            for value in (top_low[d], top_high[d]):
-                other = swap(value)
-                before = halves(roll(other, 1), other)
-                shifted.append([value, before, roll(value, 1), roll(before, 1)])
-            for e in range(2):
-                terms = []
-                for i in range(4):
-                    terms.append((low[2 * i + e], shifted[0][i]))
-                    terms.append((high[2 * i + e], shifted[1][i]))
-                value = combine(terms)
-                result[e][d] = value if b == 0 else result[e][d] + value
+            tops[b, 0, d], tops[b, 1, d] = top_low[d], top_high[d]
 
     for d in range(dec_rows):
-        evens = jnp.maximum(result[0][d] * (1.0 / BASES), 0.0)
-        odds = jnp.maximum(result[1][d] * (1.0 / BASES), 0.0)
+        images = []
+        for e in range(2):
+            parts = [
+                combine(
+                    [(float(low_pass[b, 2 * i + e]), tops[b, 0, d]) for b in range(BASES)]
+                    + [(float(high_pass[b, 2 * i + e]), tops[b, 1, d]) for b in range(BASES)]
+                )
+                for i in range(4)
+            ]
+            other = swap(parts[1] + roll(parts[3], 1))
+            value = parts[0] + roll(parts[2], 1) + halves(roll(other, 1), other)
+            images.append(jnp.maximum(value * (1.0 / BASES), 0.0))
+        evens, odds = images
         if not second:
             first_ref[0, d], first_ref[1, d] = evens, odds
         even_other, odd_other = swap(evens), swap(odds)
@@ -424,6 +461,7 @@
             pltpu.VMEM((4 * channels * dec_rows, LANES), jnp.float32),
             pltpu.VMEM((8, dec_rows, 8, LANES), jnp.float32),
             pltpu.VMEM((2 * channels * dec_rows, LANES), jnp.float32),
+            pltpu.VMEM((BASES, 2, dec_rows, 8, LANES), jnp.float32),
         ],
         compiler_params=pltpu.CompilerParams(vmem_limit_bytes=32 << 20),
         name="second_prox" if second else "first_prox",
@@ -503,10 +541,13 @@
         exchange = lambda sums: [lax.all_to_all(sums, "ra", split_axis=0, concat_axis=0, tiled=True)]
         gather = lambda tiles: lax.all_gather(tiles, "ra", axis=0, tiled=True)
 
-    sums = gradient_call(patch_of, beam_of, vis, beams, m_ra, m_dec, facets, me)
+    base = [me] if paired else []
+    sent = 1 + paired
+    sums = gradient_call([patch_of, beam_of] + base, vis, [beams, m_ra, m_dec], facets, paired, False)
+    sums, shared = sums[:sent], sums[sent:]
     first, tiles = prox_call(exchange(*sums), thresholds, step_size, dec_rows)
     tiles = gather(tiles).reshape(facets * per_facet * channels, dec_rows, width)
-    sums = gradient_call(patch_of, beam_of, vis, beams, m_ra, m_dec, facets, me, slot_of, tiles)
+    sums = gradient_call([patch_of, beam_of, slot_of] + base, vis, [*shared, tiles], facets, paired, True)
     return prox_call(exchange(*sums), thresholds, step_size, dec_rows, first)
 
 

time: 88.9 us -> 79.5 us (0.89)
  Pallas kernels: 38.6 us -> 29.2 us
    pallas_call x2, Pallas kernels: 28.5 us -> 23.6 us  [gradient_call(): pl.pallas_call(functools.partial(second_gradient_kernel if second else fi...]
    pallas_call x2, Pallas kernels: 9.78 us -> 5.28 us  [prox_call(): pl.pallas_call(functools.partial(prox_kernel, second, len(received)), out...]
where the time goes in v4:
time: 79.5 us; the launch traced here: 79.3 us
  starting transfers between devices  29.8 us (37%)
  Pallas kernels  29.2 us (37%)
  waiting for transfers between devices  19.6 us (25%)
    ppermute x21, starting transfers between devices, across(): lax.ppermute(value, 'ra', [(source, source ^ difference) for source in ra...  29.8 us
    pallas_call x2, Pallas kernels, gradient_call(): pl.pallas_call(functools.partial(second_gradient_kernel if second else fi...  23.6 us
    ppermute x21, waiting for transfers between devices, across(): lax.ppermute(value, 'ra', [(source, source ^ difference) for source in ra...  19.6 us
    pallas_call x2, Pallas kernels, prox_call(): pl.pallas_call(functools.partial(prox_kernel, second, len(received)), out...  5.28 us
  transfers between devices with their start and end apart: 21, of which 14 were waited for; matrix products, arithmetic and copies ran while one was open for 0% of the time, Pallas kernels for 0%

profile of v4, /device:TPU:0, one launch (start us, length us, event | category | flops | bytes accessed | tf_op | source)
XLA Modules:
  0.0 79.3 jit_solution(7949894677307179270)
XLA Ops:
  0.0 0.7 bitcast_add_fusion
  0.7 10.3 %first_gradient.1 = (f32[8,3,4,16,128]{4,3,2,1,0:T(8,128)S(1)}, f32[8,3,4,16,128]{4,3,2,1,0:T(8,128)S(1)}, bf16[4,16,16,128]{3,2,1,0:T(8,128)(2,1)S(1)}, bf16[25...) custom-call(s32[128]{0:T(128)S(1)} %get-tuple-element.60.patch_ref, ...), custom_call_target="tpu_custom_call" | custom-call | flops 2147483648 | bytes 8388608 | tf_op jit(solution)/shard_map/first_gradient/pallas_call | solution.py:245
  11.0 0.5 collective-permute-start
  11.5 1.9 %collective-permute-done.got_ref = f32[8,3,4,16,128]{4,3,2,1,0:T(8,128)S(1)} collective-permute-done((f32[8,3,4,16,128]{4,3,2,1,0:T(8,128)S(1)}, f32[8,3,4,16,128]{4,3,2,1,0:T(8,128)S(1)}, u32[]{:S(2)}, u32[]{:S(2)}) %collective-permute-start) | collective-permute-done | bytes 786464 | tf_op jit(solution)/shard_map/ppermute | solution.py:504
  13.6 6.0 %collective-permute-start.1 = (bf16[1,3,4,16,128]{4,3,2,1,0:T(8,128)(2,1)S(1)}, bf16[1,3,4,16,128]{4,3,2,1,0:T(8,128)(2,1)S(1)}, u32[]{:S(2)}, u32[]{:S(2)}) collective-permute-start(bf16[1,3,4,16,128]{4,3,2,1,0:T(8,128)(2,1)S(1)} %get-tuple-element.40), channel_id=1, source_target_pairs={{0,14},{1,15},{2,12},{3,13},{4,10},{5,11},{6,8},{7,9},{8,6},{9,7},... | collective-permute-start | bytes 147464 | tf_op jit(solution)/shard_map/ppermute | solution.py:504
  19.8 0.8 collective-permute-start.3
  20.5 2.0 %collective-permute-start.4 = (bf16[1,3,4,16,128]{4,3,2,1,0:T(8,128)(2,1)S(1)}, bf16[1,3,4,16,128]{4,3,2,1,0:T(8,128)(2,1)S(1)}, u32[]{:S(2)}, u32[]{:S(2)}) collective-permute-start(bf16[1,3,4,16,128]{4,3,2,1,0:T(8,128)(2,1)S(1)} %get-tuple-element.43), channel_id=1, source_target_pairs={{0,8},{1,9},{2,10},{3,11},{4,12},{5,13},{6,14},{7,15},{8,0},{9,1},... | collective-permute-start | bytes 147464 | tf_op jit(solution)/shard_map/ppermute | solution.py:504
  22.6 2.3 %collective-permute-start.5 = (bf16[1,3,4,16,128]{4,3,2,1,0:T(8,128)(2,1)S(1)}, bf16[1,3,4,16,128]{4,3,2,1,0:T(8,128)(2,1)S(1)}, u32[]{:S(2)}, u32[]{:S(2)}) collective-permute-start(bf16[1,3,4,16,128]{4,3,2,1,0:T(8,128)(2,1)S(1)} %get-tuple-element.44), channel_id=1, source_target_pairs={{0,6},{1,7},{2,4},{3,5},{4,2},{5,3},{6,0},{7,1},{8,14},{9,15},{10,... | collective-permute-start | bytes 147464 | tf_op jit(solution)/shard_map/ppermute | solution.py:504
  24.9 0.8 collective-permute-start.6
  26.1 1.0 %collective-permute-done.3 = bf16[1,3,4,16,128]{4,3,2,1,0:T(8,128)(2,1)S(1)} collective-permute-done((bf16[1,3,4,16,128]{4,3,2,1,0:T(8,128)(2,1)S(1)}, bf16[1,3,4,16,128]{4,3,2,1,0:T(8,128)(2,1)S(1)}, u32[]{:S(2)}, u32[]{:S(2)}) %collective-permute-start.3) | collective-permute-done | bytes 49184 | tf_op jit(solution)/shard_map/ppermute | solution.py:504
  27.1 0.9 %collective-permute-done.4 = bf16[1,3,4,16,128]{4,3,2,1,0:T(8,128)(2,1)S(1)} collective-permute-done((bf16[1,3,4,16,128]{4,3,2,1,0:T(8,128)(2,1)S(1)}, bf16[1,3,4,16,128]{4,3,2,1,0:T(8,128)(2,1)S(1)}, u32[]{:S(2)}, u32[]{:S(2)}) %collective-permute-start.4) | collective-permute-done | bytes 49184 | tf_op jit(solution)/shard_map/ppermute | solution.py:504
  27.9 1.1 %collective-permute-done.5 = bf16[1,3,4,16,128]{4,3,2,1,0:T(8,128)(2,1)S(1)} collective-permute-done((bf16[1,3,4,16,128]{4,3,2,1,0:T(8,128)(2,1)S(1)}, bf16[1,3,4,16,128]{4,3,2,1,0:T(8,128)(2,1)S(1)}, u32[]{:S(2)}, u32[]{:S(2)}) %collective-permute-start.5) | collective-permute-done | bytes 49184 | tf_op jit(solution)/shard_map/ppermute | solution.py:504
  29.2 0.5 collective-permute-done.7
  29.7 2.6 %first_prox.1 = (f32[2,16,8,128]{3,2,1,0:T(8,128)S(1)}, bf16[128,128]{1,0:T(8,128)(2,1)S(1)}) custom-call(f32[1,192,128]{2,1,0:T(8,128)S(1)} %bitcast.23, bf16[1,192,128]{2,1,0:T(8,128)(2,1)S(1)} %bitcast.32, bf16[1,192,128]{2,1,0:T(8,128)(2,1)S(1)} %bitcast.33, bf16[1,192,128]{2,1,0:T(8,128)(2,1)S(1)} %bitcast.34, bf16[1,192,128]{2,1,0:T(8,128)(2,1)S(1)} %bitcast.35, ...), custom_call_target="tpu_custom_call" | custom-call | tf_op jit(solution)/shard_map/first_prox/pallas_call | solution.py:455
  32.3 0.9 %collective-permute-start.8 = (bf16[128,128]{1,0:T(8,128)(2,1)S(1)}, bf16[128,128]{1,0:T(8,128)(2,1)S(1)}, u32[]{:S(2)}, u32[]{:S(2)}) collective-permute-start(bf16[128,128]{1,0:T(8,128)(2,1)S(1)} %get-tuple-element.47.refs_0_), channel_id=1, source_target_pairs={{0,2},{1,3},{2,0},{3,1},{4,6},{5,7},{6,4},{7,5},{8,10},{9,11},{10,... | collective-permute-start | bytes 98312 | tf_op jit(solution)/shard_map/ppermute | solution.py:504
  33.2 3.1 %collective-permute-done.8.refs_1_ = bf16[128,128]{1,0:T(8,128)(2,1)S(1)} collective-permute-done((bf16[128,128]{1,0:T(8,128)(2,1)S(1)}, bf16[128,128]{1,0:T(8,128)(2,1)S(1)}, u32[]{:S(2)}, u32[]{:S(2)}) %collective-permute-start.8) | collective-permute-done | bytes 32800 | tf_op jit(solution)/shard_map/ppermute | solution.py:504
  36.3 3.6 %collective-permute-start.11 = (bf16[256,128]{1,0:T(8,128)(2,1)S(1)}, bf16[256,128]{1,0:T(8,128)(2,1)S(1)}, u32[]{:S(2)}, u32[]{:S(2)}) collective-permute-start(bf16[256,128]{1,0:T(8,128)(2,1)S(1)} %join.3.refs_0_), channel_id=1, source_target_pairs={{0,12},{1,13},{2,14},{3,15},{4,8},{5,9},{6,10},{7,11},{8,4},{9,5},... | collective-permute-start | bytes 196616 | tf_op jit(solution)/shard_map/ppermute | solution.py:504
  39.9 0.8 collective-permute-start.9
  40.7 1.8 %collective-permute-done.11.refs_3_ = bf16[256,128]{1,0:T(8,128)(2,1)S(1)} collective-permute-done((bf16[256,128]{1,0:T(8,128)(2,1)S(1)}, bf16[256,128]{1,0:T(8,128)(2,1)S(1)}, u32[]{:S(2)}, u32[]{:S(2)}) %collective-permute-start.11) | collective-permute-done | bytes 65568 | tf_op jit(solution)/shard_map/ppermute | solution.py:504
  42.5 2.6 %collective-permute-done.10.refs_2_ = bf16[256,128]{1,0:T(8,128)(2,1)S(1)} collective-permute-done((bf16[256,128]{1,0:T(8,128)(2,1)S(1)}, bf16[256,128]{1,0:T(8,128)(2,1)S(1)}, u32[]{:S(2)}, u32[]{:S(2)}) %collective-permute-start.10) | collective-permute-done | bytes 65568 | tf_op jit(solution)/shard_map/ppermute | solution.py:504
  45.2 1.5 %collective-permute-done.12.refs_1_ = bf16[1024,128]{1,0:T(8,128)(2,1)S(1)} collective-permute-done((bf16[1024,128]{1,0:T(8,128)(2,1)S(1)}, bf16[1024,128]{1,0:T(8,128)(2,1)S(1)}, u32[]{:S(2)}, u32[]{:S(2)}) %collective-permute-start.12) | collective-permute-done | bytes 262176 | tf_op jit(solution)/shard_map/ppermute | solution.py:504
  46.7 13.2 %second_gradient.1 = (f32[8,3,4,16,128]{4,3,2,1,0:T(8,128)S(1)}, f32[8,3,4,16,128]{4,3,2,1,0:T(8,128)S(1)}) custom-call(s32[128]{0:T(128)S(1)} %get-tuple-element.60.patch_ref, s32[128]{0:T(128)} %beam_ref.3, s32[128]{0:T(128)S(1)} %get-tuple-element.59.slot_ref, s32[1]{0:T(128)} %bitcast.2.refs_0_, bf16[4,16,128,512]{3,2,1,0:T(8,128)(2,1)} %refs_1_.3, ...), custom_call_target="tpu_custom_call" | custom-call | flops 4294967296 | bytes 8388608 | tf_op jit(solution)/shard_map/second_gradient/pallas_call | solution.py:245
  60.2 2.1 %collective-permute-done.13.got_ref = f32[8,3,4,16,128]{4,3,2,1,0:T(8,128)S(1)} collective-permute-done((f32[8,3,4,16,128]{4,3,2,1,0:T(8,128)S(1)}, f32[8,3,4,16,128]{4,3,2,1,0:T(8,128)S(1)}, u32[]{:S(2)}, u32[]{:S(2)}) %collective-permute-start.13) | collective-permute-done | bytes 786464 | tf_op jit(solution)/shard_map/ppermute | solution.py:504
  62.5 2.0 %collective-permute-start.14 = (bf16[1,3,4,16,128]{4,3,2,1,0:T(8,128)(2,1)S(1)}, bf16[1,3,4,16,128]{4,3,2,1,0:T(8,128)(2,1)S(1)}, u32[]{:S(2)}, u32[]{:S(2)}) collective-permute-start(bf16[1,3,4,16,128]{4,3,2,1,0:T(8,128)(2,1)S(1)} %get-tuple-element.51), channel_id=1, source_target_pairs={{0,14},{1,15},{2,12},{3,13},{4,10},{5,11},{6,8},{7,9},{8,6},{9,7},... | collective-permute-start | bytes 147464 | tf_op jit(solution)/shard_map/ppermute | solution.py:504
  64.4 1.9 %collective-permute-start.15 = (bf16[1,3,4,16,128]{4,3,2,1,0:T(8,128)(2,1)S(1)}, bf16[1,3,4,16,128]{4,3,2,1,0:T(8,128)(2,1)S(1)}, u32[]{:S(2)}, u32[]{:S(2)}) collective-permute-start(bf16[1,3,4,16,128]{4,3,2,1,0:T(8,128)(2,1)S(1)} %get-tuple-element.52), channel_id=1, source_target_pairs={{0,12},{1,13},{2,14},{3,15},{4,8},{5,9},{6,10},{7,11},{8,4},{9,5},... | collective-permute-start | bytes 147464 | tf_op jit(solution)/shard_map/ppermute | solution.py:504
  66.3 1.2 %collective-permute-start.16 = (bf16[1,3,4,16,128]{4,3,2,1,0:T(8,128)(2,1)S(1)}, bf16[1,3,4,16,128]{4,3,2,1,0:T(8,128)(2,1)S(1)}, u32[]{:S(2)}, u32[]{:S(2)}) collective-permute-start(bf16[1,3,4,16,128]{4,3,2,1,0:T(8,128)(2,1)S(1)} %get-tuple-element.53), channel_id=1, source_target_pairs={{0,10},{1,11},{2,8},{3,9},{4,14},{5,15},{6,12},{7,13},{8,2},{9,3},... | collective-permute-start | bytes 147464 | tf_op jit(solution)/shard_map/ppermute | solution.py:504
  67.5 2.7 %collective-permute-start.17 = (bf16[1,3,4,16,128]{4,3,2,1,0:T(8,128)(2,1)S(1)}, bf16[1,3,4,16,128]{4,3,2,1,0:T(8,128)(2,1)S(1)}, u32[]{:S(2)}, u32[]{:S(2)}) collective-permute-start(bf16[1,3,4,16,128]{4,3,2,1,0:T(8,128)(2,1)S(1)} %get-tuple-element.54), channel_id=1, source_target_pairs={{0,8},{1,9},{2,10},{3,11},{4,12},{5,13},{6,14},{7,15},{8,0},{9,1},... | collective-permute-start | bytes 147464 | tf_op jit(solution)/shard_map/ppermute | solution.py:504
  70.2 1.9 %collective-permute-start.19 = (bf16[1,3,4,16,128]{4,3,2,1,0:T(8,128)(2,1)S(1)}, bf16[1,3,4,16,128]{4,3,2,1,0:T(8,128)(2,1)S(1)}, u32[]{:S(2)}, u32[]{:S(2)}) collective-permute-start(bf16[1,3,4,16,128]{4,3,2,1,0:T(8,128)(2,1)S(1)} %get-tuple-element.56), channel_id=1, source_target_pairs={{0,4},{1,5},{2,6},{3,7},{4,0},{5,1},{6,2},{7,3},{8,12},{9,13},{10,... | collective-permute-start | bytes 147464 | tf_op jit(solution)/shard_map/ppermute | solution.py:504
  72.2 1.5 %collective-permute-start.20 = (bf16[1,3,4,16,128]{4,3,2,1,0:T(8,128)(2,1)S(1)}, bf16[1,3,4,16,128]{4,3,2,1,0:T(8,128)(2,1)S(1)}, u32[]{:S(2)}, u32[]{:S(2)}) collective-permute-start(bf16[1,3,4,16,128]{4,3,2,1,0:T(8,128)(2,1)S(1)} %get-tuple-element.57), channel_id=1, source_target_pairs={{0,2},{1,3},{2,0},{3,1},{4,6},{5,7},{6,4},{7,5},{8,10},{9,11},{10,... | collective-permute-start | bytes 147464 | tf_op jit(solution)/shard_map/ppermute | solution.py:504
  73.7 1.0 %collective-permute-done.16 = bf16[1,3,4,16,128]{4,3,2,1,0:T(8,128)(2,1)S(1)} collective-permute-done((bf16[1,3,4,16,128]{4,3,2,1,0:T(8,128)(2,1)S(1)}, bf16[1,3,4,16,128]{4,3,2,1,0:T(8,128)(2,1)S(1)}, u32[]{:S(2)}, u32[]{:S(2)}) %collective-permute-start.16) | collective-permute-done | bytes 49184 | tf_op jit(solution)/shard_map/ppermute | solution.py:504
  74.7 1.7 %collective-permute-done.18 = bf16[1,3,4,16,128]{4,3,2,1,0:T(8,128)(2,1)S(1)} collective-permute-done((bf16[1,3,4,16,128]{4,3,2,1,0:T(8,128)(2,1)S(1)}, bf16[1,3,4,16,128]{4,3,2,1,0:T(8,128)(2,1)S(1)}, u32[]{:S(2)}, u32[]{:S(2)}) %collective-permute-start.18) | collective-permute-done | bytes 49184 | tf_op jit(solution)/shard_map/ppermute | solution.py:504
  76.6 2.7 %second_prox.1 = f32[4,16,256]{2,1,0:T(8,128)} custom-call(f32[1,192,128]{2,1,0:T(8,128)S(1)} %bitcast.24, bf16[1,192,128]{2,1,0:T(8,128)(2,1)S(1)} %bitcast.25, bf16[1,192,128]{2,1,0:T(8,128)(2,1)S(1)} %bitcast.26, bf16[1,192,128]{2,1,0:T(8,128)(2,1)S(1)} %bitcast.27, bf16[1,192,128]{2,1,0:T(8,128)(2,1)S(1)} %bitcast.28, bf16[1,192,128]{2,1,0:T(8,128)(2,1)S(1)} %bitcast.29, ...), custom_call_target="tpu_custom_call" | custom-call | tf_op jit(solution)/shard_map/second_prox/pallas_call | solution.py:455
  (24 shorter events, 1.8 us)
Async XLA Ops:
  0.0 29.7 %copy-start = (f32[4,4]{1,0:T(4,128)S(1)}, f32[4,4]{1,0:T(4,128)}, u32[]{:S(2)}) copy-start(f32[4,4]{1,0:T(4,128)} %refs_8_.3) | copy-start | bytes 196
  0.0 29.7 %copy-start.1 = (f32[4]{0:T(128)S(1)}, f32[4]{0:T(128)}, u32[]{:S(2)}) copy-start(f32[4]{0:T(128)} %refs_9_.3) | copy-start | bytes 52
  11.0 2.4 %collective-permute-start = (f32[8,3,4,16,128]{4,3,2,1,0:T(8,128)S(1)}, f32[8,3,4,16,128]{4,3,2,1,0:T(8,128)S(1)}, u32[]{:S(2)}, u32[]{:S(2)}) collective-permute-start(f32[8,3,4,16,128]{4,3,2,1,0:T(8,128)S(1)} %get-tuple-element.38), channel_id=1, source_target_pairs={{0,1},{1,0},{2,3},{3,2},{4,5},{5,4},{6,7},{7,6},{8,9},{9,8},{10,11... | collective-permute-start | bytes 2359304 | tf_op jit(solution)/shard_map/ppermute | solution.py:504
  13.6 11.3 %collective-permute-start.1 = (bf16[1,3,4,16,128]{4,3,2,1,0:T(8,128)(2,1)S(1)}, bf16[1,3,4,16,128]{4,3,2,1,0:T(8,128)(2,1)S(1)}, u32[]{:S(2)}, u32[]{:S(2)}) collective-permute-start(bf16[1,3,4,16,128]{4,3,2,1,0:T(8,128)(2,1)S(1)} %get-tuple-element.40), channel_id=1, source_target_pairs={{0,14},{1,15},{2,12},{3,13},{4,10},{5,11},{6,8},{7,9},{8,6},{9,7},... | collective-permute-start | bytes 147464 | tf_op jit(solution)/shard_map/ppermute | solution.py:504
  19.6 6.1 %collective-permute-start.2 = (bf16[1,3,4,16,128]{4,3,2,1,0:T(8,128)(2,1)S(1)}, bf16[1,3,4,16,128]{4,3,2,1,0:T(8,128)(2,1)S(1)}, u32[]{:S(2)}, u32[]{:S(2)}) collective-permute-start(bf16[1,3,4,16,128]{4,3,2,1,0:T(8,128)(2,1)S(1)} %get-tuple-element.41), channel_id=1, source_target_pairs={{0,12},{1,13},{2,14},{3,15},{4,8},{5,9},{6,10},{7,11},{8,4},{9,5},... | collective-permute-start | bytes 147464 | tf_op jit(solution)/shard_map/ppermute | solution.py:504
  19.8 7.3 %collective-permute-start.3 = (bf16[1,3,4,16,128]{4,3,2,1,0:T(8,128)(2,1)S(1)}, bf16[1,3,4,16,128]{4,3,2,1,0:T(8,128)(2,1)S(1)}, u32[]{:S(2)}, u32[]{:S(2)}) collective-permute-start(bf16[1,3,4,16,128]{4,3,2,1,0:T(8,128)(2,1)S(1)} %get-tuple-element.42), channel_id=1, source_target_pairs={{0,10},{1,11},{2,8},{3,9},{4,14},{5,15},{6,12},{7,13},{8,2},{9,3},... | collective-permute-start | bytes 147464 | tf_op jit(solution)/shard_map/ppermute | solution.py:504
  20.5 7.4 %collective-permute-start.4 = (bf16[1,3,4,16,128]{4,3,2,1,0:T(8,128)(2,1)S(1)}, bf16[1,3,4,16,128]{4,3,2,1,0:T(8,128)(2,1)S(1)}, u32[]{:S(2)}, u32[]{:S(2)}) collective-permute-start(bf16[1,3,4,16,128]{4,3,2,1,0:T(8,128)(2,1)S(1)} %get-tuple-element.43), channel_id=1, source_target_pairs={{0,8},{1,9},{2,10},{3,11},{4,12},{5,13},{6,14},{7,15},{8,0},{9,1},... | collective-permute-start | bytes 147464 | tf_op jit(solution)/shard_map/ppermute | solution.py:504
  22.6 6.5 %collective-permute-start.5 = (bf16[1,3,4,16,128]{4,3,2,1,0:T(8,128)(2,1)S(1)}, bf16[1,3,4,16,128]{4,3,2,1,0:T(8,128)(2,1)S(1)}, u32[]{:S(2)}, u32[]{:S(2)}) collective-permute-start(bf16[1,3,4,16,128]{4,3,2,1,0:T(8,128)(2,1)S(1)} %get-tuple-element.44), channel_id=1, source_target_pairs={{0,6},{1,7},{2,4},{3,5},{4,2},{5,3},{6,0},{7,1},{8,14},{9,15},{10,... | collective-permute-start | bytes 147464 | tf_op jit(solution)/shard_map/ppermute | solution.py:504
  24.9 4.4 %collective-permute-start.6 = (bf16[1,3,4,16,128]{4,3,2,1,0:T(8,128)(2,1)S(1)}, bf16[1,3,4,16,128]{4,3,2,1,0:T(8,128)(2,1)S(1)}, u32[]{:S(2)}, u32[]{:S(2)}) collective-permute-start(bf16[1,3,4,16,128]{4,3,2,1,0:T(8,128)(2,1)S(1)} %get-tuple-element.45), channel_id=1, source_target_pairs={{0,4},{1,5},{2,6},{3,7},{4,0},{5,1},{6,2},{7,3},{8,12},{9,13},{10,... | collective-permute-start | bytes 147464 | tf_op jit(solution)/shard_map/ppermute | solution.py:504
  25.6 4.1 %collective-permute-start.7 = (bf16[1,3,4,16,128]{4,3,2,1,0:T(8,128)(2,1)S(1)}, bf16[1,3,4,16,128]{4,3,2,1,0:T(8,128)(2,1)S(1)}, u32[]{:S(2)}, u32[]{:S(2)}) collective-permute-start(bf16[1,3,4,16,128]{4,3,2,1,0:T(8,128)(2,1)S(1)} %get-tuple-element.46), channel_id=1, source_target_pairs={{0,2},{1,3},{2,0},{3,1},{4,6},{5,7},{6,4},{7,5},{8,10},{9,11},{10,... | collective-permute-start | bytes 147464 | tf_op jit(solution)/shard_map/ppermute | solution.py:504
  32.3 4.0 %collective-permute-start.8 = (bf16[128,128]{1,0:T(8,128)(2,1)S(1)}, bf16[128,128]{1,0:T(8,128)(2,1)S(1)}, u32[]{:S(2)}, u32[]{:S(2)}) collective-permute-start(bf16[128,128]{1,0:T(8,128)(2,1)S(1)} %get-tuple-element.47.refs_0_), channel_id=1, source_target_pairs={{0,2},{1,3},{2,0},{3,1},{4,6},{5,7},{6,4},{7,5},{8,10},{9,11},{10,... | collective-permute-start | bytes 98312 | tf_op jit(solution)/shard_map/ppermute | solution.py:504
  36.3 6.2 %collective-permute-start.11 = (bf16[256,128]{1,0:T(8,128)(2,1)S(1)}, bf16[256,128]{1,0:T(8,128)(2,1)S(1)}, u32[]{:S(2)}, u32[]{:S(2)}) collective-permute-start(bf16[256,128]{1,0:T(8,128)(2,1)S(1)} %join.3.refs_0_), channel_id=1, source_target_pairs={{0,12},{1,13},{2,14},{3,15},{4,8},{5,9},{6,10},{7,11},{8,4},{9,5},... | collective-permute-start | bytes 196616 | tf_op jit(solution)/shard_map/ppermute | solution.py:504
  39.9 5.2 %collective-permute-start.10 = (bf16[256,128]{1,0:T(8,128)(2,1)S(1)}, bf16[256,128]{1,0:T(8,128)(2,1)S(1)}, u32[]{:S(2)}, u32[]{:S(2)}) collective-permute-start(bf16[256,128]{1,0:T(8,128)(2,1)S(1)} %join.3.refs_0_), channel_id=1, source_target_pairs={{0,8},{1,9},{2,10},{3,11},{4,12},{5,13},{6,14},{7,15},{8,0},{9,1},... | collective-permute-start | bytes 196616 | tf_op jit(solution)/shard_map/ppermute | solution.py:504
  39.9 5.2 %collective-permute-start.9 = (bf16[256,128]{1,0:T(8,128)(2,1)S(1)}, bf16[256,128]{1,0:T(8,128)(2,1)S(1)}, u32[]{:S(2)}, u32[]{:S(2)}) collective-permute-start(bf16[256,128]{1,0:T(8,128)(2,1)S(1)} %join.3.refs_0_), channel_id=1, source_target_pairs={{0,4},{1,5},{2,6},{3,7},{4,0},{5,1},{6,2},{7,3},{8,12},{9,13},{10,... | collective-permute-start | bytes 196616 | tf_op jit(solution)/shard_map/ppermute | solution.py:504
  45.1 1.6 %collective-permute-start.12 = (bf16[1024,128]{1,0:T(8,128)(2,1)S(1)}, bf16[1024,128]{1,0:T(8,128)(2,1)S(1)}, u32[]{:S(2)}, u32[]{:S(2)}) collective-permute-start(bf16[1024,128]{1,0:T(8,128)(2,1)S(1)} %join.4.refs_0_), channel_id=1, source_target_pairs={{0,1},{1,0},{2,3},{3,2},{4,5},{5,4},{6,7},{7,6},{8,9},{9,8},{10,11... | collective-permute-start | bytes 786440 | tf_op jit(solution)/shard_map/ppermute | solution.py:504
  60.0 2.4 %collective-permute-start.13 = (f32[8,3,4,16,128]{4,3,2,1,0:T(8,128)S(1)}, f32[8,3,4,16,128]{4,3,2,1,0:T(8,128)S(1)}, u32[]{:S(2)}, u32[]{:S(2)}) collective-permute-start(f32[8,3,4,16,128]{4,3,2,1,0:T(8,128)S(1)} %get-tuple-element.49), channel_id=1, source_target_pairs={{0,1},{1,0},{2,3},{3,2},{4,5},{5,4},{6,7},{7,6},{8,9},{9,8},{10,11... | collective-permute-start | bytes 2359304 | tf_op jit(solution)/shard_map/ppermute | solution.py:504
  62.5 7.7 %collective-permute-start.14 = (bf16[1,3,4,16,128]{4,3,2,1,0:T(8,128)(2,1)S(1)}, bf16[1,3,4,16,128]{4,3,2,1,0:T(8,128)(2,1)S(1)}, u32[]{:S(2)}, u32[]{:S(2)}) collective-permute-start(bf16[1,3,4,16,128]{4,3,2,1,0:T(8,128)(2,1)S(1)} %get-tuple-element.51), channel_id=1, source_target_pairs={{0,14},{1,15},{2,12},{3,13},{4,10},{5,11},{6,8},{7,9},{8,6},{9,7},... | collective-permute-start | bytes 147464 | tf_op jit(solution)/shard_map/ppermute | solution.py:504
  64.4 7.7 %collective-permute-start.15 = (bf16[1,3,4,16,128]{4,3,2,1,0:T(8,128)(2,1)S(1)}, bf16[1,3,4,16,128]{4,3,2,1,0:T(8,128)(2,1)S(1)}, u32[]{:S(2)}, u32[]{:S(2)}) collective-permute-start(bf16[1,3,4,16,128]{4,3,2,1,0:T(8,128)(2,1)S(1)} %get-tuple-element.52), channel_id=1, source_target_pairs={{0,12},{1,13},{2,14},{3,15},{4,8},{5,9},{6,10},{7,11},{8,4},{9,5},... | collective-permute-start | bytes 147464 | tf_op jit(solution)/shard_map/ppermute | solution.py:504
  66.3 8.4 %collective-permute-start.16 = (bf16[1,3,4,16,128]{4,3,2,1,0:T(8,128)(2,1)S(1)}, bf16[1,3,4,16,128]{4,3,2,1,0:T(8,128)(2,1)S(1)}, u32[]{:S(2)}, u32[]{:S(2)}) collective-permute-start(bf16[1,3,4,16,128]{4,3,2,1,0:T(8,128)(2,1)S(1)} %get-tuple-element.53), channel_id=1, source_target_pairs={{0,10},{1,11},{2,8},{3,9},{4,14},{5,15},{6,12},{7,13},{8,2},{9,3},... | collective-permute-start | bytes 147464 | tf_op jit(solution)/shard_map/ppermute | solution.py:504
  67.5 7.2 %collective-permute-start.17 = (bf16[1,3,4,16,128]{4,3,2,1,0:T(8,128)(2,1)S(1)}, bf16[1,3,4,16,128]{4,3,2,1,0:T(8,128)(2,1)S(1)}, u32[]{:S(2)}, u32[]{:S(2)}) collective-permute-start(bf16[1,3,4,16,128]{4,3,2,1,0:T(8,128)(2,1)S(1)} %get-tuple-element.54), channel_id=1, source_target_pairs={{0,8},{1,9},{2,10},{3,11},{4,12},{5,13},{6,14},{7,15},{8,0},{9,1},... | collective-permute-start | bytes 147464 | tf_op jit(solution)/shard_map/ppermute | solution.py:504
  70.2 6.1 %collective-permute-start.18 = (bf16[1,3,4,16,128]{4,3,2,1,0:T(8,128)(2,1)S(1)}, bf16[1,3,4,16,128]{4,3,2,1,0:T(8,128)(2,1)S(1)}, u32[]{:S(2)}, u32[]{:S(2)}) collective-permute-start(bf16[1,3,4,16,128]{4,3,2,1,0:T(8,128)(2,1)S(1)} %get-tuple-element.55), channel_id=1, source_target_pairs={{0,6},{1,7},{2,4},{3,5},{4,2},{5,3},{6,0},{7,1},{8,14},{9,15},{10,... | collective-permute-start | bytes 147464 | tf_op jit(solution)/shard_map/ppermute | solution.py:504
  70.2 6.1 %collective-permute-start.19 = (bf16[1,3,4,16,128]{4,3,2,1,0:T(8,128)(2,1)S(1)}, bf16[1,3,4,16,128]{4,3,2,1,0:T(8,128)(2,1)S(1)}, u32[]{:S(2)}, u32[]{:S(2)}) collective-permute-start(bf16[1,3,4,16,128]{4,3,2,1,0:T(8,128)(2,1)S(1)} %get-tuple-element.56), channel_id=1, source_target_pairs={{0,4},{1,5},{2,6},{3,7},{4,0},{5,1},{6,2},{7,3},{8,12},{9,13},{10,... | collective-permute-start | bytes 147464 | tf_op jit(solution)/shard_map/ppermute | solution.py:504
  72.2 4.5 %collective-permute-start.20 = (bf16[1,3,4,16,128]{4,3,2,1,0:T(8,128)(2,1)S(1)}, bf16[1,3,4,16,128]{4,3,2,1,0:T(8,128)(2,1)S(1)}, u32[]{:S(2)}, u32[]{:S(2)}) collective-permute-start(bf16[1,3,4,16,128]{4,3,2,1,0:T(8,128)(2,1)S(1)} %get-tuple-element.57), channel_id=1, source_target_pairs={{0,2},{1,3},{2,0},{3,1},{4,6},{5,7},{6,4},{7,5},{8,10},{9,11},{10,... | collective-permute-start | bytes 147464 | tf_op jit(solution)/shard_map/ppermute | solution.py:504

commit v5 on v4

--- a/solution.py
+++ b/solution.py
@@ -15,7 +15,6 @@
 LANES = 128
 SPAN = LANES // PHASES
 SLOTS = 3
-CHUNK = 256
 COLUMNS = 256
 
 daub_coeffs = (
@@ -93,18 +92,25 @@
     return where_equal((row % size_a) * size_b + row // size_a, column).astype(jnp.bfloat16)
 
 
-def accumulate(patch_ref, beam_ref, table, dec_back, ra_out, total):
+def accumulate(facet_ref, tile_ref, beam_ref, table, dec_back, ra_out, total, group):
     dec_rows = total.shape[1]
-    for m in range(0, dec_back.shape[0], CHUNK):
-        patches = dot(dec_back[m : m + CHUNK], ra_out[...])
-        for i in range(CHUNK // dec_rows):
-            p = m // dec_rows + i
-            patch = patches[i * dec_rows : (i + 1) * dec_rows]
-            patch_grad = (table[beam_ref[p]].astype(jnp.float32) * patch).astype(jnp.bfloat16).astype(jnp.float32)
-            total[patch_ref[p]] = total[patch_ref[p]] + patch_grad
-
-
-def write_sums(total, me_ref, outs):
+    patches = dot(dec_back[group * GROUP * dec_rows : (group + 1) * GROUP * dec_rows], ra_out[...])
+    for i in range(GROUP):
+        p = group * GROUP + i
+        patch = patches[i * dec_rows : (i + 1) * dec_rows]
+        patch_grad = (table[beam_ref[p]].astype(jnp.float32) * patch).astype(jnp.bfloat16).astype(jnp.float32)
+        tile = 2 * facet_ref[p] + tile_ref[p]
+        total[tile] = total[tile] + patch_grad
+
+
+def run_steps(groups, steps):
+    for turn in range(groups + 2*len(steps) - 2):
+        for behind, step in reversed(list(enumerate(steps))):
+            if 0 <= turn - 2*behind < groups:
+                step(turn - 2*behind)
+
+
+def write_sums(total, me_ref, outs, channel):
     tiles, dec_rows, width = total.shape
     from_left = iota((dec_rows, width), 1) % SPAN >= SPAN // 2
     paired = me_ref is not None
@@ -114,9 +120,9 @@
             facet = (2 * index + side) ^ me_ref[0] if paired else index
             own = 2 * facet
             left, right = lax.rem(own + tiles - 1, tiles), lax.rem(own + 2, tiles)
-            out_ref[index, 0, 0] = total[own].astype(out_ref.dtype)
-            out_ref[index, 1, 0] = total[own + 1].astype(out_ref.dtype)
-            out_ref[index, 2, 0] = jnp.where(from_left, total[left], total[right]).astype(out_ref.dtype)
+            out_ref[index, 0, channel] = total[own].astype(out_ref.dtype)
+            out_ref[index, 1, channel] = total[own + 1].astype(out_ref.dtype)
+            out_ref[index, 2, channel] = jnp.where(from_left, total[left], total[right]).astype(out_ref.dtype)
         return carry
 
     lax.fori_loop(0, outs[0].shape[0], one_facet, 0, unroll=4)
@@ -139,120 +145,141 @@
     return data.reshape(-1, data.shape[-1])
 
 
-def blocks(owned, samples):
-    groups = owned // GROUP
-    for group in range(groups):
-        for k in range(0, samples, COLUMNS):
-            yield group, slice(k, k + COLUMNS)
-
-
-def first_gradient_kernel(paired, patch_ref, beam_ref, *refs):
+def column_blocks(samples):
+    return [slice(k, k + COLUMNS) for k in range(0, samples, COLUMNS)]
+
+
+def first_gradient_kernel(paired, facet_ref, tile_ref, beam_ref, *refs):
     me_ref, refs = (refs[0], refs[1:]) if paired else (None, refs)
-    vis_ref, beams_ref, m_ra_ref, m_dec_ref, *refs = refs
-    outs, refs = refs[: 1 + paired], refs[1 + paired :]
-    table, back, forward, ra_out, ra_in, total, dec_back, swap, order, held, arrived = refs
-    channel = pl.program_id(0)
+    vis_ref, *small_refs = refs[:4]
+    outs, refs = refs[4 : 5 + paired], refs[5 + paired :]
+    table, back, forward, ra_out, ra_in, total, dec_back, swap, order, beams, m_ra, m_dec, held, arrived, came = refs
     channels, dec_rows, owned, samples = held.shape
-    width = m_ra_ref.shape[0]
-    beam_count = beams_ref.shape[2]
+    width = m_ra.shape[0]
+    beam_count = beams.shape[2]
     size = GROUP * dec_rows
-
-    @pl.when(channel == 0)
-    def _():
-        vis_copy(vis_ref, held, arrived, 0).start()
-        back[...] = back_matrix(m_dec_ref[...])
-        forward[...] = forward_matrix(m_dec_ref[...])
-        order[...] = phase_rows(width)
-        swap[...] = swap_rows(dec_rows, beam_count)
-        ra_out[...] = dot(m_ra_ref[...], order[...], ((0,), (1,))).astype(jnp.bfloat16)
-        ra_in[...] = dot(order[...], m_ra_ref[...]).astype(jnp.bfloat16)
-
-    swapped = dot(swap[...], beams_ref[0].reshape(dec_rows * beam_count, width)).astype(jnp.bfloat16)
-    ordered = dot(swapped, order[...], ((1,), (1,))).astype(jnp.bfloat16)
-    table[0] = ordered.reshape(beam_count, dec_rows, width)
-    total[...] = jnp.zeros_like(total)
-    wait_and_start_next(vis_ref, held, arrived, channel)
-    for group, columns in blocks(owned, samples):
-        rows = slice(group * size, (group + 1) * size)
-        dec_back[rows, columns] = dot(back[...], group_data(held, channel, group, columns)).astype(jnp.bfloat16)
-    accumulate(patch_ref, beam_ref, table.at[0], dec_back, ra_out, total)
-    write_sums(total, me_ref, outs)
-
-
-def second_gradient_kernel(paired, patch_ref, beam_ref, slot_ref, *refs):
+    copies = [
+        pltpu.make_async_copy(source, target, came.at[index])
+        for index, (source, target) in enumerate(zip(small_refs, (beams, m_ra, m_dec)))
+    ]
+    for copy in reversed(copies):
+        copy.start()
+    vis_copy(vis_ref, held, arrived, 0).start()
+    order[...] = phase_rows(width)
+    swap[...] = swap_rows(dec_rows, beam_count)
+    for copy in copies:
+        copy.wait()
+    back[...] = back_matrix(m_dec[...])
+    forward[...] = forward_matrix(m_dec[...])
+    ra_out[...] = dot(m_ra[...], order[...], ((0,), (1,))).astype(jnp.bfloat16)
+    ra_in[...] = dot(order[...], m_ra[...]).astype(jnp.bfloat16)
+
+    def one_channel(channel, carry):
+        swapped = dot(swap[...], beams[channel].reshape(dec_rows * beam_count, width)).astype(jnp.bfloat16)
+        ordered = dot(swapped, order[...], ((1,), (1,))).astype(jnp.bfloat16)
+        table[channel] = ordered.reshape(beam_count, dec_rows, width)
+        total[...] = jnp.zeros_like(total)
+        wait_and_start_next(vis_ref, held, arrived, channel)
+
+        def go_back(group):
+            rows = slice(group * size, (group + 1) * size)
+            for columns in column_blocks(samples):
+                data = group_data(held, channel, group, columns)
+                dec_back[rows, columns] = dot(back[...], data).astype(jnp.bfloat16)
+
+        gather = functools.partial(
+            accumulate, facet_ref, tile_ref, beam_ref, table.at[channel], dec_back, ra_out, total
+        )
+        run_steps(owned // GROUP, [go_back, gather])
+        write_sums(total, me_ref, outs, channel)
+        return carry
+
+    lax.fori_loop(0, channels, one_channel, 0)
+
+
+def second_gradient_kernel(paired, facet_ref, tile_ref, beam_ref, *refs):
     me_ref, refs = (refs[0], refs[1:]) if paired else (None, refs)
     vis_ref, table, back, forward, ra_out, ra_in, tiles_ref, *refs = refs
     outs, refs = refs[: 1 + paired], refs[1 + paired :]
-    total, rows_k, weighted, held, arrived = refs
-    channel = pl.program_id(0)
+    total, rows_k, held, arrived = refs
     channels, dec_rows, owned, samples = held.shape
     size = GROUP * dec_rows
-
-    @pl.when(channel == 0)
-    def _():
-        vis_copy(vis_ref, held, arrived, 0).start()
-
-    total[...] = jnp.zeros_like(total)
-    for p in range(owned):
-        weighted[p * dec_rows : (p + 1) * dec_rows] = (
-            table[0, beam_ref[p]].astype(jnp.float32)
-            * tiles_ref[slot_ref[p] * channels + channel].astype(jnp.float32)
-        ).astype(jnp.bfloat16)
-    for m in range(0, owned * dec_rows, CHUNK):
-        rows_k[m : m + CHUNK] = dot(weighted[m : m + CHUNK], ra_in[...]).astype(jnp.bfloat16)
-    wait_and_start_next(vis_ref, held, arrived, channel)
-    for group, columns in blocks(owned, samples):
-        rows = slice(group * size, (group + 1) * size)
-        predicted = dot(forward[...], rows_k[rows, columns])
-        data = group_data(held, channel, group, columns).astype(jnp.float32)
-        rows_k[rows, columns] = (predicted - data).astype(jnp.bfloat16)
-    for group, columns in blocks(owned, samples):
-        rows = slice(group * size, (group + 1) * size)
-        rows_k[rows, columns] = dot(back[...], rows_k[rows, columns]).astype(jnp.bfloat16)
-    accumulate(patch_ref, beam_ref, table.at[0], rows_k, ra_out, total)
-    write_sums(total, me_ref, outs)
+    vis_copy(vis_ref, held, arrived, 0).start()
+
+    def one_channel(channel, carry):
+        total[...] = jnp.zeros_like(total)
+
+        def go_in(group):
+            weighted = []
+            for p in range(group * GROUP, (group + 1) * GROUP):
+                facet = facet_ref[p] ^ me_ref[0] if paired else facet_ref[p]
+                tile = tiles_ref[(2 * facet + tile_ref[p]) * channels + channel].astype(jnp.float32)
+                weighted.append((table[channel, beam_ref[p]].astype(jnp.float32) * tile).astype(jnp.bfloat16))
+            weighted = jnp.concatenate(weighted, axis=0)
+            for columns in column_blocks(samples):
+                along = dot(weighted, ra_in[:, columns]).astype(jnp.bfloat16)
+                rows_k[group * size : (group + 1) * size, columns] = along
+
+        def go_forward(group):
+            if group == 0:
+                wait_and_start_next(vis_ref, held, arrived, channel)
+            rows = slice(group * size, (group + 1) * size)
+            for columns in column_blocks(samples):
+                predicted = dot(forward[...], rows_k[rows, columns])
+                data = group_data(held, channel, group, columns).astype(jnp.float32)
+                rows_k[rows, columns] = (predicted - data).astype(jnp.bfloat16)
+
+        def go_back(group):
+            rows = slice(group * size, (group + 1) * size)
+            for columns in column_blocks(samples):
+                rows_k[rows, columns] = dot(back[...], rows_k[rows, columns]).astype(jnp.bfloat16)
+
+        gather = functools.partial(
+            accumulate, facet_ref, tile_ref, beam_ref, table.at[channel], rows_k, ra_out, total
+        )
+        run_steps(owned // GROUP, [go_in, go_forward, go_back, gather])
+        write_sums(total, me_ref, outs, channel)
+        return carry
+
+    lax.fori_loop(0, channels, one_channel, 0)
 
 
 def gradient_call(scalars, vis, operands, facets, paired, second):
     channels, dec_rows, owned, samples = vis.shape
     width = LANES
-    beam_count = operands[0].shape[2] if not second else operands[0].shape[1]
     size = GROUP * dec_rows
-    whole = lambda shape: pl.BlockSpec(shape, lambda c, *_: (0,) * len(shape))
-    channel_block = lambda *shape: pl.BlockSpec((1,) + shape, lambda c, *_: (c,) + (0,) * len(shape))
-    kept, sum_type = (facets // 2, jnp.float32) if paired else (facets, jnp.bfloat16)
+    bf16 = jnp.bfloat16
+    vmem, hbm = pl.BlockSpec(memory_space=pltpu.VMEM), pl.BlockSpec(memory_space=pltpu.HBM)
+    kept, sum_type = (facets // 2, jnp.float32) if paired else (facets, bf16)
     out_shapes = [jax.ShapeDtypeStruct((kept, SLOTS, channels, dec_rows, width), sum_type)] * (1 + paired)
-    out_specs = [pl.BlockSpec((kept, SLOTS, 1, dec_rows, width), lambda c, *_: (0, 0, c, 0, 0))] * (1 + paired)
-    in_specs = [pl.BlockSpec(memory_space=pltpu.HBM)]
-    in_specs.append(channel_block(*operands[0].shape[1:]))
-    if not second:
-        shared = [(size, size), (size, size), (samples, width), (width, samples)]
-        out_shapes.append(jax.ShapeDtypeStruct((channels, beam_count, dec_rows, width), jnp.bfloat16))
-        out_specs.append(channel_block(beam_count, dec_rows, width))
-        out_shapes += [jax.ShapeDtypeStruct(shape, jnp.bfloat16) for shape in shared]
-        out_specs += [whole(shape) for shape in shared]
-    in_specs += [whole(operand.shape) for operand in operands[1:]]
     scratch = [
         pltpu.VMEM((2 * facets, dec_rows, width), jnp.float32),
-        pltpu.VMEM((owned * dec_rows, samples), jnp.bfloat16),
+        pltpu.VMEM((owned * dec_rows, samples), bf16),
     ]
     if second:
-        scratch.append(pltpu.VMEM((owned * dec_rows, width), jnp.bfloat16))
+        in_specs = [hbm] + [vmem] * len(operands)
     else:
-        scratch += [pltpu.VMEM((size, size), jnp.bfloat16), pltpu.VMEM((width, width), jnp.bfloat16)]
-    scratch += [pltpu.VMEM(vis.shape, jnp.bfloat16), pltpu.SemaphoreType.DMA((channels,))]
+        in_specs = [hbm] * (1 + len(operands))
+        beam_count = operands[0].shape[2]
+        shared = [(channels, beam_count, dec_rows, width), (size, size), (size, size), (samples, width), (width, samples)]
+        out_shapes += [jax.ShapeDtypeStruct(shape, bf16) for shape in shared]
+        scratch += [pltpu.VMEM((size, size), bf16), pltpu.VMEM((width, width), bf16)]
+        scratch += [pltpu.VMEM(operand.shape, bf16) for operand in operands]
+    scratch += [pltpu.VMEM(vis.shape, bf16), pltpu.SemaphoreType.DMA((channels,))]
+    if not second:
+        scratch.append(pltpu.SemaphoreType.DMA((len(operands),)))
     work = channels * owned * samples * dec_rows
     return pl.pallas_call(
         functools.partial(second_gradient_kernel if second else first_gradient_kernel, paired),
         out_shape=out_shapes,
         grid_spec=pltpu.PrefetchScalarGridSpec(
             num_scalar_prefetch=len(scalars),
-            grid=(channels,),
+            grid=(),
             in_specs=in_specs,
-            out_specs=out_specs,
+            out_specs=[vmem] * len(out_shapes),
             scratch_shapes=scratch,
         ),
-        compiler_params=pltpu.CompilerParams(vmem_limit_bytes=48 << 20),
+        compiler_params=pltpu.CompilerParams(vmem_limit_bytes=40 << 20),
         cost_estimate=pl.CostEstimate(
             flops=(4 if second else 2) * 256 * work, bytes_accessed=2 * work, transcendentals=0
         ),
@@ -481,6 +508,14 @@
         start += part_ref.shape[0]
 
 
+def weave_kernel(rows, *refs):
+    *parts, out_ref = refs
+    for index in range(parts[0].shape[0] // rows):
+        for side, part_ref in enumerate(parts):
+            start = (2 * index + side) * rows
+            out_ref[start : start + rows] = part_ref[index * rows : (index + 1) * rows]
+
+
 def small_call(kernel, name, out_shape, *operands):
     vmem = pl.BlockSpec(memory_space=pltpu.VMEM)
     return pl.pallas_call(
@@ -514,10 +549,12 @@
 
 
 def pair_gather(tiles):
+    rows = tiles.shape[0]
     tiles = join(tiles, across(tiles, 2))
     far = [across(tiles, difference) for difference in (12, 8, 4)]
     tiles = join(tiles, *reversed(far))
-    return join(tiles, across(tiles, 1))
+    shape = jax.ShapeDtypeStruct((2 * tiles.shape[0],) + tiles.shape[1:], tiles.dtype)
+    return small_call(functools.partial(weave_kernel, rows), "weave", shape, tiles, across(tiles, 1))
 
 
 def local(vis, beams, m_ra, m_dec, facet_of, tile_of, beam_of, step_size, thresholds):
@@ -525,29 +562,26 @@
     channels, dec_rows, owned, samples = vis.shape
     width = m_ra.shape[0]
     per_facet = RA_DEV // width
-    beams, m_ra, m_dec, beam_of = (
-        pltpu.with_memory_space_constraint(x, pltpu.HBM) for x in (beams, m_ra, m_dec, beam_of)
-    )
-    patch_of = facet_of[:, 0] * per_facet + tile_of
+    facet_of = facet_of.reshape(owned)
+    held = [vis, beams, m_ra, m_dec, facet_of, tile_of, beam_of]
+    held = [pltpu.with_memory_space_constraint(array, pltpu.HBM) for array in held]
+    vis, beams, m_ra, m_dec, facet_of, tile_of, beam_of = held
     paired = facets == 16
     if paired:
-        me = lax.axis_index("ra").astype(jnp.int32)
-        apart = facet_of[:, 0] ^ me
-        slot_of = ((apart & 1) * (facets // 2) + (apart >> 1)) * per_facet + tile_of
-        me = me.reshape(1)
+        base = [lax.axis_index("ra").astype(jnp.int32).reshape(1)]
         exchange, gather = pair_exchange, pair_gather
     else:
-        me, slot_of = None, patch_of
+        base = []
         exchange = lambda sums: [lax.all_to_all(sums, "ra", split_axis=0, concat_axis=0, tiled=True)]
         gather = lambda tiles: lax.all_gather(tiles, "ra", axis=0, tiled=True)
 
-    base = [me] if paired else []
+    scalars = [facet_of, tile_of, beam_of] + base
     sent = 1 + paired
-    sums = gradient_call([patch_of, beam_of] + base, vis, [beams, m_ra, m_dec], facets, paired, False)
+    sums = gradient_call(scalars, vis, [beams, m_ra, m_dec], facets, paired, False)
     sums, shared = sums[:sent], sums[sent:]
     first, tiles = prox_call(exchange(*sums), thresholds, step_size, dec_rows)
     tiles = gather(tiles).reshape(facets * per_facet * channels, dec_rows, width)
-    sums = gradient_call([patch_of, beam_of, slot_of] + base, vis, [*shared, tiles], facets, paired, True)
+    sums = gradient_call(scalars, vis, [*shared, tiles], facets, paired, True)
     return prox_call(exchange(*sums), thresholds, step_size, dec_rows, first)
 
 

time: 79.5 us -> 77.5 us (0.975)
  Pallas kernels: 29.2 us -> 27.8 us
    pallas_call x2, Pallas kernels: 23.6 us -> 22.4 us  [gradient_call(): pl.pallas_call(functools.partial(second_gradient_kernel if second else fi...]
where the time goes in v5:
time: 77.5 us; the launch traced here: 77.3 us
  starting transfers between devices  29.8 us (38%)
  Pallas kernels  27.8 us (36%)
  waiting for transfers between devices  19.6 us (25%)
    ppermute x21, starting transfers between devices, across(): lax.ppermute(value, 'ra', [(source, source ^ difference) for source in ra...  29.8 us
    pallas_call x2, Pallas kernels, gradient_call(): pl.pallas_call(functools.partial(second_gradient_kernel if second else fi...  22.4 us
    ppermute x21, waiting for transfers between devices, across(): lax.ppermute(value, 'ra', [(source, source ^ difference) for source in ra...  19.6 us
    pallas_call x2, Pallas kernels, prox_call(): pl.pallas_call(functools.partial(prox_kernel, second, len(received)), out...  5.28 us
  transfers between devices with their start and end apart: 21, of which 14 were waited for; matrix products, arithmetic and copies ran while one was open for 0% of the time, Pallas kernels for 0%

profile of v5, /device:TPU:0, one launch (start us, length us, event | category | flops | bytes accessed | tf_op | source)
XLA Modules:
  0.0 77.3 jit_solution(13260683654610631134)
XLA Ops:
  0.0 9.3 %first_gradient.1 = (f32[8,3,4,16,128]{4,3,2,1,0:T(8,128)S(1)}, f32[8,3,4,16,128]{4,3,2,1,0:T(8,128)S(1)}, bf16[4,16,16,128]{3,2,1,0:T(8,128)(2,1)S(1)}, bf16[25...) custom-call(s32[128]{0:T(128)} %bitcast.36, ...), custom_call_target="tpu_custom_call" | custom-call | flops 2147483648 | bytes 8388608 | tf_op jit(solution)/shard_map/first_gradient/pallas_call | solution.py:272
  9.3 0.5 collective-permute-start
  9.8 1.9 %collective-permute-done.got_ref = f32[8,3,4,16,128]{4,3,2,1,0:T(8,128)S(1)} collective-permute-done((f32[8,3,4,16,128]{4,3,2,1,0:T(8,128)S(1)}, f32[8,3,4,16,128]{4,3,2,1,0:T(8,128)S(1)}, u32[]{:S(2)}, u32[]{:S(2)}) %collective-permute-start) | collective-permute-done | bytes 786464 | tf_op jit(solution)/shard_map/ppermute | solution.py:539
  11.8 6.0 %collective-permute-start.1 = (bf16[1,3,4,16,128]{4,3,2,1,0:T(8,128)(2,1)S(1)}, bf16[1,3,4,16,128]{4,3,2,1,0:T(8,128)(2,1)S(1)}, u32[]{:S(2)}, u32[]{:S(2)}) collective-permute-start(bf16[1,3,4,16,128]{4,3,2,1,0:T(8,128)(2,1)S(1)} %get-tuple-element.40), channel_id=1, source_target_pairs={{0,14},{1,15},{2,12},{3,13},{4,10},{5,11},{6,8},{7,9},{8,6},{9,7},... | collective-permute-start | bytes 147464 | tf_op jit(solution)/shard_map/ppermute | solution.py:539
  18.0 0.7 collective-permute-start.3
  18.7 2.1 %collective-permute-start.4 = (bf16[1,3,4,16,128]{4,3,2,1,0:T(8,128)(2,1)S(1)}, bf16[1,3,4,16,128]{4,3,2,1,0:T(8,128)(2,1)S(1)}, u32[]{:S(2)}, u32[]{:S(2)}) collective-permute-start(bf16[1,3,4,16,128]{4,3,2,1,0:T(8,128)(2,1)S(1)} %get-tuple-element.43), channel_id=1, source_target_pairs={{0,8},{1,9},{2,10},{3,11},{4,12},{5,13},{6,14},{7,15},{8,0},{9,1},... | collective-permute-start | bytes 147464 | tf_op jit(solution)/shard_map/ppermute | solution.py:539
  20.8 2.3 %collective-permute-start.5 = (bf16[1,3,4,16,128]{4,3,2,1,0:T(8,128)(2,1)S(1)}, bf16[1,3,4,16,128]{4,3,2,1,0:T(8,128)(2,1)S(1)}, u32[]{:S(2)}, u32[]{:S(2)}) collective-permute-start(bf16[1,3,4,16,128]{4,3,2,1,0:T(8,128)(2,1)S(1)} %get-tuple-element.44), channel_id=1, source_target_pairs={{0,6},{1,7},{2,4},{3,5},{4,2},{5,3},{6,0},{7,1},{8,14},{9,15},{10,... | collective-permute-start | bytes 147464 | tf_op jit(solution)/shard_map/ppermute | solution.py:539
  23.1 0.8 collective-permute-start.6
  23.9 0.4 collective-permute-start.7
  24.3 1.0 %collective-permute-done.3 = bf16[1,3,4,16,128]{4,3,2,1,0:T(8,128)(2,1)S(1)} collective-permute-done((bf16[1,3,4,16,128]{4,3,2,1,0:T(8,128)(2,1)S(1)}, bf16[1,3,4,16,128]{4,3,2,1,0:T(8,128)(2,1)S(1)}, u32[]{:S(2)}, u32[]{:S(2)}) %collective-permute-start.3) | collective-permute-done | bytes 49184 | tf_op jit(solution)/shard_map/ppermute | solution.py:539
  25.3 1.4 %collective-permute-done.4 = bf16[1,3,4,16,128]{4,3,2,1,0:T(8,128)(2,1)S(1)} collective-permute-done((bf16[1,3,4,16,128]{4,3,2,1,0:T(8,128)(2,1)S(1)}, bf16[1,3,4,16,128]{4,3,2,1,0:T(8,128)(2,1)S(1)}, u32[]{:S(2)}, u32[]{:S(2)}) %collective-permute-start.4) | collective-permute-done | bytes 49184 | tf_op jit(solution)/shard_map/ppermute | solution.py:539
  26.7 0.6 collective-permute-done.5
  27.5 0.5 collective-permute-done.7
  28.0 2.6 %first_prox.1 = (f32[2,16,8,128]{3,2,1,0:T(8,128)S(1)}, bf16[128,128]{1,0:T(8,128)(2,1)S(1)}) custom-call(f32[1,192,128]{2,1,0:T(8,128)S(1)} %bitcast.20, bf16[1,192,128]{2,1,0:T(8,128)(2,1)S(1)} %bitcast.29, bf16[1,192,128]{2,1,0:T(8,128)(2,1)S(1)} %bitcast.30, bf16[1,192,128]{2,1,0:T(8,128)(2,1)S(1)} %bitcast.31, bf16[1,192,128]{2,1,0:T(8,128)(2,1)S(1)} %bitcast.32, ...), custom_call_target="tpu_custom_call" | custom-call | tf_op jit(solution)/shard_map/first_prox/pallas_call | solution.py:482
  30.6 0.9 %collective-permute-start.8 = (bf16[128,128]{1,0:T(8,128)(2,1)S(1)}, bf16[128,128]{1,0:T(8,128)(2,1)S(1)}, u32[]{:S(2)}, u32[]{:S(2)}) collective-permute-start(bf16[128,128]{1,0:T(8,128)(2,1)S(1)} %get-tuple-element.47.refs_0_), channel_id=1, source_target_pairs={{0,2},{1,3},{2,0},{3,1},{4,6},{5,7},{6,4},{7,5},{8,10},{9,11},{10,... | collective-permute-start | bytes 98312 | tf_op jit(solution)/shard_map/ppermute | solution.py:539
  31.5 3.1 %collective-permute-done.8.refs_1_ = bf16[128,128]{1,0:T(8,128)(2,1)S(1)} collective-permute-done((bf16[128,128]{1,0:T(8,128)(2,1)S(1)}, bf16[128,128]{1,0:T(8,128)(2,1)S(1)}, u32[]{:S(2)}, u32[]{:S(2)}) %collective-permute-start.8) | collective-permute-done | bytes 32800 | tf_op jit(solution)/shard_map/ppermute | solution.py:539
  34.5 3.6 %collective-permute-start.11 = (bf16[256,128]{1,0:T(8,128)(2,1)S(1)}, bf16[256,128]{1,0:T(8,128)(2,1)S(1)}, u32[]{:S(2)}, u32[]{:S(2)}) collective-permute-start(bf16[256,128]{1,0:T(8,128)(2,1)S(1)} %join.2.refs_0_), channel_id=1, source_target_pairs={{0,12},{1,13},{2,14},{3,15},{4,8},{5,9},{6,10},{7,11},{8,4},{9,5},... | collective-permute-start | bytes 196616 | tf_op jit(solution)/shard_map/ppermute | solution.py:539
  38.2 0.8 collective-permute-start.9
  38.9 1.8 %collective-permute-done.11.refs_3_ = bf16[256,128]{1,0:T(8,128)(2,1)S(1)} collective-permute-done((bf16[256,128]{1,0:T(8,128)(2,1)S(1)}, bf16[256,128]{1,0:T(8,128)(2,1)S(1)}, u32[]{:S(2)}, u32[]{:S(2)}) %collective-permute-start.11) | collective-permute-done | bytes 65568 | tf_op jit(solution)/shard_map/ppermute | solution.py:539
  40.7 2.6 %collective-permute-done.10.refs_2_ = bf16[256,128]{1,0:T(8,128)(2,1)S(1)} collective-permute-done((bf16[256,128]{1,0:T(8,128)(2,1)S(1)}, bf16[256,128]{1,0:T(8,128)(2,1)S(1)}, u32[]{:S(2)}, u32[]{:S(2)}) %collective-permute-start.10) | collective-permute-done | bytes 65568 | tf_op jit(solution)/shard_map/ppermute | solution.py:539
  43.4 1.5 %collective-permute-done.12.refs_1_ = bf16[1024,128]{1,0:T(8,128)(2,1)S(1)} collective-permute-done((bf16[1024,128]{1,0:T(8,128)(2,1)S(1)}, bf16[1024,128]{1,0:T(8,128)(2,1)S(1)}, u32[]{:S(2)}, u32[]{:S(2)}) %collective-permute-start.12) | collective-permute-done | bytes 262176 | tf_op jit(solution)/shard_map/ppermute | solution.py:539
  45.0 13.1 %second_gradient.1 = (f32[8,3,4,16,128]{4,3,2,1,0:T(8,128)S(1)}, f32[8,3,4,16,128]{4,3,2,1,0:T(8,128)S(1)}) custom-call(s32[128]{0:T(128)} %bitcast.37, s32[128]{0:T(128)} %tile_ref.3, s32[128]{0:T(128)} %beam_ref.3, s32[1]{0:T(128)} %bitcast.1.refs_0_, bf16[4,16,128,512]{3,2,1,0:T(8,128)(2,1)} %refs_1_.3, ...), custom_call_target="tpu_custom_call" | custom-call | flops 4294967296 | bytes 8388608 | tf_op jit(solution)/shard_map/second_gradient/pallas_call | solution.py:272
  58.3 2.1 %collective-permute-done.13.got_ref = f32[8,3,4,16,128]{4,3,2,1,0:T(8,128)S(1)} collective-permute-done((f32[8,3,4,16,128]{4,3,2,1,0:T(8,128)S(1)}, f32[8,3,4,16,128]{4,3,2,1,0:T(8,128)S(1)}, u32[]{:S(2)}, u32[]{:S(2)}) %collective-permute-start.13) | collective-permute-done | bytes 786464 | tf_op jit(solution)/shard_map/ppermute | solution.py:539
  60.5 2.0 %collective-permute-start.14 = (bf16[1,3,4,16,128]{4,3,2,1,0:T(8,128)(2,1)S(1)}, bf16[1,3,4,16,128]{4,3,2,1,0:T(8,128)(2,1)S(1)}, u32[]{:S(2)}, u32[]{:S(2)}) collective-permute-start(bf16[1,3,4,16,128]{4,3,2,1,0:T(8,128)(2,1)S(1)} %get-tuple-element.51), channel_id=1, source_target_pairs={{0,14},{1,15},{2,12},{3,13},{4,10},{5,11},{6,8},{7,9},{8,6},{9,7},... | collective-permute-start | bytes 147464 | tf_op jit(solution)/shard_map/ppermute | solution.py:539
  62.5 1.8 %collective-permute-start.15 = (bf16[1,3,4,16,128]{4,3,2,1,0:T(8,128)(2,1)S(1)}, bf16[1,3,4,16,128]{4,3,2,1,0:T(8,128)(2,1)S(1)}, u32[]{:S(2)}, u32[]{:S(2)}) collective-permute-start(bf16[1,3,4,16,128]{4,3,2,1,0:T(8,128)(2,1)S(1)} %get-tuple-element.52), channel_id=1, source_target_pairs={{0,12},{1,13},{2,14},{3,15},{4,8},{5,9},{6,10},{7,11},{8,4},{9,5},... | collective-permute-start | bytes 147464 | tf_op jit(solution)/shard_map/ppermute | solution.py:539
  64.3 1.1 %collective-permute-start.16 = (bf16[1,3,4,16,128]{4,3,2,1,0:T(8,128)(2,1)S(1)}, bf16[1,3,4,16,128]{4,3,2,1,0:T(8,128)(2,1)S(1)}, u32[]{:S(2)}, u32[]{:S(2)}) collective-permute-start(bf16[1,3,4,16,128]{4,3,2,1,0:T(8,128)(2,1)S(1)} %get-tuple-element.53), channel_id=1, source_target_pairs={{0,10},{1,11},{2,8},{3,9},{4,14},{5,15},{6,12},{7,13},{8,2},{9,3},... | collective-permute-start | bytes 147464 | tf_op jit(solution)/shard_map/ppermute | solution.py:539
  65.5 2.8 %collective-permute-start.17 = (bf16[1,3,4,16,128]{4,3,2,1,0:T(8,128)(2,1)S(1)}, bf16[1,3,4,16,128]{4,3,2,1,0:T(8,128)(2,1)S(1)}, u32[]{:S(2)}, u32[]{:S(2)}) collective-permute-start(bf16[1,3,4,16,128]{4,3,2,1,0:T(8,128)(2,1)S(1)} %get-tuple-element.54), channel_id=1, source_target_pairs={{0,8},{1,9},{2,10},{3,11},{4,12},{5,13},{6,14},{7,15},{8,0},{9,1},... | collective-permute-start | bytes 147464 | tf_op jit(solution)/shard_map/ppermute | solution.py:539
  68.2 1.9 %collective-permute-start.19 = (bf16[1,3,4,16,128]{4,3,2,1,0:T(8,128)(2,1)S(1)}, bf16[1,3,4,16,128]{4,3,2,1,0:T(8,128)(2,1)S(1)}, u32[]{:S(2)}, u32[]{:S(2)}) collective-permute-start(bf16[1,3,4,16,128]{4,3,2,1,0:T(8,128)(2,1)S(1)} %get-tuple-element.56), channel_id=1, source_target_pairs={{0,4},{1,5},{2,6},{3,7},{4,0},{5,1},{6,2},{7,3},{8,12},{9,13},{10,... | collective-permute-start | bytes 147464 | tf_op jit(solution)/shard_map/ppermute | solution.py:539
  70.2 1.5 %collective-permute-start.20 = (bf16[1,3,4,16,128]{4,3,2,1,0:T(8,128)(2,1)S(1)}, bf16[1,3,4,16,128]{4,3,2,1,0:T(8,128)(2,1)S(1)}, u32[]{:S(2)}, u32[]{:S(2)}) collective-permute-start(bf16[1,3,4,16,128]{4,3,2,1,0:T(8,128)(2,1)S(1)} %get-tuple-element.57), channel_id=1, source_target_pairs={{0,2},{1,3},{2,0},{3,1},{4,6},{5,7},{6,4},{7,5},{8,10},{9,11},{10,... | collective-permute-start | bytes 147464 | tf_op jit(solution)/shard_map/ppermute | solution.py:539
  71.7 0.9 %collective-permute-done.16 = bf16[1,3,4,16,128]{4,3,2,1,0:T(8,128)(2,1)S(1)} collective-permute-done((bf16[1,3,4,16,128]{4,3,2,1,0:T(8,128)(2,1)S(1)}, bf16[1,3,4,16,128]{4,3,2,1,0:T(8,128)(2,1)S(1)}, u32[]{:S(2)}, u32[]{:S(2)}) %collective-permute-start.16) | collective-permute-done | bytes 49184 | tf_op jit(solution)/shard_map/ppermute | solution.py:539
  72.7 1.6 %collective-permute-done.18 = bf16[1,3,4,16,128]{4,3,2,1,0:T(8,128)(2,1)S(1)} collective-permute-done((bf16[1,3,4,16,128]{4,3,2,1,0:T(8,128)(2,1)S(1)}, bf16[1,3,4,16,128]{4,3,2,1,0:T(8,128)(2,1)S(1)}, u32[]{:S(2)}, u32[]{:S(2)}) %collective-permute-start.18) | collective-permute-done | bytes 49184 | tf_op jit(solution)/shard_map/ppermute | solution.py:539
  74.6 2.7 %second_prox.1 = f32[4,16,256]{2,1,0:T(8,128)} custom-call(f32[1,192,128]{2,1,0:T(8,128)S(1)} %bitcast.21, bf16[1,192,128]{2,1,0:T(8,128)(2,1)S(1)} %bitcast.22, bf16[1,192,128]{2,1,0:T(8,128)(2,1)S(1)} %bitcast.23, bf16[1,192,128]{2,1,0:T(8,128)(2,1)S(1)} %bitcast.24, bf16[1,192,128]{2,1,0:T(8,128)(2,1)S(1)} %bitcast.25, bf16[1,192,128]{2,1,0:T(8,128)(2,1)S(1)} %bitcast.26, ...), custom_call_target="tpu_custom_call" | custom-call | tf_op jit(solution)/shard_map/second_prox/pallas_call | solution.py:482
  (23 shorter events, 1.3 us)
Async XLA Ops:
  0.0 28.0 %copy-start = (f32[4,4]{1,0:T(4,128)S(1)}, f32[4,4]{1,0:T(4,128)}, u32[]{:S(2)}) copy-start(f32[4,4]{1,0:T(4,128)} %refs_8_.3) | copy-start | bytes 196
  0.0 28.0 %copy-start.1 = (f32[4]{0:T(128)S(1)}, f32[4]{0:T(128)}, u32[]{:S(2)}) copy-start(f32[4]{0:T(128)} %refs_9_.3) | copy-start | bytes 52
  9.3 2.5 %collective-permute-start = (f32[8,3,4,16,128]{4,3,2,1,0:T(8,128)S(1)}, f32[8,3,4,16,128]{4,3,2,1,0:T(8,128)S(1)}, u32[]{:S(2)}, u32[]{:S(2)}) collective-permute-start(f32[8,3,4,16,128]{4,3,2,1,0:T(8,128)S(1)} %get-tuple-element.38), channel_id=1, source_target_pairs={{0,1},{1,0},{2,3},{3,2},{4,5},{5,4},{6,7},{7,6},{8,9},{9,8},{10,11... | collective-permute-start | bytes 2359304 | tf_op jit(solution)/shard_map/ppermute | solution.py:539
  11.8 11.3 %collective-permute-start.1 = (bf16[1,3,4,16,128]{4,3,2,1,0:T(8,128)(2,1)S(1)}, bf16[1,3,4,16,128]{4,3,2,1,0:T(8,128)(2,1)S(1)}, u32[]{:S(2)}, u32[]{:S(2)}) collective-permute-start(bf16[1,3,4,16,128]{4,3,2,1,0:T(8,128)(2,1)S(1)} %get-tuple-element.40), channel_id=1, source_target_pairs={{0,14},{1,15},{2,12},{3,13},{4,10},{5,11},{6,8},{7,9},{8,6},{9,7},... | collective-permute-start | bytes 147464 | tf_op jit(solution)/shard_map/ppermute | solution.py:539
  17.8 6.1 %collective-permute-start.2 = (bf16[1,3,4,16,128]{4,3,2,1,0:T(8,128)(2,1)S(1)}, bf16[1,3,4,16,128]{4,3,2,1,0:T(8,128)(2,1)S(1)}, u32[]{:S(2)}, u32[]{:S(2)}) collective-permute-start(bf16[1,3,4,16,128]{4,3,2,1,0:T(8,128)(2,1)S(1)} %get-tuple-element.41), channel_id=1, source_target_pairs={{0,12},{1,13},{2,14},{3,15},{4,8},{5,9},{6,10},{7,11},{8,4},{9,5},... | collective-permute-start | bytes 147464 | tf_op jit(solution)/shard_map/ppermute | solution.py:539
  18.0 7.3 %collective-permute-start.3 = (bf16[1,3,4,16,128]{4,3,2,1,0:T(8,128)(2,1)S(1)}, bf16[1,3,4,16,128]{4,3,2,1,0:T(8,128)(2,1)S(1)}, u32[]{:S(2)}, u32[]{:S(2)}) collective-permute-start(bf16[1,3,4,16,128]{4,3,2,1,0:T(8,128)(2,1)S(1)} %get-tuple-element.42), channel_id=1, source_target_pairs={{0,10},{1,11},{2,8},{3,9},{4,14},{5,15},{6,12},{7,13},{8,2},{9,3},... | collective-permute-start | bytes 147464 | tf_op jit(solution)/shard_map/ppermute | solution.py:539
  18.7 7.9 %collective-permute-start.4 = (bf16[1,3,4,16,128]{4,3,2,1,0:T(8,128)(2,1)S(1)}, bf16[1,3,4,16,128]{4,3,2,1,0:T(8,128)(2,1)S(1)}, u32[]{:S(2)}, u32[]{:S(2)}) collective-permute-start(bf16[1,3,4,16,128]{4,3,2,1,0:T(8,128)(2,1)S(1)} %get-tuple-element.43), channel_id=1, source_target_pairs={{0,8},{1,9},{2,10},{3,11},{4,12},{5,13},{6,14},{7,15},{8,0},{9,1},... | collective-permute-start | bytes 147464 | tf_op jit(solution)/shard_map/ppermute | solution.py:539
  20.8 6.4 %collective-permute-start.5 = (bf16[1,3,4,16,128]{4,3,2,1,0:T(8,128)(2,1)S(1)}, bf16[1,3,4,16,128]{4,3,2,1,0:T(8,128)(2,1)S(1)}, u32[]{:S(2)}, u32[]{:S(2)}) collective-permute-start(bf16[1,3,4,16,128]{4,3,2,1,0:T(8,128)(2,1)S(1)} %get-tuple-element.44), channel_id=1, source_target_pairs={{0,6},{1,7},{2,4},{3,5},{4,2},{5,3},{6,0},{7,1},{8,14},{9,15},{10,... | collective-permute-start | bytes 147464 | tf_op jit(solution)/shard_map/ppermute | solution.py:539
  23.1 4.4 %collective-permute-start.6 = (bf16[1,3,4,16,128]{4,3,2,1,0:T(8,128)(2,1)S(1)}, bf16[1,3,4,16,128]{4,3,2,1,0:T(8,128)(2,1)S(1)}, u32[]{:S(2)}, u32[]{:S(2)}) collective-permute-start(bf16[1,3,4,16,128]{4,3,2,1,0:T(8,128)(2,1)S(1)} %get-tuple-element.45), channel_id=1, source_target_pairs={{0,4},{1,5},{2,6},{3,7},{4,0},{5,1},{6,2},{7,3},{8,12},{9,13},{10,... | collective-permute-start | bytes 147464 | tf_op jit(solution)/shard_map/ppermute | solution.py:539
  23.9 4.1 %collective-permute-start.7 = (bf16[1,3,4,16,128]{4,3,2,1,0:T(8,128)(2,1)S(1)}, bf16[1,3,4,16,128]{4,3,2,1,0:T(8,128)(2,1)S(1)}, u32[]{:S(2)}, u32[]{:S(2)}) collective-permute-start(bf16[1,3,4,16,128]{4,3,2,1,0:T(8,128)(2,1)S(1)} %get-tuple-element.46), channel_id=1, source_target_pairs={{0,2},{1,3},{2,0},{3,1},{4,6},{5,7},{6,4},{7,5},{8,10},{9,11},{10,... | collective-permute-start | bytes 147464 | tf_op jit(solution)/shard_map/ppermute | solution.py:539
  30.6 4.0 %collective-permute-start.8 = (bf16[128,128]{1,0:T(8,128)(2,1)S(1)}, bf16[128,128]{1,0:T(8,128)(2,1)S(1)}, u32[]{:S(2)}, u32[]{:S(2)}) collective-permute-start(bf16[128,128]{1,0:T(8,128)(2,1)S(1)} %get-tuple-element.47.refs_0_), channel_id=1, source_target_pairs={{0,2},{1,3},{2,0},{3,1},{4,6},{5,7},{6,4},{7,5},{8,10},{9,11},{10,... | collective-permute-start | bytes 98312 | tf_op jit(solution)/shard_map/ppermute | solution.py:539
  34.5 6.2 %collective-permute-start.11 = (bf16[256,128]{1,0:T(8,128)(2,1)S(1)}, bf16[256,128]{1,0:T(8,128)(2,1)S(1)}, u32[]{:S(2)}, u32[]{:S(2)}) collective-permute-start(bf16[256,128]{1,0:T(8,128)(2,1)S(1)} %join.2.refs_0_), channel_id=1, source_target_pairs={{0,12},{1,13},{2,14},{3,15},{4,8},{5,9},{6,10},{7,11},{8,4},{9,5},... | collective-permute-start | bytes 196616 | tf_op jit(solution)/shard_map/ppermute | solution.py:539
  38.2 5.2 %collective-permute-start.10 = (bf16[256,128]{1,0:T(8,128)(2,1)S(1)}, bf16[256,128]{1,0:T(8,128)(2,1)S(1)}, u32[]{:S(2)}, u32[]{:S(2)}) collective-permute-start(bf16[256,128]{1,0:T(8,128)(2,1)S(1)} %join.2.refs_0_), channel_id=1, source_target_pairs={{0,8},{1,9},{2,10},{3,11},{4,12},{5,13},{6,14},{7,15},{8,0},{9,1},... | collective-permute-start | bytes 196616 | tf_op jit(solution)/shard_map/ppermute | solution.py:539
  38.2 5.2 %collective-permute-start.9 = (bf16[256,128]{1,0:T(8,128)(2,1)S(1)}, bf16[256,128]{1,0:T(8,128)(2,1)S(1)}, u32[]{:S(2)}, u32[]{:S(2)}) collective-permute-start(bf16[256,128]{1,0:T(8,128)(2,1)S(1)} %join.2.refs_0_), channel_id=1, source_target_pairs={{0,4},{1,5},{2,6},{3,7},{4,0},{5,1},{6,2},{7,3},{8,12},{9,13},{10,... | collective-permute-start | bytes 196616 | tf_op jit(solution)/shard_map/ppermute | solution.py:539
  43.3 1.6 %collective-permute-start.12 = (bf16[1024,128]{1,0:T(8,128)(2,1)S(1)}, bf16[1024,128]{1,0:T(8,128)(2,1)S(1)}, u32[]{:S(2)}, u32[]{:S(2)}) collective-permute-start(bf16[1024,128]{1,0:T(8,128)(2,1)S(1)} %join.3.refs_0_), channel_id=1, source_target_pairs={{0,1},{1,0},{2,3},{3,2},{4,5},{5,4},{6,7},{7,6},{8,9},{9,8},{10,11... | collective-permute-start | bytes 786440 | tf_op jit(solution)/shard_map/ppermute | solution.py:539
  58.1 2.4 %collective-permute-start.13 = (f32[8,3,4,16,128]{4,3,2,1,0:T(8,128)S(1)}, f32[8,3,4,16,128]{4,3,2,1,0:T(8,128)S(1)}, u32[]{:S(2)}, u32[]{:S(2)}) collective-permute-start(f32[8,3,4,16,128]{4,3,2,1,0:T(8,128)S(1)} %get-tuple-element.49), channel_id=1, source_target_pairs={{0,1},{1,0},{2,3},{3,2},{4,5},{5,4},{6,7},{7,6},{8,9},{9,8},{10,11... | collective-permute-start | bytes 2359304 | tf_op jit(solution)/shard_map/ppermute | solution.py:539
  60.5 7.7 %collective-permute-start.14 = (bf16[1,3,4,16,128]{4,3,2,1,0:T(8,128)(2,1)S(1)}, bf16[1,3,4,16,128]{4,3,2,1,0:T(8,128)(2,1)S(1)}, u32[]{:S(2)}, u32[]{:S(2)}) collective-permute-start(bf16[1,3,4,16,128]{4,3,2,1,0:T(8,128)(2,1)S(1)} %get-tuple-element.51), channel_id=1, source_target_pairs={{0,14},{1,15},{2,12},{3,13},{4,10},{5,11},{6,8},{7,9},{8,6},{9,7},... | collective-permute-start | bytes 147464 | tf_op jit(solution)/shard_map/ppermute | solution.py:539
  62.5 7.7 %collective-permute-start.15 = (bf16[1,3,4,16,128]{4,3,2,1,0:T(8,128)(2,1)S(1)}, bf16[1,3,4,16,128]{4,3,2,1,0:T(8,128)(2,1)S(1)}, u32[]{:S(2)}, u32[]{:S(2)}) collective-permute-start(bf16[1,3,4,16,128]{4,3,2,1,0:T(8,128)(2,1)S(1)} %get-tuple-element.52), channel_id=1, source_target_pairs={{0,12},{1,13},{2,14},{3,15},{4,8},{5,9},{6,10},{7,11},{8,4},{9,5},... | collective-permute-start | bytes 147464 | tf_op jit(solution)/shard_map/ppermute | solution.py:539
  64.3 8.3 %collective-permute-start.16 = (bf16[1,3,4,16,128]{4,3,2,1,0:T(8,128)(2,1)S(1)}, bf16[1,3,4,16,128]{4,3,2,1,0:T(8,128)(2,1)S(1)}, u32[]{:S(2)}, u32[]{:S(2)}) collective-permute-start(bf16[1,3,4,16,128]{4,3,2,1,0:T(8,128)(2,1)S(1)} %get-tuple-element.53), channel_id=1, source_target_pairs={{0,10},{1,11},{2,8},{3,9},{4,14},{5,15},{6,12},{7,13},{8,2},{9,3},... | collective-permute-start | bytes 147464 | tf_op jit(solution)/shard_map/ppermute | solution.py:539
  65.5 7.2 %collective-permute-start.17 = (bf16[1,3,4,16,128]{4,3,2,1,0:T(8,128)(2,1)S(1)}, bf16[1,3,4,16,128]{4,3,2,1,0:T(8,128)(2,1)S(1)}, u32[]{:S(2)}, u32[]{:S(2)}) collective-permute-start(bf16[1,3,4,16,128]{4,3,2,1,0:T(8,128)(2,1)S(1)} %get-tuple-element.54), channel_id=1, source_target_pairs={{0,8},{1,9},{2,10},{3,11},{4,12},{5,13},{6,14},{7,15},{8,0},{9,1},... | collective-permute-start | bytes 147464 | tf_op jit(solution)/shard_map/ppermute | solution.py:539
  68.2 6.1 %collective-permute-start.18 = (bf16[1,3,4,16,128]{4,3,2,1,0:T(8,128)(2,1)S(1)}, bf16[1,3,4,16,128]{4,3,2,1,0:T(8,128)(2,1)S(1)}, u32[]{:S(2)}, u32[]{:S(2)}) collective-permute-start(bf16[1,3,4,16,128]{4,3,2,1,0:T(8,128)(2,1)S(1)} %get-tuple-element.55), channel_id=1, source_target_pairs={{0,6},{1,7},{2,4},{3,5},{4,2},{5,3},{6,0},{7,1},{8,14},{9,15},{10,... | collective-permute-start | bytes 147464 | tf_op jit(solution)/shard_map/ppermute | solution.py:539
  68.2 6.1 %collective-permute-start.19 = (bf16[1,3,4,16,128]{4,3,2,1,0:T(8,128)(2,1)S(1)}, bf16[1,3,4,16,128]{4,3,2,1,0:T(8,128)(2,1)S(1)}, u32[]{:S(2)}, u32[]{:S(2)}) collective-permute-start(bf16[1,3,4,16,128]{4,3,2,1,0:T(8,128)(2,1)S(1)} %get-tuple-element.56), channel_id=1, source_target_pairs={{0,4},{1,5},{2,6},{3,7},{4,0},{5,1},{6,2},{7,3},{8,12},{9,13},{10,... | collective-permute-start | bytes 147464 | tf_op jit(solution)/shard_map/ppermute | solution.py:539
  70.2 4.4 %collective-permute-start.20 = (bf16[1,3,4,16,128]{4,3,2,1,0:T(8,128)(2,1)S(1)}, bf16[1,3,4,16,128]{4,3,2,1,0:T(8,128)(2,1)S(1)}, u32[]{:S(2)}, u32[]{:S(2)}) collective-permute-start(bf16[1,3,4,16,128]{4,3,2,1,0:T(8,128)(2,1)S(1)} %get-tuple-element.57), channel_id=1, source_target_pairs={{0,2},{1,3},{2,0},{3,1},{4,6},{5,7},{6,4},{7,5},{8,10},{9,11},{10,... | collective-permute-start | bytes 147464 | tf_op jit(solution)/shard_map/ppermute | solution.py:539

commit v6 on v5

--- a/solution.py
+++ b/solution.py
@@ -110,6 +110,11 @@
                 step(turn - 2*behind)
 
 
+def served_facet(me, index, side):
+    chip = (me >> 1) ^ ((index & ~1) + ((me & 1) ^ side))
+    return 2 * chip + (index & 1)
+
+
 def write_sums(total, me_ref, outs, channel):
     tiles, dec_rows, width = total.shape
     from_left = iota((dec_rows, width), 1) % SPAN >= SPAN // 2
@@ -117,7 +122,7 @@
 
     def one_facet(index, carry):
         for side, out_ref in enumerate(outs):
-            facet = (2 * index + side) ^ me_ref[0] if paired else index
+            facet = served_facet(me_ref[0], index, side) if paired else index
             own = 2 * facet
             left, right = lax.rem(own + tiles - 1, tiles), lax.rem(own + 2, tiles)
             out_ref[index, 0, channel] = total[own].astype(out_ref.dtype)
@@ -173,11 +178,12 @@
     forward[...] = forward_matrix(m_dec[...])
     ra_out[...] = dot(m_ra[...], order[...], ((0,), (1,))).astype(jnp.bfloat16)
     ra_in[...] = dot(order[...], m_ra[...]).astype(jnp.bfloat16)
-
-    def one_channel(channel, carry):
+    for channel in range(channels):
         swapped = dot(swap[...], beams[channel].reshape(dec_rows * beam_count, width)).astype(jnp.bfloat16)
         ordered = dot(swapped, order[...], ((1,), (1,))).astype(jnp.bfloat16)
         table[channel] = ordered.reshape(beam_count, dec_rows, width)
+
+    def one_channel(channel, carry):
         total[...] = jnp.zeros_like(total)
         wait_and_start_next(vis_ref, held, arrived, channel)
 
@@ -495,9 +501,23 @@
     )(*received, thresholds, step_size, *([first] if second else []))
 
 
-def fold_kernel(keep_ref, got_ref, *outs):
-    for index, out_ref in enumerate(outs):
-        out_ref[0] = (keep_ref[index] + got_ref[index]).astype(out_ref.dtype)
+def fold_kernel(me_ref, keep_ref, got_ref, own_ref, *outs):
+    here = jnp.where(me_ref[0] & 1 == 0, 1.0, 0.0).astype(jnp.float32)
+    for parity in range(2):
+        own_ref[parity] = here * (keep_ref[parity] + got_ref[parity])
+        for z, out_ref in enumerate(outs):
+            index = 2 * z + parity
+            out_ref[parity] = (keep_ref[index] + got_ref[index]).astype(out_ref.dtype)
+
+
+def settle_kernel(me_ref, own_ref, *refs):
+    *far, mine_ref, theirs_ref = refs
+    first, second = (
+        own_ref[parity] + sum(far_ref[parity].astype(jnp.float32) for far_ref in far) for parity in range(2)
+    )
+    even = me_ref[0] & 1 == 0
+    mine_ref[0] = jnp.where(even, first, second)
+    theirs_ref[0] = jnp.where(even, second, first)
 
 
 def join_kernel(*refs):
@@ -516,16 +536,16 @@
             out_ref[start : start + rows] = part_ref[index * rows : (index + 1) * rows]
 
 
-def small_call(kernel, name, out_shape, *operands):
-    vmem = pl.BlockSpec(memory_space=pltpu.VMEM)
+def small_call(kernel, name, out_shape, *operands, scalars=()):
+    vmem, smem = pl.BlockSpec(memory_space=pltpu.VMEM), pl.BlockSpec(memory_space=pltpu.SMEM)
     return pl.pallas_call(
         kernel,
         out_shape=out_shape,
-        in_specs=[vmem] * len(operands),
+        in_specs=[smem] * len(scalars) + [vmem] * len(operands),
         out_specs=jax.tree.map(lambda _: vmem, out_shape),
         compiler_params=pltpu.CompilerParams(vmem_limit_bytes=16 << 20),
         name=name,
-    )(*operands)
+    )(*scalars, *operands)
 
 
 def join(*parts):
@@ -539,13 +559,22 @@
     return lax.ppermute(value, "ra", [(source, source ^ difference) for source in range(count)])
 
 
-def pair_exchange(keep, send):
+def pair_exchange(me, keep, send):
+    count = lax.axis_size("ra")
     got = across(send, 1)
-    shape = (1,) + keep.shape[1:]
-    kinds = [jnp.float32] + [jnp.bfloat16] * (keep.shape[0] - 1)
-    parts = small_call(fold_kernel, "fold", [jax.ShapeDtypeStruct(shape, kind) for kind in kinds], keep, got)
-    far = [across(parts[index], 2 * index) for index in reversed(range(1, len(parts)))]
-    return [parts[0]] + far
+    shape = (2,) + keep.shape[1:]
+    steps = keep.shape[0] // 2
+    kinds = [jnp.float32] + [jnp.bfloat16] * steps
+    outs = [jax.ShapeDtypeStruct(shape, kind) for kind in kinds]
+    own, *parts = small_call(fold_kernel, "fold", outs, keep, got, scalars=[me])
+    far = []
+    for z in reversed(range(steps)):
+        pairs = [(source, source ^ (4 * z + 2 * (source & 1))) for source in range(count)]
+        pairs = [(source, target) for source, target in pairs if source != target]
+        far.append(lax.ppermute(parts[z], "ra", pairs))
+    outs = [jax.ShapeDtypeStruct((1,) + keep.shape[1:], jnp.float32)] * 2
+    mine, theirs = small_call(settle_kernel, "settle", outs, own, *far, scalars=[me])
+    return [mine, across(theirs, 1)]
 
 
 def pair_gather(tiles):
@@ -569,7 +598,7 @@
     paired = facets == 16
     if paired:
         base = [lax.axis_index("ra").astype(jnp.int32).reshape(1)]
-        exchange, gather = pair_exchange, pair_gather
+        exchange, gather = functools.partial(pair_exchange, base[0]), pair_gather
     else:
         base = []
         exchange = lambda sums: [lax.all_to_all(sums, "ra", split_axis=0, concat_axis=0, tiled=True)]

time: 77.5 us -> 75.8 us (0.978)
  starting transfers between devices: 29.8 us -> 18.1 us
  waiting for transfers between devices: 19.6 us -> 29.2 us
    ppermute x21 -> x9, starting transfers between devices: 29.8 us -> 6.6 us  [across(): lax.ppermute(value, 'ra', [(source, source ^ difference) for source in ra...]
    ppermute x0 -> x8, waiting for transfers between devices: none -> 14.4 us  [pair_exchange(): far.append(lax.ppermute(parts[z], 'ra', pairs))]
    ppermute x0 -> x8, starting transfers between devices: none -> 11.4 us  [pair_exchange(): far.append(lax.ppermute(parts[z], 'ra', pairs))]
    ppermute x21 -> x9, waiting for transfers between devices: 19.6 us -> 14.8 us  [across(): lax.ppermute(value, 'ra', [(source, source ^ difference) for source in ra...]
  transfers between devices with their start and end apart: 21 -> 17, of which waited for: 14 -> 12; matrix products, arithmetic and copies ran while one was open for 0% -> 0% of each run, Pallas kernels for 0% -> 0%
where the time goes in v6:
time: 75.8 us; the launch traced here: 75.5 us
  waiting for transfers between devices  29.2 us (39%)
  Pallas kernels  28.1 us (37%)
  starting transfers between devices  18.1 us (24%)
    pallas_call x2, Pallas kernels, gradient_call(): pl.pallas_call(functools.partial(second_gradient_kernel if second else fi...  22.4 us
    ppermute x9, waiting for transfers between devices, across(): lax.ppermute(value, 'ra', [(source, source ^ difference) for source in ra...  14.8 us
    ppermute x8, waiting for transfers between devices, pair_exchange(): far.append(lax.ppermute(parts[z], 'ra', pairs))  14.4 us
    ppermute x8, starting transfers between devices, pair_exchange(): far.append(lax.ppermute(parts[z], 'ra', pairs))  11.4 us
    ppermute x9, starting transfers between devices, across(): lax.ppermute(value, 'ra', [(source, source ^ difference) for source in ra...  6.6 us
    pallas_call x2, Pallas kernels, prox_call(): pl.pallas_call(functools.partial(prox_kernel, second, len(received)), out...  5.36 us
  transfers between devices with their start and end apart: 17, of which 12 were waited for; matrix products, arithmetic and copies ran while one was open for 0% of the time, Pallas kernels for 0%

profile of v6, /device:TPU:0, one launch (start us, length us, event | category | flops | bytes accessed | tf_op | source)
XLA Modules:
  0.0 75.5 jit_solution(3161160496344362404)
XLA Ops:
  0.0 9.3 %first_gradient.1 = (f32[8,3,4,16,128]{4,3,2,1,0:T(8,128)S(1)}, f32[8,3,4,16,128]{4,3,2,1,0:T(8,128)S(1)}, bf16[4,16,16,128]{3,2,1,0:T(8,128)(2,1)S(1)}, bf16[25...) custom-call(s32[128]{0:T(128)} %bitcast.12, ...), custom_call_target="tpu_custom_call" | custom-call | flops 2147483648 | bytes 8388608 | tf_op jit(solution)/shard_map/first_gradient/pallas_call | solution.py:278
  9.3 0.5 collective-permute-start
  9.8 1.9 %collective-permute-done.got_ref = f32[8,3,4,16,128]{4,3,2,1,0:T(8,128)S(1)} collective-permute-done((f32[8,3,4,16,128]{4,3,2,1,0:T(8,128)S(1)}, f32[8,3,4,16,128]{4,3,2,1,0:T(8,128)S(1)}, u32[]{:S(2)}, u32[]{:S(2)}) %collective-permute-start) | collective-permute-done | bytes 786464 | tf_op jit(solution)/shard_map/ppermute | solution.py:559
  11.7 0.1 fold.2
  11.8 5.0 %collective-permute-start.1 = (bf16[2,3,4,16,128]{4,3,2,1,0:T(8,128)(2,1)S(1)}, bf16[2,3,4,16,128]{4,3,2,1,0:T(8,128)(2,1)S(1)}, u32[]{:S(2)}, u32[]{:S(2)}) collective-permute-start(bf16[2,3,4,16,128]{4,3,2,1,0:T(8,128)(2,1)S(1)} %get-tuple-element.38), channel_id=1, source_target_pairs={{0,12},{1,15},{2,14},{3,13},{4,8},{5,11},{6,10},{7,9},{8,4},{9,7},... | collective-permute-start | bytes 294920 | tf_op jit(solution)/shard_map/ppermute | solution.py:574
  16.8 0.6 collective-permute-start.3
  17.5 0.7 collective-permute-start.4
  18.1 2.1 %collective-permute-done.1.refs_0_ = bf16[2,3,4,16,128]{4,3,2,1,0:T(8,128)(2,1)S(1)} collective-permute-done((bf16[2,3,4,16,128]{4,3,2,1,0:T(8,128)(2,1)S(1)}, bf16[2,3,4,16,128]{4,3,2,1,0:T(8,128)(2,1)S(1)}, u32[]{:S(2)}, u32[]{:S(2)}) %collective-permute-start.1) | collective-permute-done | bytes 98336 | tf_op jit(solution)/shard_map/ppermute | solution.py:574
  20.2 5.9 %collective-permute-done.2.refs_1_ = bf16[2,3,4,16,128]{4,3,2,1,0:T(8,128)(2,1)S(1)} collective-permute-done((bf16[2,3,4,16,128]{4,3,2,1,0:T(8,128)(2,1)S(1)}, bf16[2,3,4,16,128]{4,3,2,1,0:T(8,128)(2,1)S(1)}, u32[]{:S(2)}, u32[]{:S(2)}) %collective-permute-start.2) | collective-permute-done | bytes 98336 | tf_op jit(solution)/shard_map/ppermute | solution.py:574
  26.2 0.1 collective-permute-start.5
  26.3 1.3 %collective-permute-done.5 = f32[1,3,4,16,128]{4,3,2,1,0:T(8,128)S(1)} collective-permute-done((f32[1,3,4,16,128]{4,3,2,1,0:T(8,128)S(1)}, f32[1,3,4,16,128]{4,3,2,1,0:T(8,128)S(1)}, u32[]{:S(2)}, u32[]{:S(2)}) %collective-permute-start.5) | collective-permute-done | bytes 98336 | tf_op jit(solution)/shard_map/ppermute | solution.py:559
  27.6 2.7 %first_prox.1 = (f32[2,16,8,128]{3,2,1,0:T(8,128)S(1)}, bf16[128,128]{1,0:T(8,128)(2,1)S(1)}) custom-call(f32[1,192,128]{2,1,0:T(8,128)S(1)} %bitcast.8, f32[1,192,128]{2,1,0:T(8,128)S(1)} %bitcast.9, f32[4,4]{1,0:T(4,128)S(1)} %copy-done, f32[4]{0:T(128)S(1)} %copy-done.1), custom_call_target="tpu_custom_call" | custom-call | tf_op jit(solution)/shard_map/first_prox/pallas_call | solution.py:488
  30.2 1.1 %collective-permute-start.6 = (bf16[128,128]{1,0:T(8,128)(2,1)S(1)}, bf16[128,128]{1,0:T(8,128)(2,1)S(1)}, u32[]{:S(2)}, u32[]{:S(2)}) collective-permute-start(bf16[128,128]{1,0:T(8,128)(2,1)S(1)} %get-tuple-element.44.refs_0_), channel_id=1, source_target_pairs={{0,2},{1,3},{2,0},{3,1},{4,6},{5,7},{6,4},{7,5},{8,10},{9,11},{10,... | collective-permute-start | bytes 98312 | tf_op jit(solution)/shard_map/ppermute | solution.py:559
  31.4 2.9 %collective-permute-done.6.refs_1_ = bf16[128,128]{1,0:T(8,128)(2,1)S(1)} collective-permute-done((bf16[128,128]{1,0:T(8,128)(2,1)S(1)}, bf16[128,128]{1,0:T(8,128)(2,1)S(1)}, u32[]{:S(2)}, u32[]{:S(2)}) %collective-permute-start.6) | collective-permute-done | bytes 32800 | tf_op jit(solution)/shard_map/ppermute | solution.py:559
  34.2 2.5 %collective-permute-start.9 = (bf16[256,128]{1,0:T(8,128)(2,1)S(1)}, bf16[256,128]{1,0:T(8,128)(2,1)S(1)}, u32[]{:S(2)}, u32[]{:S(2)}) collective-permute-start(bf16[256,128]{1,0:T(8,128)(2,1)S(1)} %join.2.refs_0_), channel_id=1, source_target_pairs={{0,12},{1,13},{2,14},{3,15},{4,8},{5,9},{6,10},{7,11},{8,4},{9,5},... | collective-permute-start | bytes 196616 | tf_op jit(solution)/shard_map/ppermute | solution.py:559
  36.7 1.9 %collective-permute-start.7 = (bf16[256,128]{1,0:T(8,128)(2,1)S(1)}, bf16[256,128]{1,0:T(8,128)(2,1)S(1)}, u32[]{:S(2)}, u32[]{:S(2)}) collective-permute-start(bf16[256,128]{1,0:T(8,128)(2,1)S(1)} %join.2.refs_0_), channel_id=1, source_target_pairs={{0,4},{1,5},{2,6},{3,7},{4,0},{5,1},{6,2},{7,3},{8,12},{9,13},{10,... | collective-permute-start | bytes 196616 | tf_op jit(solution)/shard_map/ppermute | solution.py:559
  38.6 2.0 %collective-permute-done.9.refs_3_ = bf16[256,128]{1,0:T(8,128)(2,1)S(1)} collective-permute-done((bf16[256,128]{1,0:T(8,128)(2,1)S(1)}, bf16[256,128]{1,0:T(8,128)(2,1)S(1)}, u32[]{:S(2)}, u32[]{:S(2)}) %collective-permute-start.9) | collective-permute-done | bytes 65568 | tf_op jit(solution)/shard_map/ppermute | solution.py:559
  40.6 1.9 %collective-permute-done.8.refs_2_ = bf16[256,128]{1,0:T(8,128)(2,1)S(1)} collective-permute-done((bf16[256,128]{1,0:T(8,128)(2,1)S(1)}, bf16[256,128]{1,0:T(8,128)(2,1)S(1)}, u32[]{:S(2)}, u32[]{:S(2)}) %collective-permute-start.8) | collective-permute-done | bytes 65568 | tf_op jit(solution)/shard_map/ppermute | solution.py:559
  42.6 0.1 collective-permute-start.10
  42.6 1.5 %collective-permute-done.10.refs_1_ = bf16[1024,128]{1,0:T(8,128)(2,1)S(1)} collective-permute-done((bf16[1024,128]{1,0:T(8,128)(2,1)S(1)}, bf16[1024,128]{1,0:T(8,128)(2,1)S(1)}, u32[]{:S(2)}, u32[]{:S(2)}) %collective-permute-start.10) | collective-permute-done | bytes 262176 | tf_op jit(solution)/shard_map/ppermute | solution.py:559
  44.2 13.2 %second_gradient.1 = (f32[8,3,4,16,128]{4,3,2,1,0:T(8,128)S(1)}, f32[8,3,4,16,128]{4,3,2,1,0:T(8,128)S(1)}) custom-call(s32[128]{0:T(128)} %bitcast.13, s32[128]{0:T(128)} %tile_ref.3, s32[128]{0:T(128)} %beam_ref.3, s32[1]{0:T(128)} %bitcast.refs_0_.me_ref, bf16[4,16,128,512]{3,2,1,0:T(8,128)(2,1)} %refs_1_.3, ...), custom_call_target="tpu_custom_call" | custom-call | flops 4294967296 | bytes 8388608 | tf_op jit(solution)/shard_map/second_gradient/pallas_call | solution.py:278
  57.4 0.2 collective-permute-start.11
  57.6 2.2 %collective-permute-done.11.got_ref = f32[8,3,4,16,128]{4,3,2,1,0:T(8,128)S(1)} collective-permute-done((f32[8,3,4,16,128]{4,3,2,1,0:T(8,128)S(1)}, f32[8,3,4,16,128]{4,3,2,1,0:T(8,128)S(1)}, u32[]{:S(2)}, u32[]{:S(2)}) %collective-permute-start.11) | collective-permute-done | bytes 786464 | tf_op jit(solution)/shard_map/ppermute | solution.py:559
  59.7 0.1 fold.3
  59.8 1.8 %collective-permute-start.12 = (bf16[2,3,4,16,128]{4,3,2,1,0:T(8,128)(2,1)S(1)}, bf16[2,3,4,16,128]{4,3,2,1,0:T(8,128)(2,1)S(1)}, u32[]{:S(2)}, u32[]{:S(2)}) collective-permute-start(bf16[2,3,4,16,128]{4,3,2,1,0:T(8,128)(2,1)S(1)} %get-tuple-element.48), channel_id=1, source_target_pairs={{0,12},{1,15},{2,14},{3,13},{4,8},{5,11},{6,10},{7,9},{8,4},{9,7},... | collective-permute-start | bytes 294920 | tf_op jit(solution)/shard_map/ppermute | solution.py:574
  61.7 2.6 %collective-permute-start.14 = (bf16[2,3,4,16,128]{4,3,2,1,0:T(8,128)(2,1)S(1)}, bf16[2,3,4,16,128]{4,3,2,1,0:T(8,128)(2,1)S(1)}, u32[]{:S(2)}, u32[]{:S(2)}) collective-permute-start(bf16[2,3,4,16,128]{4,3,2,1,0:T(8,128)(2,1)S(1)} %get-tuple-element.50), channel_id=1, source_target_pairs={{0,4},{1,7},{2,6},{3,5},{4,0},{5,3},{6,2},{7,1},{8,12},{9,15},{10,... | collective-permute-start | bytes 294920 | tf_op jit(solution)/shard_map/ppermute | solution.py:574
  64.3 0.7 collective-permute-start.15
  64.9 2.5 %collective-permute-done.12.refs_0_ = bf16[2,3,4,16,128]{4,3,2,1,0:T(8,128)(2,1)S(1)} collective-permute-done((bf16[2,3,4,16,128]{4,3,2,1,0:T(8,128)(2,1)S(1)}, bf16[2,3,4,16,128]{4,3,2,1,0:T(8,128)(2,1)S(1)}, u32[]{:S(2)}, u32[]{:S(2)}) %collective-permute-start.12) | collective-permute-done | bytes 98336 | tf_op jit(solution)/shard_map/ppermute | solution.py:574
  67.4 3.9 %collective-permute-done.13.refs_1_ = bf16[2,3,4,16,128]{4,3,2,1,0:T(8,128)(2,1)S(1)} collective-permute-done((bf16[2,3,4,16,128]{4,3,2,1,0:T(8,128)(2,1)S(1)}, bf16[2,3,4,16,128]{4,3,2,1,0:T(8,128)(2,1)S(1)}, u32[]{:S(2)}, u32[]{:S(2)}) %collective-permute-start.13) | collective-permute-done | bytes 98336 | tf_op jit(solution)/shard_map/ppermute | solution.py:574
  71.4 0.3 collective-permute-start.16
  71.7 1.1 %collective-permute-done.16 = f32[1,3,4,16,128]{4,3,2,1,0:T(8,128)S(1)} collective-permute-done((f32[1,3,4,16,128]{4,3,2,1,0:T(8,128)S(1)}, f32[1,3,4,16,128]{4,3,2,1,0:T(8,128)S(1)}, u32[]{:S(2)}, u32[]{:S(2)}) %collective-permute-start.16) | collective-permute-done | bytes 98336 | tf_op jit(solution)/shard_map/ppermute | solution.py:559
  72.8 2.7 %second_prox.1 = f32[4,16,256]{2,1,0:T(8,128)} custom-call(f32[1,192,128]{2,1,0:T(8,128)S(1)} %bitcast.10, f32[1,192,128]{2,1,0:T(8,128)S(1)} %bitcast.11, f32[4,4]{1,0:T(4,128)S(1)} %copy-done, f32[4]{0:T(128)S(1)} %copy-done.1, f32[2,16,8,128]{3,2,1,0:T(8,128)S(1)} %get-tuple-element.54.refs_4_), custom_call_target="tpu_custom_call" | custom-call | tf_op jit(solution)/shard_map/second_prox/pallas_call | solution.py:488
  (17 shorter events, 0.2 us)
Async XLA Ops:
  0.0 27.6 %copy-start = (f32[4,4]{1,0:T(4,128)S(1)}, f32[4,4]{1,0:T(4,128)}, u32[]{:S(2)}) copy-start(f32[4,4]{1,0:T(4,128)} %refs_2_.5) | copy-start | bytes 196
  0.0 27.6 %copy-start.1 = (f32[4]{0:T(128)S(1)}, f32[4]{0:T(128)}, u32[]{:S(2)}) copy-start(f32[4]{0:T(128)} %refs_3_.5) | copy-start | bytes 52
  9.3 2.4 %collective-permute-start = (f32[8,3,4,16,128]{4,3,2,1,0:T(8,128)S(1)}, f32[8,3,4,16,128]{4,3,2,1,0:T(8,128)S(1)}, u32[]{:S(2)}, u32[]{:S(2)}) collective-permute-start(f32[8,3,4,16,128]{4,3,2,1,0:T(8,128)S(1)} %get-tuple-element.36), channel_id=1, source_target_pairs={{0,1},{1,0},{2,3},{3,2},{4,5},{5,4},{6,7},{7,6},{8,9},{9,8},{10,11... | collective-permute-start | bytes 2359304 | tf_op jit(solution)/shard_map/ppermute | solution.py:559
  11.8 8.5 %collective-permute-start.1 = (bf16[2,3,4,16,128]{4,3,2,1,0:T(8,128)(2,1)S(1)}, bf16[2,3,4,16,128]{4,3,2,1,0:T(8,128)(2,1)S(1)}, u32[]{:S(2)}, u32[]{:S(2)}) collective-permute-start(bf16[2,3,4,16,128]{4,3,2,1,0:T(8,128)(2,1)S(1)} %get-tuple-element.38), channel_id=1, source_target_pairs={{0,12},{1,15},{2,14},{3,13},{4,8},{5,11},{6,10},{7,9},{8,4},{9,7},... | collective-permute-start | bytes 294920 | tf_op jit(solution)/shard_map/ppermute | solution.py:574
  16.8 9.3 %collective-permute-start.2 = (bf16[2,3,4,16,128]{4,3,2,1,0:T(8,128)(2,1)S(1)}, bf16[2,3,4,16,128]{4,3,2,1,0:T(8,128)(2,1)S(1)}, u32[]{:S(2)}, u32[]{:S(2)}) collective-permute-start(bf16[2,3,4,16,128]{4,3,2,1,0:T(8,128)(2,1)S(1)} %get-tuple-element.39), channel_id=1, source_target_pairs={{0,8},{1,11},{2,10},{3,9},{4,12},{5,15},{6,14},{7,13},{8,0},{9,3},... | collective-permute-start | bytes 294920 | tf_op jit(solution)/shard_map/ppermute | solution.py:574
  16.8 9.3 %collective-permute-start.3 = (bf16[2,3,4,16,128]{4,3,2,1,0:T(8,128)(2,1)S(1)}, bf16[2,3,4,16,128]{4,3,2,1,0:T(8,128)(2,1)S(1)}, u32[]{:S(2)}, u32[]{:S(2)}) collective-permute-start(bf16[2,3,4,16,128]{4,3,2,1,0:T(8,128)(2,1)S(1)} %get-tuple-element.40), channel_id=1, source_target_pairs={{0,4},{1,7},{2,6},{3,5},{4,0},{5,3},{6,2},{7,1},{8,12},{9,15},{10,... | collective-permute-start | bytes 294920 | tf_op jit(solution)/shard_map/ppermute | solution.py:574
  17.5 8.6 %collective-permute-start.4 = (bf16[2,3,4,16,128]{4,3,2,1,0:T(8,128)(2,1)S(1)}, bf16[2,3,4,16,128]{4,3,2,1,0:T(8,128)(2,1)S(1)}, u32[]{:S(2)}, u32[]{:S(2)}) collective-permute-start(bf16[2,3,4,16,128]{4,3,2,1,0:T(8,128)(2,1)S(1)} %get-tuple-element.41), channel_id=1, source_target_pairs={{1,3},{3,1},{5,7},{7,5},{9,11},{11,9},{13,15},{15,13},{17,19},{19,... | collective-permute-start | bytes 294920 | tf_op jit(solution)/shard_map/ppermute | solution.py:574
  26.2 1.4 %collective-permute-start.5 = (f32[1,3,4,16,128]{4,3,2,1,0:T(8,128)S(1)}, f32[1,3,4,16,128]{4,3,2,1,0:T(8,128)S(1)}, u32[]{:S(2)}, u32[]{:S(2)}) collective-permute-start(f32[1,3,4,16,128]{4,3,2,1,0:T(8,128)S(1)} %get-tuple-element.43), channel_id=1, source_target_pairs={{0,1},{1,0},{2,3},{3,2},{4,5},{5,4},{6,7},{7,6},{8,9},{9,8},{10,11... | collective-permute-start | bytes 294920 | tf_op jit(solution)/shard_map/ppermute | solution.py:559
  30.2 4.0 %collective-permute-start.6 = (bf16[128,128]{1,0:T(8,128)(2,1)S(1)}, bf16[128,128]{1,0:T(8,128)(2,1)S(1)}, u32[]{:S(2)}, u32[]{:S(2)}) collective-permute-start(bf16[128,128]{1,0:T(8,128)(2,1)S(1)} %get-tuple-element.44.refs_0_), channel_id=1, source_target_pairs={{0,2},{1,3},{2,0},{3,1},{4,6},{5,7},{6,4},{7,5},{8,10},{9,11},{10,... | collective-permute-start | bytes 98312 | tf_op jit(solution)/shard_map/ppermute | solution.py:559
  34.2 6.4 %collective-permute-start.9 = (bf16[256,128]{1,0:T(8,128)(2,1)S(1)}, bf16[256,128]{1,0:T(8,128)(2,1)S(1)}, u32[]{:S(2)}, u32[]{:S(2)}) collective-permute-start(bf16[256,128]{1,0:T(8,128)(2,1)S(1)} %join.2.refs_0_), channel_id=1, source_target_pairs={{0,12},{1,13},{2,14},{3,15},{4,8},{5,9},{6,10},{7,11},{8,4},{9,5},... | collective-permute-start | bytes 196616 | tf_op jit(solution)/shard_map/ppermute | solution.py:559
  36.7 5.9 %collective-permute-start.8 = (bf16[256,128]{1,0:T(8,128)(2,1)S(1)}, bf16[256,128]{1,0:T(8,128)(2,1)S(1)}, u32[]{:S(2)}, u32[]{:S(2)}) collective-permute-start(bf16[256,128]{1,0:T(8,128)(2,1)S(1)} %join.2.refs_0_), channel_id=1, source_target_pairs={{0,8},{1,9},{2,10},{3,11},{4,12},{5,13},{6,14},{7,15},{8,0},{9,1},... | collective-permute-start | bytes 196616 | tf_op jit(solution)/shard_map/ppermute | solution.py:559
  36.7 5.9 %collective-permute-start.7 = (bf16[256,128]{1,0:T(8,128)(2,1)S(1)}, bf16[256,128]{1,0:T(8,128)(2,1)S(1)}, u32[]{:S(2)}, u32[]{:S(2)}) collective-permute-start(bf16[256,128]{1,0:T(8,128)(2,1)S(1)} %join.2.refs_0_), channel_id=1, source_target_pairs={{0,4},{1,5},{2,6},{3,7},{4,0},{5,1},{6,2},{7,3},{8,12},{9,13},{10,... | collective-permute-start | bytes 196616 | tf_op jit(solution)/shard_map/ppermute | solution.py:559
  42.6 1.6 %collective-permute-start.10 = (bf16[1024,128]{1,0:T(8,128)(2,1)S(1)}, bf16[1024,128]{1,0:T(8,128)(2,1)S(1)}, u32[]{:S(2)}, u32[]{:S(2)}) collective-permute-start(bf16[1024,128]{1,0:T(8,128)(2,1)S(1)} %join.3.refs_0_), channel_id=1, source_target_pairs={{0,1},{1,0},{2,3},{3,2},{4,5},{5,4},{6,7},{7,6},{8,9},{9,8},{10,11... | collective-permute-start | bytes 786440 | tf_op jit(solution)/shard_map/ppermute | solution.py:559
  57.4 2.4 %collective-permute-start.11 = (f32[8,3,4,16,128]{4,3,2,1,0:T(8,128)S(1)}, f32[8,3,4,16,128]{4,3,2,1,0:T(8,128)S(1)}, u32[]{:S(2)}, u32[]{:S(2)}) collective-permute-start(f32[8,3,4,16,128]{4,3,2,1,0:T(8,128)S(1)} %get-tuple-element.46), channel_id=1, source_target_pairs={{0,1},{1,0},{2,3},{3,2},{4,5},{5,4},{6,7},{7,6},{8,9},{9,8},{10,11... | collective-permute-start | bytes 2359304 | tf_op jit(solution)/shard_map/ppermute | solution.py:559
  59.8 7.6 %collective-permute-start.12 = (bf16[2,3,4,16,128]{4,3,2,1,0:T(8,128)(2,1)S(1)}, bf16[2,3,4,16,128]{4,3,2,1,0:T(8,128)(2,1)S(1)}, u32[]{:S(2)}, u32[]{:S(2)}) collective-permute-start(bf16[2,3,4,16,128]{4,3,2,1,0:T(8,128)(2,1)S(1)} %get-tuple-element.48), channel_id=1, source_target_pairs={{0,12},{1,15},{2,14},{3,13},{4,8},{5,11},{6,10},{7,9},{8,4},{9,7},... | collective-permute-start | bytes 294920 | tf_op jit(solution)/shard_map/ppermute | solution.py:574
  61.7 9.7 %collective-permute-start.13 = (bf16[2,3,4,16,128]{4,3,2,1,0:T(8,128)(2,1)S(1)}, bf16[2,3,4,16,128]{4,3,2,1,0:T(8,128)(2,1)S(1)}, u32[]{:S(2)}, u32[]{:S(2)}) collective-permute-start(bf16[2,3,4,16,128]{4,3,2,1,0:T(8,128)(2,1)S(1)} %get-tuple-element.49), channel_id=1, source_target_pairs={{0,8},{1,11},{2,10},{3,9},{4,12},{5,15},{6,14},{7,13},{8,0},{9,3},... | collective-permute-start | bytes 294920 | tf_op jit(solution)/shard_map/ppermute | solution.py:574
  61.7 9.7 %collective-permute-start.14 = (bf16[2,3,4,16,128]{4,3,2,1,0:T(8,128)(2,1)S(1)}, bf16[2,3,4,16,128]{4,3,2,1,0:T(8,128)(2,1)S(1)}, u32[]{:S(2)}, u32[]{:S(2)}) collective-permute-start(bf16[2,3,4,16,128]{4,3,2,1,0:T(8,128)(2,1)S(1)} %get-tuple-element.50), channel_id=1, source_target_pairs={{0,4},{1,7},{2,6},{3,5},{4,0},{5,3},{6,2},{7,1},{8,12},{9,15},{10,... | collective-permute-start | bytes 294920 | tf_op jit(solution)/shard_map/ppermute | solution.py:574
  64.3 7.1 %collective-permute-start.15 = (bf16[2,3,4,16,128]{4,3,2,1,0:T(8,128)(2,1)S(1)}, bf16[2,3,4,16,128]{4,3,2,1,0:T(8,128)(2,1)S(1)}, u32[]{:S(2)}, u32[]{:S(2)}) collective-permute-start(bf16[2,3,4,16,128]{4,3,2,1,0:T(8,128)(2,1)S(1)} %get-tuple-element.51), channel_id=1, source_target_pairs={{1,3},{3,1},{5,7},{7,5},{9,11},{11,9},{13,15},{15,13},{17,19},{19,... | collective-permute-start | bytes 294920 | tf_op jit(solution)/shard_map/ppermute | solution.py:574
  71.4 1.4 %collective-permute-start.16 = (f32[1,3,4,16,128]{4,3,2,1,0:T(8,128)S(1)}, f32[1,3,4,16,128]{4,3,2,1,0:T(8,128)S(1)}, u32[]{:S(2)}, u32[]{:S(2)}) collective-permute-start(f32[1,3,4,16,128]{4,3,2,1,0:T(8,128)S(1)} %get-tuple-element.53), channel_id=1, source_target_pairs={{0,1},{1,0},{2,3},{3,2},{4,5},{5,4},{6,7},{7,6},{8,9},{9,8},{10,11... | collective-permute-start | bytes 294920 | tf_op jit(solution)/shard_map/ppermute | solution.py:559

commit v7 on v6

--- a/solution.py
+++ b/solution.py
@@ -528,12 +528,25 @@
         start += part_ref.shape[0]
 
 
-def weave_kernel(rows, *refs):
-    *parts, out_ref = refs
-    for index in range(parts[0].shape[0] // rows):
-        for side, part_ref in enumerate(parts):
-            start = (2 * index + side) * rows
-            out_ref[start : start + rows] = part_ref[index * rows : (index + 1) * rows]
+def served_kernel(me_ref, own_ref, *refs):
+    *far, out_ref = refs
+    even = me_ref[0] & 1 == 0
+    rows = own_ref.shape[0]
+    nearest = jnp.where(even, own_ref[...].astype(jnp.float32), far[0][...].astype(jnp.float32))
+    out_ref[:rows] = nearest.astype(out_ref.dtype)
+    for z in range(1, len(far)):
+        out_ref[z * rows : (z + 1) * rows] = far[z][...]
+
+
+def weave_kernel(rows, me_ref, mine_ref, theirs_ref, out_ref):
+    core = me_ref[0] & 1
+    for index in range(mine_ref.shape[0] // rows):
+        z, b = index // 2, index % 2
+        block = slice(index * rows, (index + 1) * rows)
+        start = pl.multiple_of((4 * z + 2 * core + b) * rows, rows)
+        out_ref[pl.ds(start, rows)] = mine_ref[block]
+        start = pl.multiple_of((4 * z + 2 * (1 - core) + (1 - b)) * rows, rows)
+        out_ref[pl.ds(start, rows)] = theirs_ref[block]
 
 
 def small_call(kernel, name, out_shape, *operands, scalars=()):
@@ -559,31 +572,35 @@
     return lax.ppermute(value, "ra", [(source, source ^ difference) for source in range(count)])
 
 
+def to_served(value, z):
+    count = lax.axis_size("ra")
+    pairs = [(source, source ^ (4 * z + 2 * (source & 1))) for source in range(count)]
+    return lax.ppermute(value, "ra", [(source, target) for source, target in pairs if source != target])
+
+
 def pair_exchange(me, keep, send):
-    count = lax.axis_size("ra")
     got = across(send, 1)
     shape = (2,) + keep.shape[1:]
     steps = keep.shape[0] // 2
     kinds = [jnp.float32] + [jnp.bfloat16] * steps
     outs = [jax.ShapeDtypeStruct(shape, kind) for kind in kinds]
     own, *parts = small_call(fold_kernel, "fold", outs, keep, got, scalars=[me])
-    far = []
-    for z in reversed(range(steps)):
-        pairs = [(source, source ^ (4 * z + 2 * (source & 1))) for source in range(count)]
-        pairs = [(source, target) for source, target in pairs if source != target]
-        far.append(lax.ppermute(parts[z], "ra", pairs))
+    far = [to_served(parts[z], z) for z in reversed(range(steps))]
     outs = [jax.ShapeDtypeStruct((1,) + keep.shape[1:], jnp.float32)] * 2
     mine, theirs = small_call(settle_kernel, "settle", outs, own, *far, scalars=[me])
     return [mine, across(theirs, 1)]
 
 
-def pair_gather(tiles):
-    rows = tiles.shape[0]
-    tiles = join(tiles, across(tiles, 2))
-    far = [across(tiles, difference) for difference in (12, 8, 4)]
-    tiles = join(tiles, *reversed(far))
-    shape = jax.ShapeDtypeStruct((2 * tiles.shape[0],) + tiles.shape[1:], tiles.dtype)
-    return small_call(functools.partial(weave_kernel, rows), "weave", shape, tiles, across(tiles, 1))
+def pair_gather(me, tiles):
+    rows, width = tiles.shape
+    facets = lax.axis_size("ra")
+    both = join(tiles, across(tiles, 1))
+    far = [to_served(both, z) for z in reversed(range(facets // 4))]
+    shape = jax.ShapeDtypeStruct((facets // 2 * rows, width), tiles.dtype)
+    mine = small_call(served_kernel, "served", shape, both, *reversed(far), scalars=[me])
+    shape = jax.ShapeDtypeStruct((facets * rows, width), tiles.dtype)
+    weave = functools.partial(weave_kernel, rows)
+    return small_call(weave, "weave", shape, mine, across(mine, 1), scalars=[me])
 
 
 def local(vis, beams, m_ra, m_dec, facet_of, tile_of, beam_of, step_size, thresholds):
@@ -598,7 +615,7 @@
     paired = facets == 16
     if paired:
         base = [lax.axis_index("ra").astype(jnp.int32).reshape(1)]
-        exchange, gather = functools.partial(pair_exchange, base[0]), pair_gather
+        exchange, gather = functools.partial(pair_exchange, base[0]), functools.partial(pair_gather, base[0])
     else:
         base = []
         exchange = lambda sums: [lax.all_to_all(sums, "ra", split_axis=0, concat_axis=0, tiled=True)]

time: 75.8 us -> 74.8 us (0.987)
  waiting for transfers between devices: 29.2 us -> 27.4 us
    ppermute x9 -> x6, waiting for transfers between devices: 14.8 us -> 8.49 us  [across(): lax.ppermute(value, 'ra', [(source, source ^ difference) for source in ra...]
    ppermute x8 -> x12, starting transfers between devices: 11.4 us -> 16.5 us  [to_served(): lax.ppermute(value, 'ra', [(source, target) for source, target in pairs i...]
    ppermute x8 -> x12, waiting for transfers between devices: 14.4 us -> 18.9 us  [to_served(): lax.ppermute(value, 'ra', [(source, target) for source, target in pairs i...]
    ppermute x9 -> x6, starting transfers between devices: 6.6 us -> 2.35 us  [across(): lax.ppermute(value, 'ra', [(source, source ^ difference) for source in ra...]
  transfers between devices with their start and end apart: 17 -> 18, of which waited for: 12 -> 12; matrix products, arithmetic and copies ran while one was open for 0% -> 0% of each run, Pallas kernels for 0% -> 0%
where the time goes in v7:
time: 74.8 us; the launch traced here: 74.5 us
  Pallas kernels  28.1 us (38%)
  waiting for transfers between devices  27.4 us (37%)
  starting transfers between devices  18.8 us (25%)
    pallas_call x2, Pallas kernels, gradient_call(): pl.pallas_call(functools.partial(second_gradient_kernel if second else fi...  22.4 us
    ppermute x12, waiting for transfers between devices, to_served(): lax.ppermute(value, 'ra', [(source, target) for source, target in pairs i...  18.9 us
    ppermute x12, starting transfers between devices, to_served(): lax.ppermute(value, 'ra', [(source, target) for source, target in pairs i...  16.5 us
    ppermute x6, waiting for transfers between devices, across(): lax.ppermute(value, 'ra', [(source, source ^ difference) for source in ra...  8.49 us
    pallas_call x2, Pallas kernels, prox_call(): pl.pallas_call(functools.partial(prox_kernel, second, len(received)), out...  5.36 us
    ppermute x6, starting transfers between devices, across(): lax.ppermute(value, 'ra', [(source, source ^ difference) for source in ra...  2.35 us
  transfers between devices with their start and end apart: 18, of which 12 were waited for; matrix products, arithmetic and copies ran while one was open for 0% of the time, Pallas kernels for 0%

profile of v7, /device:TPU:0, one launch (start us, length us, event | category | flops | bytes accessed | tf_op | source)
XLA Modules:
  0.0 74.5 jit_solution(9271545597339679237)
XLA Ops:
  0.0 9.3 %first_gradient.1 = (f32[8,3,4,16,128]{4,3,2,1,0:T(8,128)S(1)}, f32[8,3,4,16,128]{4,3,2,1,0:T(8,128)S(1)}, bf16[4,16,16,128]{3,2,1,0:T(8,128)(2,1)S(1)}, bf16[25...) custom-call(s32[128]{0:T(128)} %bitcast.12, ...), custom_call_target="tpu_custom_call" | custom-call | flops 2147483648 | bytes 8388608 | tf_op jit(solution)/shard_map/first_gradient/pallas_call | solution.py:278
  9.3 0.5 collective-permute-start
  9.8 1.9 %collective-permute-done.got_ref = f32[8,3,4,16,128]{4,3,2,1,0:T(8,128)S(1)} collective-permute-done((f32[8,3,4,16,128]{4,3,2,1,0:T(8,128)S(1)}, f32[8,3,4,16,128]{4,3,2,1,0:T(8,128)S(1)}, u32[]{:S(2)}, u32[]{:S(2)}) %collective-permute-start) | collective-permute-done | bytes 786464 | tf_op jit(solution)/shard_map/ppermute | solution.py:572
  11.7 0.1 fold.2
  11.8 5.0 %collective-permute-start.1 = (bf16[2,3,4,16,128]{4,3,2,1,0:T(8,128)(2,1)S(1)}, bf16[2,3,4,16,128]{4,3,2,1,0:T(8,128)(2,1)S(1)}, u32[]{:S(2)}, u32[]{:S(2)}) collective-permute-start(bf16[2,3,4,16,128]{4,3,2,1,0:T(8,128)(2,1)S(1)} %get-tuple-element.38), channel_id=1, source_target_pairs={{0,12},{1,15},{2,14},{3,13},{4,8},{5,11},{6,10},{7,9},{8,4},{9,7},... | collective-permute-start | bytes 294920 | tf_op jit(solution)/shard_map/ppermute | solution.py:578
  16.8 0.6 collective-permute-start.3
  17.5 0.7 collective-permute-start.4
  18.1 2.1 %collective-permute-done.1.refs_0_ = bf16[2,3,4,16,128]{4,3,2,1,0:T(8,128)(2,1)S(1)} collective-permute-done((bf16[2,3,4,16,128]{4,3,2,1,0:T(8,128)(2,1)S(1)}, bf16[2,3,4,16,128]{4,3,2,1,0:T(8,128)(2,1)S(1)}, u32[]{:S(2)}, u32[]{:S(2)}) %collective-permute-start.1) | collective-permute-done | bytes 98336 | tf_op jit(solution)/shard_map/ppermute | solution.py:578
  20.2 5.9 %collective-permute-done.2.refs_1_ = bf16[2,3,4,16,128]{4,3,2,1,0:T(8,128)(2,1)S(1)} collective-permute-done((bf16[2,3,4,16,128]{4,3,2,1,0:T(8,128)(2,1)S(1)}, bf16[2,3,4,16,128]{4,3,2,1,0:T(8,128)(2,1)S(1)}, u32[]{:S(2)}, u32[]{:S(2)}) %collective-permute-start.2) | collective-permute-done | bytes 98336 | tf_op jit(solution)/shard_map/ppermute | solution.py:578
  26.3 1.3 %collective-permute-done.5 = f32[1,3,4,16,128]{4,3,2,1,0:T(8,128)S(1)} collective-permute-done((f32[1,3,4,16,128]{4,3,2,1,0:T(8,128)S(1)}, f32[1,3,4,16,128]{4,3,2,1,0:T(8,128)S(1)}, u32[]{:S(2)}, u32[]{:S(2)}) %collective-permute-start.5) | collective-permute-done | bytes 98336 | tf_op jit(solution)/shard_map/ppermute | solution.py:572
  27.5 2.7 %first_prox.1 = (f32[2,16,8,128]{3,2,1,0:T(8,128)S(1)}, bf16[128,128]{1,0:T(8,128)(2,1)S(1)}) custom-call(f32[1,192,128]{2,1,0:T(8,128)S(1)} %bitcast.8, f32[1,192,128]{2,1,0:T(8,128)S(1)} %bitcast.9, f32[4,4]{1,0:T(4,128)S(1)} %copy-done, f32[4]{0:T(128)S(1)} %copy-done.1), custom_call_target="tpu_custom_call" | custom-call | tf_op jit(solution)/shard_map/first_prox/pallas_call | solution.py:488
  30.2 0.2 collective-permute-start.6
  30.4 1.1 %collective-permute-done.6.refs_1_ = bf16[128,128]{1,0:T(8,128)(2,1)S(1)} collective-permute-done((bf16[128,128]{1,0:T(8,128)(2,1)S(1)}, bf16[128,128]{1,0:T(8,128)(2,1)S(1)}, u32[]{:S(2)}, u32[]{:S(2)}) %collective-permute-start.6) | collective-permute-done | bytes 32800 | tf_op jit(solution)/shard_map/ppermute | solution.py:572
  31.5 2.5 %collective-permute-start.10 = (bf16[256,128]{1,0:T(8,128)(2,1)S(1)}, bf16[256,128]{1,0:T(8,128)(2,1)S(1)}, u32[]{:S(2)}, u32[]{:S(2)}) collective-permute-start(bf16[256,128]{1,0:T(8,128)(2,1)S(1)} %join.1.own_ref), channel_id=1, source_target_pairs={{0,12},{1,15},{2,14},{3,13},{4,8},{5,11},{6,10},{7,9},{8,4},{9,7},... | collective-permute-start | bytes 196616 | tf_op jit(solution)/shard_map/ppermute | solution.py:578
  34.0 1.9 %collective-permute-start.8 = (bf16[256,128]{1,0:T(8,128)(2,1)S(1)}, bf16[256,128]{1,0:T(8,128)(2,1)S(1)}, u32[]{:S(2)}, u32[]{:S(2)}) collective-permute-start(bf16[256,128]{1,0:T(8,128)(2,1)S(1)} %join.1.own_ref), channel_id=1, source_target_pairs={{0,4},{1,7},{2,6},{3,5},{4,0},{5,3},{6,2},{7,1},{8,12},{9,15},{10,... | collective-permute-start | bytes 196616 | tf_op jit(solution)/shard_map/ppermute | solution.py:578
  35.9 0.7 collective-permute-start.7
  36.6 1.7 %collective-permute-done.10.refs_3_ = bf16[256,128]{1,0:T(8,128)(2,1)S(1)} collective-permute-done((bf16[256,128]{1,0:T(8,128)(2,1)S(1)}, bf16[256,128]{1,0:T(8,128)(2,1)S(1)}, u32[]{:S(2)}, u32[]{:S(2)}) %collective-permute-start.10) | collective-permute-done | bytes 65568 | tf_op jit(solution)/shard_map/ppermute | solution.py:578
  38.3 2.7 %collective-permute-done.9.refs_2_ = bf16[256,128]{1,0:T(8,128)(2,1)S(1)} collective-permute-done((bf16[256,128]{1,0:T(8,128)(2,1)S(1)}, bf16[256,128]{1,0:T(8,128)(2,1)S(1)}, u32[]{:S(2)}, u32[]{:S(2)}) %collective-permute-start.9) | collective-permute-done | bytes 65568 | tf_op jit(solution)/shard_map/ppermute | solution.py:578
  41.0 0.9 %collective-permute-start.11 = (bf16[1024,128]{1,0:T(8,128)(2,1)S(1)}, bf16[1024,128]{1,0:T(8,128)(2,1)S(1)}, u32[]{:S(2)}, u32[]{:S(2)}) collective-permute-start(bf16[1024,128]{1,0:T(8,128)(2,1)S(1)} %served.1.mine_ref), channel_id=1, source_target_pairs={{0,1},{1,0},{2,3},{3,2},{4,5},{5,4},{6,7},{7,6},{8,9},{9,8},{10,11... | collective-permute-start | bytes 786440 | tf_op jit(solution)/shard_map/ppermute | solution.py:572
  41.9 1.2 %collective-permute-done.11.theirs_ref = bf16[1024,128]{1,0:T(8,128)(2,1)S(1)} collective-permute-done((bf16[1024,128]{1,0:T(8,128)(2,1)S(1)}, bf16[1024,128]{1,0:T(8,128)(2,1)S(1)}, u32[]{:S(2)}, u32[]{:S(2)}) %collective-permute-start.11) | collective-permute-done | bytes 262176 | tf_op jit(solution)/shard_map/ppermute | solution.py:572
  43.1 13.2 %second_gradient.1 = (f32[8,3,4,16,128]{4,3,2,1,0:T(8,128)S(1)}, f32[8,3,4,16,128]{4,3,2,1,0:T(8,128)S(1)}) custom-call(s32[128]{0:T(128)} %bitcast.13, s32[128]{0:T(128)} %tile_ref.3, s32[128]{0:T(128)} %beam_ref.3, s32[1]{0:T(128)} %bitcast.refs_0_.me_ref, bf16[4,16,128,512]{3,2,1,0:T(8,128)(2,1)} %refs_1_.3, ...), custom_call_target="tpu_custom_call" | custom-call | flops 4294967296 | bytes 8388608 | tf_op jit(solution)/shard_map/second_gradient/pallas_call | solution.py:278
  56.3 0.4 collective-permute-start.12
  56.7 1.9 %collective-permute-done.12.got_ref = f32[8,3,4,16,128]{4,3,2,1,0:T(8,128)S(1)} collective-permute-done((f32[8,3,4,16,128]{4,3,2,1,0:T(8,128)S(1)}, f32[8,3,4,16,128]{4,3,2,1,0:T(8,128)S(1)}, u32[]{:S(2)}, u32[]{:S(2)}) %collective-permute-start.12) | collective-permute-done | bytes 786464 | tf_op jit(solution)/shard_map/ppermute | solution.py:572
  58.6 0.1 fold.3
  58.7 2.6 %collective-permute-start.13 = (bf16[2,3,4,16,128]{4,3,2,1,0:T(8,128)(2,1)S(1)}, bf16[2,3,4,16,128]{4,3,2,1,0:T(8,128)(2,1)S(1)}, u32[]{:S(2)}, u32[]{:S(2)}) collective-permute-start(bf16[2,3,4,16,128]{4,3,2,1,0:T(8,128)(2,1)S(1)} %get-tuple-element.48), channel_id=1, source_target_pairs={{0,12},{1,15},{2,14},{3,13},{4,8},{5,11},{6,10},{7,9},{8,4},{9,7},... | collective-permute-start | bytes 294920 | tf_op jit(solution)/shard_map/ppermute | solution.py:578
  61.3 1.9 %collective-permute-start.15 = (bf16[2,3,4,16,128]{4,3,2,1,0:T(8,128)(2,1)S(1)}, bf16[2,3,4,16,128]{4,3,2,1,0:T(8,128)(2,1)S(1)}, u32[]{:S(2)}, u32[]{:S(2)}) collective-permute-start(bf16[2,3,4,16,128]{4,3,2,1,0:T(8,128)(2,1)S(1)} %get-tuple-element.50), channel_id=1, source_target_pairs={{0,4},{1,7},{2,6},{3,5},{4,0},{5,3},{6,2},{7,1},{8,12},{9,15},{10,... | collective-permute-start | bytes 294920 | tf_op jit(solution)/shard_map/ppermute | solution.py:578
  63.2 0.7 collective-permute-start.16
  63.8 2.5 %collective-permute-done.13.refs_0_ = bf16[2,3,4,16,128]{4,3,2,1,0:T(8,128)(2,1)S(1)} collective-permute-done((bf16[2,3,4,16,128]{4,3,2,1,0:T(8,128)(2,1)S(1)}, bf16[2,3,4,16,128]{4,3,2,1,0:T(8,128)(2,1)S(1)}, u32[]{:S(2)}, u32[]{:S(2)}) %collective-permute-start.13) | collective-permute-done | bytes 98336 | tf_op jit(solution)/shard_map/ppermute | solution.py:578
  66.3 4.0 %collective-permute-done.14.refs_1_ = bf16[2,3,4,16,128]{4,3,2,1,0:T(8,128)(2,1)S(1)} collective-permute-done((bf16[2,3,4,16,128]{4,3,2,1,0:T(8,128)(2,1)S(1)}, bf16[2,3,4,16,128]{4,3,2,1,0:T(8,128)(2,1)S(1)}, u32[]{:S(2)}, u32[]{:S(2)}) %collective-permute-start.14) | collective-permute-done | bytes 98336 | tf_op jit(solution)/shard_map/ppermute | solution.py:578
  70.5 0.2 collective-permute-start.17
  70.7 1.1 %collective-permute-done.17 = f32[1,3,4,16,128]{4,3,2,1,0:T(8,128)S(1)} collective-permute-done((f32[1,3,4,16,128]{4,3,2,1,0:T(8,128)S(1)}, f32[1,3,4,16,128]{4,3,2,1,0:T(8,128)S(1)}, u32[]{:S(2)}, u32[]{:S(2)}) %collective-permute-start.17) | collective-permute-done | bytes 98336 | tf_op jit(solution)/shard_map/ppermute | solution.py:572
  71.8 2.7 %second_prox.1 = f32[4,16,256]{2,1,0:T(8,128)} custom-call(f32[1,192,128]{2,1,0:T(8,128)S(1)} %bitcast.10, f32[1,192,128]{2,1,0:T(8,128)S(1)} %bitcast.11, f32[4,4]{1,0:T(4,128)S(1)} %copy-done, f32[4]{0:T(128)S(1)} %copy-done.1, f32[2,16,8,128]{3,2,1,0:T(8,128)S(1)} %get-tuple-element.54.refs_4_), custom_call_target="tpu_custom_call" | custom-call | tf_op jit(solution)/shard_map/second_prox/pallas_call | solution.py:488
  (19 shorter events, 0.3 us)
Async XLA Ops:
  0.0 27.5 %copy-start = (f32[4,4]{1,0:T(4,128)S(1)}, f32[4,4]{1,0:T(4,128)}, u32[]{:S(2)}) copy-start(f32[4,4]{1,0:T(4,128)} %refs_2_.5) | copy-start | bytes 196
  0.0 27.5 %copy-start.1 = (f32[4]{0:T(128)S(1)}, f32[4]{0:T(128)}, u32[]{:S(2)}) copy-start(f32[4]{0:T(128)} %refs_3_.5) | copy-start | bytes 52
  9.3 2.4 %collective-permute-start = (f32[8,3,4,16,128]{4,3,2,1,0:T(8,128)S(1)}, f32[8,3,4,16,128]{4,3,2,1,0:T(8,128)S(1)}, u32[]{:S(2)}, u32[]{:S(2)}) collective-permute-start(f32[8,3,4,16,128]{4,3,2,1,0:T(8,128)S(1)} %get-tuple-element.36), channel_id=1, source_target_pairs={{0,1},{1,0},{2,3},{3,2},{4,5},{5,4},{6,7},{7,6},{8,9},{9,8},{10,11... | collective-permute-start | bytes 2359304 | tf_op jit(solution)/shard_map/ppermute | solution.py:572
  11.8 8.5 %collective-permute-start.1 = (bf16[2,3,4,16,128]{4,3,2,1,0:T(8,128)(2,1)S(1)}, bf16[2,3,4,16,128]{4,3,2,1,0:T(8,128)(2,1)S(1)}, u32[]{:S(2)}, u32[]{:S(2)}) collective-permute-start(bf16[2,3,4,16,128]{4,3,2,1,0:T(8,128)(2,1)S(1)} %get-tuple-element.38), channel_id=1, source_target_pairs={{0,12},{1,15},{2,14},{3,13},{4,8},{5,11},{6,10},{7,9},{8,4},{9,7},... | collective-permute-start | bytes 294920 | tf_op jit(solution)/shard_map/ppermute | solution.py:578
  16.8 9.3 %collective-permute-start.2 = (bf16[2,3,4,16,128]{4,3,2,1,0:T(8,128)(2,1)S(1)}, bf16[2,3,4,16,128]{4,3,2,1,0:T(8,128)(2,1)S(1)}, u32[]{:S(2)}, u32[]{:S(2)}) collective-permute-start(bf16[2,3,4,16,128]{4,3,2,1,0:T(8,128)(2,1)S(1)} %get-tuple-element.39), channel_id=1, source_target_pairs={{0,8},{1,11},{2,10},{3,9},{4,12},{5,15},{6,14},{7,13},{8,0},{9,3},... | collective-permute-start | bytes 294920 | tf_op jit(solution)/shard_map/ppermute | solution.py:578
  16.8 9.3 %collective-permute-start.3 = (bf16[2,3,4,16,128]{4,3,2,1,0:T(8,128)(2,1)S(1)}, bf16[2,3,4,16,128]{4,3,2,1,0:T(8,128)(2,1)S(1)}, u32[]{:S(2)}, u32[]{:S(2)}) collective-permute-start(bf16[2,3,4,16,128]{4,3,2,1,0:T(8,128)(2,1)S(1)} %get-tuple-element.40), channel_id=1, source_target_pairs={{0,4},{1,7},{2,6},{3,5},{4,0},{5,3},{6,2},{7,1},{8,12},{9,15},{10,... | collective-permute-start | bytes 294920 | tf_op jit(solution)/shard_map/ppermute | solution.py:578
  17.5 8.6 %collective-permute-start.4 = (bf16[2,3,4,16,128]{4,3,2,1,0:T(8,128)(2,1)S(1)}, bf16[2,3,4,16,128]{4,3,2,1,0:T(8,128)(2,1)S(1)}, u32[]{:S(2)}, u32[]{:S(2)}) collective-permute-start(bf16[2,3,4,16,128]{4,3,2,1,0:T(8,128)(2,1)S(1)} %get-tuple-element.41), channel_id=1, source_target_pairs={{1,3},{3,1},{5,7},{7,5},{9,11},{11,9},{13,15},{15,13},{17,19},{19,... | collective-permute-start | bytes 294920 | tf_op jit(solution)/shard_map/ppermute | solution.py:578
  26.2 1.4 %collective-permute-start.5 = (f32[1,3,4,16,128]{4,3,2,1,0:T(8,128)S(1)}, f32[1,3,4,16,128]{4,3,2,1,0:T(8,128)S(1)}, u32[]{:S(2)}, u32[]{:S(2)}) collective-permute-start(f32[1,3,4,16,128]{4,3,2,1,0:T(8,128)S(1)} %get-tuple-element.43), channel_id=1, source_target_pairs={{0,1},{1,0},{2,3},{3,2},{4,5},{5,4},{6,7},{7,6},{8,9},{9,8},{10,11... | collective-permute-start | bytes 294920 | tf_op jit(solution)/shard_map/ppermute | solution.py:572
  30.2 1.3 %collective-permute-start.6 = (bf16[128,128]{1,0:T(8,128)(2,1)S(1)}, bf16[128,128]{1,0:T(8,128)(2,1)S(1)}, u32[]{:S(2)}, u32[]{:S(2)}) collective-permute-start(bf16[128,128]{1,0:T(8,128)(2,1)S(1)} %get-tuple-element.44.refs_0_), channel_id=1, source_target_pairs={{0,1},{1,0},{2,3},{3,2},{4,5},{5,4},{6,7},{7,6},{8,9},{9,8},{10,11... | collective-permute-start | bytes 98312 | tf_op jit(solution)/shard_map/ppermute | solution.py:572
  31.5 6.8 %collective-permute-start.10 = (bf16[256,128]{1,0:T(8,128)(2,1)S(1)}, bf16[256,128]{1,0:T(8,128)(2,1)S(1)}, u32[]{:S(2)}, u32[]{:S(2)}) collective-permute-start(bf16[256,128]{1,0:T(8,128)(2,1)S(1)} %join.1.own_ref), channel_id=1, source_target_pairs={{0,12},{1,15},{2,14},{3,13},{4,8},{5,11},{6,10},{7,9},{8,4},{9,7},... | collective-permute-start | bytes 196616 | tf_op jit(solution)/shard_map/ppermute | solution.py:578
  34.0 7.0 %collective-permute-start.9 = (bf16[256,128]{1,0:T(8,128)(2,1)S(1)}, bf16[256,128]{1,0:T(8,128)(2,1)S(1)}, u32[]{:S(2)}, u32[]{:S(2)}) collective-permute-start(bf16[256,128]{1,0:T(8,128)(2,1)S(1)} %join.1.own_ref), channel_id=1, source_target_pairs={{0,8},{1,11},{2,10},{3,9},{4,12},{5,15},{6,14},{7,13},{8,0},{9,3},... | collective-permute-start | bytes 196616 | tf_op jit(solution)/shard_map/ppermute | solution.py:578
  34.0 7.0 %collective-permute-start.8 = (bf16[256,128]{1,0:T(8,128)(2,1)S(1)}, bf16[256,128]{1,0:T(8,128)(2,1)S(1)}, u32[]{:S(2)}, u32[]{:S(2)}) collective-permute-start(bf16[256,128]{1,0:T(8,128)(2,1)S(1)} %join.1.own_ref), channel_id=1, source_target_pairs={{0,4},{1,7},{2,6},{3,5},{4,0},{5,3},{6,2},{7,1},{8,12},{9,15},{10,... | collective-permute-start | bytes 196616 | tf_op jit(solution)/shard_map/ppermute | solution.py:578
  35.9 5.1 %collective-permute-start.7 = (bf16[256,128]{1,0:T(8,128)(2,1)S(1)}, bf16[256,128]{1,0:T(8,128)(2,1)S(1)}, u32[]{:S(2)}, u32[]{:S(2)}) collective-permute-start(bf16[256,128]{1,0:T(8,128)(2,1)S(1)} %join.1.own_ref), channel_id=1, source_target_pairs={{1,3},{3,1},{5,7},{7,5},{9,11},{11,9},{13,15},{15,13},{17,19},{19,... | collective-permute-start | bytes 196616 | tf_op jit(solution)/shard_map/ppermute | solution.py:578
  41.0 2.1 %collective-permute-start.11 = (bf16[1024,128]{1,0:T(8,128)(2,1)S(1)}, bf16[1024,128]{1,0:T(8,128)(2,1)S(1)}, u32[]{:S(2)}, u32[]{:S(2)}) collective-permute-start(bf16[1024,128]{1,0:T(8,128)(2,1)S(1)} %served.1.mine_ref), channel_id=1, source_target_pairs={{0,1},{1,0},{2,3},{3,2},{4,5},{5,4},{6,7},{7,6},{8,9},{9,8},{10,11... | collective-permute-start | bytes 786440 | tf_op jit(solution)/shard_map/ppermute | solution.py:572
  56.3 2.4 %collective-permute-start.12 = (f32[8,3,4,16,128]{4,3,2,1,0:T(8,128)S(1)}, f32[8,3,4,16,128]{4,3,2,1,0:T(8,128)S(1)}, u32[]{:S(2)}, u32[]{:S(2)}) collective-permute-start(f32[8,3,4,16,128]{4,3,2,1,0:T(8,128)S(1)} %get-tuple-element.46), channel_id=1, source_target_pairs={{0,1},{1,0},{2,3},{3,2},{4,5},{5,4},{6,7},{7,6},{8,9},{9,8},{10,11... | collective-permute-start | bytes 2359304 | tf_op jit(solution)/shard_map/ppermute | solution.py:572
  58.7 7.6 %collective-permute-start.13 = (bf16[2,3,4,16,128]{4,3,2,1,0:T(8,128)(2,1)S(1)}, bf16[2,3,4,16,128]{4,3,2,1,0:T(8,128)(2,1)S(1)}, u32[]{:S(2)}, u32[]{:S(2)}) collective-permute-start(bf16[2,3,4,16,128]{4,3,2,1,0:T(8,128)(2,1)S(1)} %get-tuple-element.48), channel_id=1, source_target_pairs={{0,12},{1,15},{2,14},{3,13},{4,8},{5,11},{6,10},{7,9},{8,4},{9,7},... | collective-permute-start | bytes 294920 | tf_op jit(solution)/shard_map/ppermute | solution.py:578
  61.3 9.1 %collective-permute-start.14 = (bf16[2,3,4,16,128]{4,3,2,1,0:T(8,128)(2,1)S(1)}, bf16[2,3,4,16,128]{4,3,2,1,0:T(8,128)(2,1)S(1)}, u32[]{:S(2)}, u32[]{:S(2)}) collective-permute-start(bf16[2,3,4,16,128]{4,3,2,1,0:T(8,128)(2,1)S(1)} %get-tuple-element.49), channel_id=1, source_target_pairs={{0,8},{1,11},{2,10},{3,9},{4,12},{5,15},{6,14},{7,13},{8,0},{9,3},... | collective-permute-start | bytes 294920 | tf_op jit(solution)/shard_map/ppermute | solution.py:578
  61.3 9.1 %collective-permute-start.15 = (bf16[2,3,4,16,128]{4,3,2,1,0:T(8,128)(2,1)S(1)}, bf16[2,3,4,16,128]{4,3,2,1,0:T(8,128)(2,1)S(1)}, u32[]{:S(2)}, u32[]{:S(2)}) collective-permute-start(bf16[2,3,4,16,128]{4,3,2,1,0:T(8,128)(2,1)S(1)} %get-tuple-element.50), channel_id=1, source_target_pairs={{0,4},{1,7},{2,6},{3,5},{4,0},{5,3},{6,2},{7,1},{8,12},{9,15},{10,... | collective-permute-start | bytes 294920 | tf_op jit(solution)/shard_map/ppermute | solution.py:578
  63.2 7.2 %collective-permute-start.16 = (bf16[2,3,4,16,128]{4,3,2,1,0:T(8,128)(2,1)S(1)}, bf16[2,3,4,16,128]{4,3,2,1,0:T(8,128)(2,1)S(1)}, u32[]{:S(2)}, u32[]{:S(2)}) collective-permute-start(bf16[2,3,4,16,128]{4,3,2,1,0:T(8,128)(2,1)S(1)} %get-tuple-element.51), channel_id=1, source_target_pairs={{1,3},{3,1},{5,7},{7,5},{9,11},{11,9},{13,15},{15,13},{17,19},{19,... | collective-permute-start | bytes 294920 | tf_op jit(solution)/shard_map/ppermute | solution.py:578
  70.5 1.4 %collective-permute-start.17 = (f32[1,3,4,16,128]{4,3,2,1,0:T(8,128)S(1)}, f32[1,3,4,16,128]{4,3,2,1,0:T(8,128)S(1)}, u32[]{:S(2)}, u32[]{:S(2)}) collective-permute-start(f32[1,3,4,16,128]{4,3,2,1,0:T(8,128)S(1)} %get-tuple-element.53), channel_id=1, source_target_pairs={{0,1},{1,0},{2,3},{3,2},{4,5},{5,4},{6,7},{7,6},{8,9},{9,8},{10,11... | collective-permute-start | bytes 294920 | tf_op jit(solution)/shard_map/ppermute | solution.py:572

commit v8 on v7

--- a/solution.py
+++ b/solution.py
@@ -104,10 +104,11 @@
 
 
 def run_steps(groups, steps):
-    for turn in range(groups + 2*len(steps) - 2):
+    apart = 3 if len(steps) == 2 else 2
+    for turn in range(groups + apart * (len(steps) - 1)):
         for behind, step in reversed(list(enumerate(steps))):
-            if 0 <= turn - 2*behind < groups:
-                step(turn - 2*behind)
+            if 0 <= turn - apart * behind < groups:
+                step(turn - apart * behind)
 
 
 def served_facet(me, index, side):
@@ -130,7 +131,7 @@
             out_ref[index, 2, channel] = jnp.where(from_left, total[left], total[right]).astype(out_ref.dtype)
         return carry
 
-    lax.fori_loop(0, outs[0].shape[0], one_facet, 0, unroll=4)
+    lax.fori_loop(0, outs[0].shape[0], one_facet, 0, unroll=8)
 
 
 def vis_copy(vis_ref, held, arrived, channel):

time: 74.8 us -> 74.6 us (level)
  no operation moved by 1% of the time
where the time goes in v8:
time: 74.6 us; the launch traced here: 74.2 us
  Pallas kernels  27.9 us (37%)
  waiting for transfers between devices  27.3 us (37%)
  starting transfers between devices  18.9 us (25%)
    pallas_call x2, Pallas kernels, gradient_call(): pl.pallas_call(functools.partial(second_gradient_kernel if second else fi...  22.2 us
    ppermute x12, waiting for transfers between devices, to_served(): lax.ppermute(value, 'ra', [(source, target) for source, target in pairs i...  18.9 us
    ppermute x12, starting transfers between devices, to_served(): lax.ppermute(value, 'ra', [(source, target) for source, target in pairs i...  16.5 us
    ppermute x6, waiting for transfers between devices, across(): lax.ppermute(value, 'ra', [(source, source ^ difference) for source in ra...  8.4 us
    pallas_call x2, Pallas kernels, prox_call(): pl.pallas_call(functools.partial(prox_kernel, second, len(received)), out...  5.36 us
    ppermute x6, starting transfers between devices, across(): lax.ppermute(value, 'ra', [(source, source ^ difference) for source in ra...  2.45 us
  transfers between devices with their start and end apart: 18, of which 12 were waited for; matrix products, arithmetic and copies ran while one was open for 0% of the time, Pallas kernels for 0%

profile of v8, /device:TPU:0, one launch (start us, length us, event | category | flops | bytes accessed | tf_op | source)
XLA Modules:
  0.0 74.2 jit_solution(2228403295320583842)
XLA Ops:
  0.0 9.3 %first_gradient.1 = (f32[8,3,4,16,128]{4,3,2,1,0:T(8,128)S(1)}, f32[8,3,4,16,128]{4,3,2,1,0:T(8,128)S(1)}, bf16[4,16,16,128]{3,2,1,0:T(8,128)(2,1)S(1)}, bf16[25...) custom-call(s32[128]{0:T(128)} %bitcast.12, ...), custom_call_target="tpu_custom_call" | custom-call | flops 2147483648 | bytes 8388608 | tf_op jit(solution)/shard_map/first_gradient/pallas_call | solution.py:279
  9.3 0.5 collective-permute-start
  9.8 1.9 %collective-permute-done.got_ref = f32[8,3,4,16,128]{4,3,2,1,0:T(8,128)S(1)} collective-permute-done((f32[8,3,4,16,128]{4,3,2,1,0:T(8,128)S(1)}, f32[8,3,4,16,128]{4,3,2,1,0:T(8,128)S(1)}, u32[]{:S(2)}, u32[]{:S(2)}) %collective-permute-start) | collective-permute-done | bytes 786464 | tf_op jit(solution)/shard_map/ppermute | solution.py:573
  11.7 0.1 fold.2
  11.8 5.0 %collective-permute-start.1 = (bf16[2,3,4,16,128]{4,3,2,1,0:T(8,128)(2,1)S(1)}, bf16[2,3,4,16,128]{4,3,2,1,0:T(8,128)(2,1)S(1)}, u32[]{:S(2)}, u32[]{:S(2)}) collective-permute-start(bf16[2,3,4,16,128]{4,3,2,1,0:T(8,128)(2,1)S(1)} %get-tuple-element.38), channel_id=1, source_target_pairs={{0,12},{1,15},{2,14},{3,13},{4,8},{5,11},{6,10},{7,9},{8,4},{9,7},... | collective-permute-start | bytes 294920 | tf_op jit(solution)/shard_map/ppermute | solution.py:579
  16.8 0.6 collective-permute-start.3
  17.5 0.7 collective-permute-start.4
  18.1 2.1 %collective-permute-done.1.refs_0_ = bf16[2,3,4,16,128]{4,3,2,1,0:T(8,128)(2,1)S(1)} collective-permute-done((bf16[2,3,4,16,128]{4,3,2,1,0:T(8,128)(2,1)S(1)}, bf16[2,3,4,16,128]{4,3,2,1,0:T(8,128)(2,1)S(1)}, u32[]{:S(2)}, u32[]{:S(2)}) %collective-permute-start.1) | collective-permute-done | bytes 98336 | tf_op jit(solution)/shard_map/ppermute | solution.py:579
  20.2 5.9 %collective-permute-done.2.refs_1_ = bf16[2,3,4,16,128]{4,3,2,1,0:T(8,128)(2,1)S(1)} collective-permute-done((bf16[2,3,4,16,128]{4,3,2,1,0:T(8,128)(2,1)S(1)}, bf16[2,3,4,16,128]{4,3,2,1,0:T(8,128)(2,1)S(1)}, u32[]{:S(2)}, u32[]{:S(2)}) %collective-permute-start.2) | collective-permute-done | bytes 98336 | tf_op jit(solution)/shard_map/ppermute | solution.py:579
  26.3 1.3 %collective-permute-done.5 = f32[1,3,4,16,128]{4,3,2,1,0:T(8,128)S(1)} collective-permute-done((f32[1,3,4,16,128]{4,3,2,1,0:T(8,128)S(1)}, f32[1,3,4,16,128]{4,3,2,1,0:T(8,128)S(1)}, u32[]{:S(2)}, u32[]{:S(2)}) %collective-permute-start.5) | collective-permute-done | bytes 98336 | tf_op jit(solution)/shard_map/ppermute | solution.py:573
  27.6 2.7 %first_prox.1 = (f32[2,16,8,128]{3,2,1,0:T(8,128)S(1)}, bf16[128,128]{1,0:T(8,128)(2,1)S(1)}) custom-call(f32[1,192,128]{2,1,0:T(8,128)S(1)} %bitcast.8, f32[1,192,128]{2,1,0:T(8,128)S(1)} %bitcast.9, f32[4,4]{1,0:T(4,128)S(1)} %copy-done, f32[4]{0:T(128)S(1)} %copy-done.1), custom_call_target="tpu_custom_call" | custom-call | tf_op jit(solution)/shard_map/first_prox/pallas_call | solution.py:489
  30.2 0.2 collective-permute-start.6
  30.5 1.1 %collective-permute-done.6.refs_1_ = bf16[128,128]{1,0:T(8,128)(2,1)S(1)} collective-permute-done((bf16[128,128]{1,0:T(8,128)(2,1)S(1)}, bf16[128,128]{1,0:T(8,128)(2,1)S(1)}, u32[]{:S(2)}, u32[]{:S(2)}) %collective-permute-start.6) | collective-permute-done | bytes 32800 | tf_op jit(solution)/shard_map/ppermute | solution.py:573
  31.5 2.5 %collective-permute-start.10 = (bf16[256,128]{1,0:T(8,128)(2,1)S(1)}, bf16[256,128]{1,0:T(8,128)(2,1)S(1)}, u32[]{:S(2)}, u32[]{:S(2)}) collective-permute-start(bf16[256,128]{1,0:T(8,128)(2,1)S(1)} %join.1.own_ref), channel_id=1, source_target_pairs={{0,12},{1,15},{2,14},{3,13},{4,8},{5,11},{6,10},{7,9},{8,4},{9,7},... | collective-permute-start | bytes 196616 | tf_op jit(solution)/shard_map/ppermute | solution.py:579
  34.0 1.9 %collective-permute-start.8 = (bf16[256,128]{1,0:T(8,128)(2,1)S(1)}, bf16[256,128]{1,0:T(8,128)(2,1)S(1)}, u32[]{:S(2)}, u32[]{:S(2)}) collective-permute-start(bf16[256,128]{1,0:T(8,128)(2,1)S(1)} %join.1.own_ref), channel_id=1, source_target_pairs={{0,4},{1,7},{2,6},{3,5},{4,0},{5,3},{6,2},{7,1},{8,12},{9,15},{10,... | collective-permute-start | bytes 196616 | tf_op jit(solution)/shard_map/ppermute | solution.py:579
  35.9 0.7 collective-permute-start.7
  36.6 1.7 %collective-permute-done.10.refs_3_ = bf16[256,128]{1,0:T(8,128)(2,1)S(1)} collective-permute-done((bf16[256,128]{1,0:T(8,128)(2,1)S(1)}, bf16[256,128]{1,0:T(8,128)(2,1)S(1)}, u32[]{:S(2)}, u32[]{:S(2)}) %collective-permute-start.10) | collective-permute-done | bytes 65568 | tf_op jit(solution)/shard_map/ppermute | solution.py:579
  38.3 2.7 %collective-permute-done.9.refs_2_ = bf16[256,128]{1,0:T(8,128)(2,1)S(1)} collective-permute-done((bf16[256,128]{1,0:T(8,128)(2,1)S(1)}, bf16[256,128]{1,0:T(8,128)(2,1)S(1)}, u32[]{:S(2)}, u32[]{:S(2)}) %collective-permute-start.9) | collective-permute-done | bytes 65568 | tf_op jit(solution)/shard_map/ppermute | solution.py:579
  41.0 0.9 %collective-permute-start.11 = (bf16[1024,128]{1,0:T(8,128)(2,1)S(1)}, bf16[1024,128]{1,0:T(8,128)(2,1)S(1)}, u32[]{:S(2)}, u32[]{:S(2)}) collective-permute-start(bf16[1024,128]{1,0:T(8,128)(2,1)S(1)} %served.1.mine_ref), channel_id=1, source_target_pairs={{0,1},{1,0},{2,3},{3,2},{4,5},{5,4},{6,7},{7,6},{8,9},{9,8},{10,11... | collective-permute-start | bytes 786440 | tf_op jit(solution)/shard_map/ppermute | solution.py:573
  41.9 1.2 %collective-permute-done.11.theirs_ref = bf16[1024,128]{1,0:T(8,128)(2,1)S(1)} collective-permute-done((bf16[1024,128]{1,0:T(8,128)(2,1)S(1)}, bf16[1024,128]{1,0:T(8,128)(2,1)S(1)}, u32[]{:S(2)}, u32[]{:S(2)}) %collective-permute-start.11) | collective-permute-done | bytes 262176 | tf_op jit(solution)/shard_map/ppermute | solution.py:573
  43.1 12.9 %second_gradient.1 = (f32[8,3,4,16,128]{4,3,2,1,0:T(8,128)S(1)}, f32[8,3,4,16,128]{4,3,2,1,0:T(8,128)S(1)}) custom-call(s32[128]{0:T(128)} %bitcast.13, s32[128]{0:T(128)} %tile_ref.3, s32[128]{0:T(128)} %beam_ref.3, s32[1]{0:T(128)} %bitcast.refs_0_.me_ref, bf16[4,16,128,512]{3,2,1,0:T(8,128)(2,1)} %refs_1_.3, ...), custom_call_target="tpu_custom_call" | custom-call | flops 4294967296 | bytes 8388608 | tf_op jit(solution)/shard_map/second_gradient/pallas_call | solution.py:279
  56.0 0.4 collective-permute-start.12
  56.5 1.9 %collective-permute-done.12.got_ref = f32[8,3,4,16,128]{4,3,2,1,0:T(8,128)S(1)} collective-permute-done((f32[8,3,4,16,128]{4,3,2,1,0:T(8,128)S(1)}, f32[8,3,4,16,128]{4,3,2,1,0:T(8,128)S(1)}, u32[]{:S(2)}, u32[]{:S(2)}) %collective-permute-start.12) | collective-permute-done | bytes 786464 | tf_op jit(solution)/shard_map/ppermute | solution.py:573
  58.4 0.1 fold.3
  58.5 2.5 %collective-permute-start.13 = (bf16[2,3,4,16,128]{4,3,2,1,0:T(8,128)(2,1)S(1)}, bf16[2,3,4,16,128]{4,3,2,1,0:T(8,128)(2,1)S(1)}, u32[]{:S(2)}, u32[]{:S(2)}) collective-permute-start(bf16[2,3,4,16,128]{4,3,2,1,0:T(8,128)(2,1)S(1)} %get-tuple-element.48), channel_id=1, source_target_pairs={{0,12},{1,15},{2,14},{3,13},{4,8},{5,11},{6,10},{7,9},{8,4},{9,7},... | collective-permute-start | bytes 294920 | tf_op jit(solution)/shard_map/ppermute | solution.py:579
  61.0 1.9 %collective-permute-start.15 = (bf16[2,3,4,16,128]{4,3,2,1,0:T(8,128)(2,1)S(1)}, bf16[2,3,4,16,128]{4,3,2,1,0:T(8,128)(2,1)S(1)}, u32[]{:S(2)}, u32[]{:S(2)}) collective-permute-start(bf16[2,3,4,16,128]{4,3,2,1,0:T(8,128)(2,1)S(1)} %get-tuple-element.50), channel_id=1, source_target_pairs={{0,4},{1,7},{2,6},{3,5},{4,0},{5,3},{6,2},{7,1},{8,12},{9,15},{10,... | collective-permute-start | bytes 294920 | tf_op jit(solution)/shard_map/ppermute | solution.py:579
  62.9 0.7 collective-permute-start.16
  63.6 2.5 %collective-permute-done.13.refs_0_ = bf16[2,3,4,16,128]{4,3,2,1,0:T(8,128)(2,1)S(1)} collective-permute-done((bf16[2,3,4,16,128]{4,3,2,1,0:T(8,128)(2,1)S(1)}, bf16[2,3,4,16,128]{4,3,2,1,0:T(8,128)(2,1)S(1)}, u32[]{:S(2)}, u32[]{:S(2)}) %collective-permute-start.13) | collective-permute-done | bytes 98336 | tf_op jit(solution)/shard_map/ppermute | solution.py:579
  66.1 4.0 %collective-permute-done.14.refs_1_ = bf16[2,3,4,16,128]{4,3,2,1,0:T(8,128)(2,1)S(1)} collective-permute-done((bf16[2,3,4,16,128]{4,3,2,1,0:T(8,128)(2,1)S(1)}, bf16[2,3,4,16,128]{4,3,2,1,0:T(8,128)(2,1)S(1)}, u32[]{:S(2)}, u32[]{:S(2)}) %collective-permute-start.14) | collective-permute-done | bytes 98336 | tf_op jit(solution)/shard_map/ppermute | solution.py:579
  70.1 0.3 collective-permute-start.17
  70.5 1.1 %collective-permute-done.17 = f32[1,3,4,16,128]{4,3,2,1,0:T(8,128)S(1)} collective-permute-done((f32[1,3,4,16,128]{4,3,2,1,0:T(8,128)S(1)}, f32[1,3,4,16,128]{4,3,2,1,0:T(8,128)S(1)}, u32[]{:S(2)}, u32[]{:S(2)}) %collective-permute-start.17) | collective-permute-done | bytes 98336 | tf_op jit(solution)/shard_map/ppermute | solution.py:573
  71.5 2.7 %second_prox.1 = f32[4,16,256]{2,1,0:T(8,128)} custom-call(f32[1,192,128]{2,1,0:T(8,128)S(1)} %bitcast.10, f32[1,192,128]{2,1,0:T(8,128)S(1)} %bitcast.11, f32[4,4]{1,0:T(4,128)S(1)} %copy-done, f32[4]{0:T(128)S(1)} %copy-done.1, f32[2,16,8,128]{3,2,1,0:T(8,128)S(1)} %get-tuple-element.54.refs_4_), custom_call_target="tpu_custom_call" | custom-call | tf_op jit(solution)/shard_map/second_prox/pallas_call | solution.py:489
  (19 shorter events, 0.3 us)
Async XLA Ops:
  0.0 27.6 %copy-start = (f32[4,4]{1,0:T(4,128)S(1)}, f32[4,4]{1,0:T(4,128)}, u32[]{:S(2)}) copy-start(f32[4,4]{1,0:T(4,128)} %refs_2_.5) | copy-start | bytes 196
  0.0 27.6 %copy-start.1 = (f32[4]{0:T(128)S(1)}, f32[4]{0:T(128)}, u32[]{:S(2)}) copy-start(f32[4]{0:T(128)} %refs_3_.5) | copy-start | bytes 52
  9.3 2.4 %collective-permute-start = (f32[8,3,4,16,128]{4,3,2,1,0:T(8,128)S(1)}, f32[8,3,4,16,128]{4,3,2,1,0:T(8,128)S(1)}, u32[]{:S(2)}, u32[]{:S(2)}) collective-permute-start(f32[8,3,4,16,128]{4,3,2,1,0:T(8,128)S(1)} %get-tuple-element.36), channel_id=1, source_target_pairs={{0,1},{1,0},{2,3},{3,2},{4,5},{5,4},{6,7},{7,6},{8,9},{9,8},{10,11... | collective-permute-start | bytes 2359304 | tf_op jit(solution)/shard_map/ppermute | solution.py:573
  11.8 8.5 %collective-permute-start.1 = (bf16[2,3,4,16,128]{4,3,2,1,0:T(8,128)(2,1)S(1)}, bf16[2,3,4,16,128]{4,3,2,1,0:T(8,128)(2,1)S(1)}, u32[]{:S(2)}, u32[]{:S(2)}) collective-permute-start(bf16[2,3,4,16,128]{4,3,2,1,0:T(8,128)(2,1)S(1)} %get-tuple-element.38), channel_id=1, source_target_pairs={{0,12},{1,15},{2,14},{3,13},{4,8},{5,11},{6,10},{7,9},{8,4},{9,7},... | collective-permute-start | bytes 294920 | tf_op jit(solution)/shard_map/ppermute | solution.py:579
  16.8 9.3 %collective-permute-start.2 = (bf16[2,3,4,16,128]{4,3,2,1,0:T(8,128)(2,1)S(1)}, bf16[2,3,4,16,128]{4,3,2,1,0:T(8,128)(2,1)S(1)}, u32[]{:S(2)}, u32[]{:S(2)}) collective-permute-start(bf16[2,3,4,16,128]{4,3,2,1,0:T(8,128)(2,1)S(1)} %get-tuple-element.39), channel_id=1, source_target_pairs={{0,8},{1,11},{2,10},{3,9},{4,12},{5,15},{6,14},{7,13},{8,0},{9,3},... | collective-permute-start | bytes 294920 | tf_op jit(solution)/shard_map/ppermute | solution.py:579
  16.8 9.3 %collective-permute-start.3 = (bf16[2,3,4,16,128]{4,3,2,1,0:T(8,128)(2,1)S(1)}, bf16[2,3,4,16,128]{4,3,2,1,0:T(8,128)(2,1)S(1)}, u32[]{:S(2)}, u32[]{:S(2)}) collective-permute-start(bf16[2,3,4,16,128]{4,3,2,1,0:T(8,128)(2,1)S(1)} %get-tuple-element.40), channel_id=1, source_target_pairs={{0,4},{1,7},{2,6},{3,5},{4,0},{5,3},{6,2},{7,1},{8,12},{9,15},{10,... | collective-permute-start | bytes 294920 | tf_op jit(solution)/shard_map/ppermute | solution.py:579
  17.5 8.7 %collective-permute-start.4 = (bf16[2,3,4,16,128]{4,3,2,1,0:T(8,128)(2,1)S(1)}, bf16[2,3,4,16,128]{4,3,2,1,0:T(8,128)(2,1)S(1)}, u32[]{:S(2)}, u32[]{:S(2)}) collective-permute-start(bf16[2,3,4,16,128]{4,3,2,1,0:T(8,128)(2,1)S(1)} %get-tuple-element.41), channel_id=1, source_target_pairs={{1,3},{3,1},{5,7},{7,5},{9,11},{11,9},{13,15},{15,13},{17,19},{19,... | collective-permute-start | bytes 294920 | tf_op jit(solution)/shard_map/ppermute | solution.py:579
  26.2 1.4 %collective-permute-start.5 = (f32[1,3,4,16,128]{4,3,2,1,0:T(8,128)S(1)}, f32[1,3,4,16,128]{4,3,2,1,0:T(8,128)S(1)}, u32[]{:S(2)}, u32[]{:S(2)}) collective-permute-start(f32[1,3,4,16,128]{4,3,2,1,0:T(8,128)S(1)} %get-tuple-element.43), channel_id=1, source_target_pairs={{0,1},{1,0},{2,3},{3,2},{4,5},{5,4},{6,7},{7,6},{8,9},{9,8},{10,11... | collective-permute-start | bytes 294920 | tf_op jit(solution)/shard_map/ppermute | solution.py:573
  30.2 1.3 %collective-permute-start.6 = (bf16[128,128]{1,0:T(8,128)(2,1)S(1)}, bf16[128,128]{1,0:T(8,128)(2,1)S(1)}, u32[]{:S(2)}, u32[]{:S(2)}) collective-permute-start(bf16[128,128]{1,0:T(8,128)(2,1)S(1)} %get-tuple-element.44.refs_0_), channel_id=1, source_target_pairs={{0,1},{1,0},{2,3},{3,2},{4,5},{5,4},{6,7},{7,6},{8,9},{9,8},{10,11... | collective-permute-start | bytes 98312 | tf_op jit(solution)/shard_map/ppermute | solution.py:573
  31.5 6.8 %collective-permute-start.10 = (bf16[256,128]{1,0:T(8,128)(2,1)S(1)}, bf16[256,128]{1,0:T(8,128)(2,1)S(1)}, u32[]{:S(2)}, u32[]{:S(2)}) collective-permute-start(bf16[256,128]{1,0:T(8,128)(2,1)S(1)} %join.1.own_ref), channel_id=1, source_target_pairs={{0,12},{1,15},{2,14},{3,13},{4,8},{5,11},{6,10},{7,9},{8,4},{9,7},... | collective-permute-start | bytes 196616 | tf_op jit(solution)/shard_map/ppermute | solution.py:579
  34.0 7.0 %collective-permute-start.9 = (bf16[256,128]{1,0:T(8,128)(2,1)S(1)}, bf16[256,128]{1,0:T(8,128)(2,1)S(1)}, u32[]{:S(2)}, u32[]{:S(2)}) collective-permute-start(bf16[256,128]{1,0:T(8,128)(2,1)S(1)} %join.1.own_ref), channel_id=1, source_target_pairs={{0,8},{1,11},{2,10},{3,9},{4,12},{5,15},{6,14},{7,13},{8,0},{9,3},... | collective-permute-start | bytes 196616 | tf_op jit(solution)/shard_map/ppermute | solution.py:579
  34.0 7.0 %collective-permute-start.8 = (bf16[256,128]{1,0:T(8,128)(2,1)S(1)}, bf16[256,128]{1,0:T(8,128)(2,1)S(1)}, u32[]{:S(2)}, u32[]{:S(2)}) collective-permute-start(bf16[256,128]{1,0:T(8,128)(2,1)S(1)} %join.1.own_ref), channel_id=1, source_target_pairs={{0,4},{1,7},{2,6},{3,5},{4,0},{5,3},{6,2},{7,1},{8,12},{9,15},{10,... | collective-permute-start | bytes 196616 | tf_op jit(solution)/shard_map/ppermute | solution.py:579
  35.9 5.1 %collective-permute-start.7 = (bf16[256,128]{1,0:T(8,128)(2,1)S(1)}, bf16[256,128]{1,0:T(8,128)(2,1)S(1)}, u32[]{:S(2)}, u32[]{:S(2)}) collective-permute-start(bf16[256,128]{1,0:T(8,128)(2,1)S(1)} %join.1.own_ref), channel_id=1, source_target_pairs={{1,3},{3,1},{5,7},{7,5},{9,11},{11,9},{13,15},{15,13},{17,19},{19,... | collective-permute-start | bytes 196616 | tf_op jit(solution)/shard_map/ppermute | solution.py:579
  41.0 2.1 %collective-permute-start.11 = (bf16[1024,128]{1,0:T(8,128)(2,1)S(1)}, bf16[1024,128]{1,0:T(8,128)(2,1)S(1)}, u32[]{:S(2)}, u32[]{:S(2)}) collective-permute-start(bf16[1024,128]{1,0:T(8,128)(2,1)S(1)} %served.1.mine_ref), channel_id=1, source_target_pairs={{0,1},{1,0},{2,3},{3,2},{4,5},{5,4},{6,7},{7,6},{8,9},{9,8},{10,11... | collective-permute-start | bytes 786440 | tf_op jit(solution)/shard_map/ppermute | solution.py:573
  56.0 2.4 %collective-permute-start.12 = (f32[8,3,4,16,128]{4,3,2,1,0:T(8,128)S(1)}, f32[8,3,4,16,128]{4,3,2,1,0:T(8,128)S(1)}, u32[]{:S(2)}, u32[]{:S(2)}) collective-permute-start(f32[8,3,4,16,128]{4,3,2,1,0:T(8,128)S(1)} %get-tuple-element.46), channel_id=1, source_target_pairs={{0,1},{1,0},{2,3},{3,2},{4,5},{5,4},{6,7},{7,6},{8,9},{9,8},{10,11... | collective-permute-start | bytes 2359304 | tf_op jit(solution)/shard_map/ppermute | solution.py:573
  58.5 7.6 %collective-permute-start.13 = (bf16[2,3,4,16,128]{4,3,2,1,0:T(8,128)(2,1)S(1)}, bf16[2,3,4,16,128]{4,3,2,1,0:T(8,128)(2,1)S(1)}, u32[]{:S(2)}, u32[]{:S(2)}) collective-permute-start(bf16[2,3,4,16,128]{4,3,2,1,0:T(8,128)(2,1)S(1)} %get-tuple-element.48), channel_id=1, source_target_pairs={{0,12},{1,15},{2,14},{3,13},{4,8},{5,11},{6,10},{7,9},{8,4},{9,7},... | collective-permute-start | bytes 294920 | tf_op jit(solution)/shard_map/ppermute | solution.py:579
  61.0 9.1 %collective-permute-start.14 = (bf16[2,3,4,16,128]{4,3,2,1,0:T(8,128)(2,1)S(1)}, bf16[2,3,4,16,128]{4,3,2,1,0:T(8,128)(2,1)S(1)}, u32[]{:S(2)}, u32[]{:S(2)}) collective-permute-start(bf16[2,3,4,16,128]{4,3,2,1,0:T(8,128)(2,1)S(1)} %get-tuple-element.49), channel_id=1, source_target_pairs={{0,8},{1,11},{2,10},{3,9},{4,12},{5,15},{6,14},{7,13},{8,0},{9,3},... | collective-permute-start | bytes 294920 | tf_op jit(solution)/shard_map/ppermute | solution.py:579
  61.0 9.1 %collective-permute-start.15 = (bf16[2,3,4,16,128]{4,3,2,1,0:T(8,128)(2,1)S(1)}, bf16[2,3,4,16,128]{4,3,2,1,0:T(8,128)(2,1)S(1)}, u32[]{:S(2)}, u32[]{:S(2)}) collective-permute-start(bf16[2,3,4,16,128]{4,3,2,1,0:T(8,128)(2,1)S(1)} %get-tuple-element.50), channel_id=1, source_target_pairs={{0,4},{1,7},{2,6},{3,5},{4,0},{5,3},{6,2},{7,1},{8,12},{9,15},{10,... | collective-permute-start | bytes 294920 | tf_op jit(solution)/shard_map/ppermute | solution.py:579
  62.9 7.2 %collective-permute-start.16 = (bf16[2,3,4,16,128]{4,3,2,1,0:T(8,128)(2,1)S(1)}, bf16[2,3,4,16,128]{4,3,2,1,0:T(8,128)(2,1)S(1)}, u32[]{:S(2)}, u32[]{:S(2)}) collective-permute-start(bf16[2,3,4,16,128]{4,3,2,1,0:T(8,128)(2,1)S(1)} %get-tuple-element.51), channel_id=1, source_target_pairs={{1,3},{3,1},{5,7},{7,5},{9,11},{11,9},{13,15},{15,13},{17,19},{19,... | collective-permute-start | bytes 294920 | tf_op jit(solution)/shard_map/ppermute | solution.py:579
  70.1 1.4 %collective-permute-start.17 = (f32[1,3,4,16,128]{4,3,2,1,0:T(8,128)S(1)}, f32[1,3,4,16,128]{4,3,2,1,0:T(8,128)S(1)}, u32[]{:S(2)}, u32[]{:S(2)}) collective-permute-start(f32[1,3,4,16,128]{4,3,2,1,0:T(8,128)S(1)} %get-tuple-element.53), channel_id=1, source_target_pairs={{0,1},{1,0},{2,3},{3,2},{4,5},{5,4},{6,7},{7,6},{8,9},{9,8},{10,11... | collective-permute-start | bytes 294920 | tf_op jit(solution)/shard_map/ppermute | solution.py:573
